TPU v7x, 256 devices: a whole 4x4x8 slice. The times are simulated.
256 devices in a mesh: dp: 32 (over x, z_hi, core), tensor: 8 (over y, z_lo).
Axes of the slice: x: 4, y: 4, z: 8 (z_hi: 4, z_lo: 2; z = z_hi * 2 + z_lo), core: 2. Of those that a mesh axis runs over, the one named last changes fastest.
Arguments:
- tokens: bfloat16 [64, 192, 4096], P('dp', None, 'tensor'), may hold values from -6 to 6
- grad_out: bfloat16 [64, 192, 4096], P('dp', None, 'tensor'), may hold values from -6 to 6
- counts: int32 [32], replicated, may hold values from 0 to 2, as said below
- gain: bfloat16 [4096], P('dp'), may hold values from 0.5 to 1.5
- wq: bfloat16 [4096, 4096], P('dp', 'tensor'), may hold values from -2.5 to 2.5
- wk: bfloat16 [4096, 1024], P('dp', 'tensor'), may hold values from -0.09375 to 0.09375
- wv: bfloat16 [4096, 1024], P('dp', 'tensor'), may hold values from -0.09375 to 0.09375
- wo: bfloat16 [4096, 4096], P('tensor', 'dp'), may hold values from -0.09375 to 0.09375
Outputs:
- mixed: bfloat16 [64, 192, 4096], P('dp', None, 'tensor')
- grad_tokens: bfloat16 [64, 192, 4096], P('dp', None, 'tensor')
- grad_gain: float32 [4096], P('dp')
- grad_wq: float32 [4096, 4096], P('dp', 'tensor')
- grad_wk: float32 [4096, 1024], P('dp', 'tensor')
- grad_wv: float32 [4096, 1024], P('dp', 'tensor')
- grad_wo: float32 [4096, 4096], P('tensor', 'dp')
Inputs may be any that keep to these rules, and one draw needn't show every extreme that they name: `counts`: replica r and replica r + 16 hold 2 live blocks together; in every draw some replica holds 2.
All inputs are finite; a program needn't handle non-finite values.
Results may differ from a plain program's by a relative error of at most 0.025.
Values may be sent and summed in bfloat16 or wider, within the bound.
No kernel may reach another device: no remote copies, remote signals or barrier semaphores. Data moves between devices by JAX's collectives and lax.ppermute only.
A program may use at most 128 MiB of HBM per device.

v0:
```python
import jax
import jax.numpy as jnp
from jax import lax
from jax.sharding import PartitionSpec as P

HEADS = 32
KV = 8
HD = 128


epsilon = 1e-05


def attention_forward(query_heads, key_heads, value_heads):
    length = query_heads.shape[1]
    score_scale = query_heads.shape[-1] ** (-0.5)
    position = jnp.arange(length)
    causal = position[None, :] <= position[:, None]
    scores = (
        jnp.einsum("btgrh,bugh->bgrtu", query_heads, key_heads, preferred_element_type=jnp.float32)
        * score_scale
    )
    scores = jnp.where(causal, scores, -1e30)
    row_max = jnp.max(scores, axis=-1, keepdims=True)
    exp_scores = jnp.exp(scores - row_max)
    softmax_out = exp_scores / jnp.sum(exp_scores, axis=-1, keepdims=True)
    softmax_low = softmax_out.astype(jnp.bfloat16)
    context = jnp.einsum(
        "bgrtu,bugh->btgrh", softmax_low, value_heads, preferred_element_type=jnp.float32
    ).astype(jnp.bfloat16)
    return (softmax_out, softmax_low, context)


def attention_backward(grad_context, query_heads, key_heads, value_heads, softmax_out, softmax_low):
    score_scale = query_heads.shape[-1] ** (-0.5)
    grad_soft = jnp.einsum(
        "btgrh,bugh->bgrtu", grad_context, value_heads, preferred_element_type=jnp.float32
    )
    row_inner = jnp.sum(grad_soft * softmax_out, axis=-1, keepdims=True)
    grad_scores = (softmax_out * (grad_soft - row_inner) * score_scale).astype(jnp.bfloat16)
    grad_query = jnp.einsum(
        "bgrtu,bugh->btgrh", grad_scores, key_heads, preferred_element_type=jnp.float32
    ).astype(jnp.bfloat16)
    grad_key = jnp.einsum(
        "bgrtu,btgrh->bugh", grad_scores, query_heads, preferred_element_type=jnp.float32
    ).astype(jnp.bfloat16)
    grad_value = jnp.einsum(
        "bgrtu,btgrh->bugh", softmax_low, grad_context, preferred_element_type=jnp.float32
    ).astype(jnp.bfloat16)
    return (grad_query, grad_key, grad_value)


def on_device(tokens, grad_out, counts, gain, wq, wk, wv, wo):
    groups = lax.axis_size("tensor")
    dp_size = lax.axis_size("dp")
    replica = lax.axis_index("dp")
    own_count = counts[replica]
    blocks, length, shard_width = tokens.shape
    full_width = shard_width * groups
    d_local = gain.shape[0]
    q_cols = wq.shape[1]
    k_cols = wk.shape[1]
    o_rows = wo.shape[0]
    lane = wo.shape[1]
    pack = jnp.concatenate(
        [
            jnp.pad(gain.reshape(1, d_local), ((0, 7), (0, 0))),
            wq.reshape(d_local * q_cols // lane, lane),
            wk.reshape(d_local * k_cols // lane, lane),
            wv.reshape(d_local * k_cols // lane, lane),
            wo,
        ],
        axis=0,
    )
    packed = lax.all_gather(pack, "dp", axis=0, tiled=False)
    r0 = 8
    r1 = r0 + d_local * q_cols // lane
    r2 = r1 + d_local * k_cols // lane
    r3 = r2 + d_local * k_cols // lane
    r4 = r3 + o_rows
    gain_all = packed[:, 0, :].reshape(full_width)
    wq_all = packed[:, r0:r1, :].reshape(dp_size * d_local, q_cols)
    wk_all = packed[:, r1:r2, :].reshape(dp_size * d_local, k_cols)
    wv_all = packed[:, r2:r3, :].reshape(dp_size * d_local, k_cols)
    wo_blk = packed[:, r3:r4, :]
    half = dp_size // 2
    pair = [(i, (i + half) % dp_size) for i in range(dp_size)]
    partner_count = counts[(replica + half) % dp_size]
    lent = lax.ppermute(jnp.stack([tokens[1], grad_out[1]]), "dp", pair)
    borrow = own_count == 0
    work_live = jnp.where(borrow, partner_count >= 2, own_count >= 1)
    live_mask = work_live.astype(jnp.bfloat16)
    work_tokens = jnp.where(borrow, lent[0], tokens[0])[None]
    block_grad = (jnp.where(borrow, lent[1], grad_out[0]) * live_mask)[None]
    full_blocks = blocks
    blocks = 1
    piece = jnp.stack([work_tokens, block_grad])
    spread = jnp.broadcast_to(piece[None], (groups,) + piece.shape)
    gathered = lax.all_to_all(spread, "tensor", 0, 0, tiled=True)
    both = jnp.moveaxis(gathered, 0, 3).reshape(2, blocks, length, full_width)
    wide_in, upstream = both[0], both[1]
    repeat = HEADS // KV
    kv_local = wk_all.shape[1] // HD
    wide_float = wide_in.astype(jnp.float32)
    inverse_rms = lax.rsqrt(jnp.mean(wide_float * wide_float, axis=-1, keepdims=True) + epsilon)
    unit_rows = wide_float * inverse_rms
    gain_float = gain_all.astype(jnp.float32)
    normed_float = unit_rows * gain_float
    normed = normed_float.astype(jnp.bfloat16)
    queries = jnp.einsum("btd,dk->btk", normed, wq_all, preferred_element_type=jnp.float32).astype(
        jnp.bfloat16
    )
    key_rows = jnp.einsum("btd,dk->btk", normed, wk_all, preferred_element_type=jnp.float32).astype(
        jnp.bfloat16
    )
    values = jnp.einsum("btd,dk->btk", normed, wv_all, preferred_element_type=jnp.float32).astype(
        jnp.bfloat16
    )
    query_heads = queries.reshape(blocks, length, kv_local, repeat, HD)
    key_heads = key_rows.reshape(blocks, length, kv_local, HD)
    value_heads = values.reshape(blocks, length, kv_local, HD)
    softmax_out, softmax_low, context = attention_forward(query_heads, key_heads, value_heads)
    context_flat = context.reshape(blocks, length, kv_local * repeat * HD)
    partial_value = jnp.einsum(
        "btk,jkl->btjl", context_flat, wo_blk, preferred_element_type=jnp.float32
    ).reshape(blocks, length, full_width)
    upstream_blk = upstream.reshape(blocks, length, dp_size, lane)
    grad_context = jnp.einsum(
        "btjl,jkl->btk", upstream_blk, wo_blk, preferred_element_type=jnp.float32
    ).astype(jnp.bfloat16)
    grad_output_proj = jnp.einsum(
        "btk,btjl->jkl", context_flat, upstream_blk, preferred_element_type=jnp.float32
    )
    grad_query, grad_key, grad_value = attention_backward(
        grad_context.reshape(blocks, length, kv_local, repeat, HD),
        query_heads,
        key_heads,
        value_heads,
        softmax_out,
        softmax_low,
    )
    grad_query = grad_query.reshape(blocks, length, -1)
    grad_key = grad_key.reshape(blocks, length, -1)
    grad_value = grad_value.reshape(blocks, length, -1)
    normed_terms = jnp.einsum("btk,dk->btd", grad_query, wq_all, preferred_element_type=jnp.float32)
    normed_terms = normed_terms + jnp.einsum(
        "btk,dk->btd", grad_key, wk_all, preferred_element_type=jnp.float32
    )
    normed_terms = normed_terms + jnp.einsum(
        "btk,dk->btd", grad_value, wv_all, preferred_element_type=jnp.float32
    )
    grad_query_proj = jnp.einsum(
        "btd,btk->dk", normed, grad_query, preferred_element_type=jnp.float32
    )
    grad_key_proj = jnp.einsum("btd,btk->dk", normed, grad_key, preferred_element_type=jnp.float32)
    grad_value_proj = jnp.einsum(
        "btd,btk->dk", normed, grad_value, preferred_element_type=jnp.float32
    )
    term_low = normed_terms.astype(jnp.bfloat16)
    term_float = term_low.astype(jnp.float32)
    rows = blocks * length
    row_dot = jnp.sum(term_float * normed_float, axis=-1).reshape(rows)
    gain_part = jnp.sum(term_float * unit_rows, axis=(0, 1))
    extra = jnp.pad(row_dot, (0, shard_width - rows)).reshape(1, shard_width)
    extra = jnp.pad(extra, ((0, 7), (0, 0))).astype(jnp.bfloat16)

    def by_chunk(x):
        return x.reshape(rows, groups, shard_width).transpose(1, 0, 2)

    payload = jnp.concatenate(
        [
            by_chunk(partial_value.astype(jnp.bfloat16)),
            by_chunk(term_low),
            jnp.broadcast_to(extra[None], (groups,) + extra.shape),
        ],
        axis=1,
    )
    received = lax.all_to_all(payload, "tensor", 0, 0, tiled=True)
    reduced = jnp.sum(received.astype(jnp.float32), axis=0)
    attn_sum = reduced[:rows].reshape(blocks, length, shard_width)
    grad_normed = reduced[rows : 2 * rows].reshape(blocks, length, shard_width)
    row_mean = (reduced[2 * rows, :rows] / full_width).reshape(blocks, length, 1)
    mixed_block = ((work_tokens.astype(jnp.float32) + attn_sum) * live_mask.astype(jnp.float32)).astype(
        jnp.bfloat16
    )
    shard_start = lax.axis_index("tensor") * shard_width
    own_unit = lax.dynamic_slice_in_dim(unit_rows, shard_start, shard_width, 2)
    own_gain = lax.dynamic_slice_in_dim(gain_float, shard_start, shard_width, 0)
    own_grad = inverse_rms * (grad_normed * own_gain - own_unit * row_mean)
    grad_block = (block_grad.astype(jnp.float32) + own_grad).astype(jnp.bfloat16)
    work_out = jnp.stack([mixed_block[0], grad_block[0]])
    returned = lax.ppermute(work_out, "dp", pair)
    first = jnp.where(own_count >= 1, work_out, jnp.zeros_like(work_out))
    second = jnp.where(own_count >= 2, returned, jnp.zeros_like(returned))
    mixed_block = jnp.stack([first[0], second[0]])
    grad_block = jnp.stack([first[1], second[1]])
    gpack = jnp.concatenate(
        [
            jnp.pad(gain_part.reshape(dp_size, 1, d_local), ((0, 0), (0, 7), (0, 0))),
            grad_query_proj.reshape(dp_size, d_local * q_cols // lane, lane),
            grad_key_proj.reshape(dp_size, d_local * k_cols // lane, lane),
            grad_value_proj.reshape(dp_size, d_local * k_cols // lane, lane),
            grad_output_proj,
        ],
        axis=1,
    ).astype(jnp.bfloat16)
    greduced = lax.psum_scatter(gpack, "dp", scatter_dimension=0, tiled=True)[0].astype(jnp.float32)
    gain_spread = jnp.broadcast_to(greduced[0][None], (groups, d_local))
    grad_gain = jnp.sum(lax.all_to_all(gain_spread, "tensor", 0, 0, tiled=True), axis=0)
    grad_wq = greduced[r0:r1].reshape(d_local, q_cols)
    grad_wk = greduced[r1:r2].reshape(d_local, k_cols)
    grad_wv = greduced[r2:r3].reshape(d_local, k_cols)
    grad_wo = greduced[r3:r4]
    return (mixed_block, grad_block, grad_gain, grad_wq, grad_wk, grad_wv, grad_wo)


def solution(mesh):
    return jax.shard_map(
        on_device,
        mesh=mesh,
        in_specs=(
            P("dp", None, "tensor"),
            P("dp", None, "tensor"),
            P(),
            P("dp"),
            P("dp", "tensor"),
            P("dp", "tensor"),
            P("dp", "tensor"),
            P("tensor", "dp"),
        ),
        out_specs=(
            P("dp", None, "tensor"),
            P("dp", None, "tensor"),
            P("dp"),
            P("dp", "tensor"),
            P("dp", "tensor"),
            P("dp", "tensor"),
            P("tensor", "dp"),
        ),
        check_vma=False,
    )
```

profile of v0, /device:TPU:4, one launch (start us, length us, event | category | flops | bytes accessed | tf_op | source)
XLA Modules:
  0.0 374.2 jit_solution(9788769772524827395)
XLA Ops:
  7.2 1.0 reshape.464
  8.2 0.7 constant_dynamic-update-slice_fusion.4
  8.9 0.8 constant_dynamic-update-slice_fusion.2
  9.7 0.8 constant_dynamic-update-slice_fusion.1
  10.4 0.9 constant_dynamic-update-slice_fusion
  11.4 0.7 copy-done.19
  12.1 0.9 slice.90
  13.1 0.9 slice.91
  14.0 2.3 collective-permute-start
  16.3 1.3 fusion.89
  19.6 6.9 %collective-permute-done = bf16[2,192,512]{2,1,0:T(8,128)(2,1)S(1)} collective-permute-done((bf16[2,192,512]{2,1,0:T(8,128)(2,1)S(1)}, bf16[2,192,512]{2,1,0:T(8,128)(2,1)S(1)}, u32[]{:S(2)}, u32[]{:S(2)}) %collective-permute-start) | collective-permute-done | bytes 393248 | tf_op jit(solution)/shard_map/ppermute | solution.py:89
  26.5 1.2 fusion.80
  27.8 2.0 broadcast_in_dim.17
  29.7 5.8 %all-to-all-start = ((bf16[8,2,1,192,512]{4,3,2,1,0:T(8,128)(2,1)}), bf16[8,2,1,192,512]{4,3,2,1,0:T(8,128)(2,1)S(1)}, u32[]{:S(2)}, u32[]{:S(2)}) async-start(bf16[8,2,1,192,512]{4,3,2,1,0:T(8,128)(2,1)} %broadcast_in_dim.17), calls=%async_computation | async-start | bytes 6291456 | tf_op jit(solution)/shard_map/all_to_all | solution.py:99
  35.6 84.0 %all-to-all-done = bf16[8,2,1,192,512]{4,3,2,1,0:T(8,128)(2,1)S(1)} async-done(((bf16[8,2,1,192,512]{4,3,2,1,0:T(8,128)(2,1)}), bf16[8,2,1,192,512]{4,3,2,1,0:T(8,128)(2,1)S(1)}, u32[]{:S(2)}, u32[]{:S(2)}) %all-to-all-start) | async-done | bytes 3145760 | tf_op jit(solution)/shard_map/all_to_all | solution.py:99
  119.6 1.7 copy-done.2
  121.3 2.5 fusion.86
  123.8 2.1 copy.135
  126.0 3.8 %reshape.472 = bf16[192,32,128]{2,1,0:T(8,128)(2,1)} reshape(bf16[1,1,192,8,512]{4,3,2,1,0:T(8,128)(2,1)} %copy.135) | data formatting | bytes 3145728 | tf_op jit(solution)/shard_map/reshape.24
  129.8 2.1 copy.167
  131.9 0.9 copy-done.3
  133.2 0.9 fusion.82
  134.1 0.9 slice_convert_fusion.1
  135.0 3.1 fusion.85
  138.1 6.2 %slice_bitcast_fusion = (bf16[32,128,512]{1,2,0:T(8,128)(2,1)}, bf16[32,512,128]{2,1,0:T(8,128)(2,1)}) fusion(bf16[32,1288,128]{2,1,0:T(8,128)(2,1)} %bitcast.207), kind=kLoop, calls=%fused_computation.11 | loop fusion | bytes 16777216 | tf_op jit(solution)/shard_map/btk,jkl->btjl/dot_general | solution.py:124
  146.7 3.7 fusion.35
  150.5 7.6 %reshape.467 = bf16[4096,512]{1,0:T(8,128)(2,1)} reshape(bf16[32,512,128]{2,1,0:T(8,128)(2,1)} %get-tuple-element.52) | data formatting | bytes 8388608 | tf_op jit(solution)/shard_map/reshape | solution.py:82
  158.1 3.2 fusion.34
  163.7 0.9 copy-done.5
  164.5 1.5 fusion.59
  167.9 1.3 copy-done.6
  169.2 1.8 fusion.4
  170.9 1.8 fusion.13
  172.7 1.8 fusion.10
  174.5 3.4 convolution_convert_fusion
  178.1 2.3 copy.150
  180.4 1.3 copy.151
  181.7 1.4 copy.145
  183.1 7.6 %reshape.481 = bf16[32,512,128]{2,1,0:T(8,128)(2,1)} reshape(bf16[4096,512]{1,0:T(8,128)(2,1)} %convolution_convert_fusion) | data formatting | bytes 8388608 | tf_op jit(solution)/shard_map/reshape | solution.py:200
  190.7 6.7 %copy.149 = bf16[32,512,128]{1,2,0:T(8,128)(2,1)} copy(bf16[32,512,128]{2,1,0:T(8,128)(2,1)} %reshape.481) | data formatting | bytes 8388608 | tf_op jit(solution)/shard_map/reshape | solution.py:200
  197.3 3.4 convert_bitcast_fusion
  201.0 20.3 %concatenate.12 = bf16[32,1288,128]{1,2,0:T(8,128)(2,1)} concatenate(bf16[32,8,128]{1,2,0:T(8,128)(2,1)S(1)} %pad.22, bf16[32,512,128]{1,2,0:T(8,128)(2,1)} %copy.149, bf16[32,128,128]{1,2,0:T(8,128)(2,1)} %copy.150, bf16[32,128,128]{1,2,0:T(8,128)(2,1)} %copy.151, bf16[32,512,128]{1,2,0:T(8,128)(2,1)} %convert_bitcast_fusion), dimensions={1} | concatenate | bytes 21102592 | tf_op jit(solution)/shard_map/concatenate | solution.py:197
  221.4 6.5 %copy.133 = bf16[32,128,512]{2,1,0:T(8,128)(2,1)} copy(bf16[32,128,512]{1,2,0:T(8,128)(2,1)} %get-tuple-element.51) | data formatting | bytes 8388608 | tf_op jit(solution)/shard_map/btk,jkl->btjl/dot_general | solution.py:124
  227.9 4.0 %convolution_convert_fusion.1 = bf16[192,4096]{1,0:T(8,128)(2,1)S(1)} fusion(bf16[4096,512]{1,0:T(8,128)(2,1)} %bitcast.201, bf16[24,8,4,128]{3,2,1,0:T(4,128)(2,1)S(1)} %bitcast.216), kind=kOutput, calls=%fused_computation.5 | convolution fusion | flops 806092800 | bytes 5963776 | tf_op jit(solution)/shard_map/btk,jkl->btjl/dot_general | solution.py:124
  232.2 2.0 pad_maximum_fusion
  234.2 4.8 %all-to-all-start.1 = ((bf16[8,392,512]{2,1,0:T(8,128)(2,1)}), bf16[8,392,512]{2,1,0:T(8,128)(2,1)}, u32[]{:S(2)}, u32[]{:S(2)}) async-start(bf16[8,392,512]{2,1,0:T(8,128)(2,1)} %pad_maximum_fusion), calls=%async_computation.1 | async-start | bytes 6422528 | tf_op jit(solution)/shard_map/all_to_all | solution.py:178
  239.0 3.5 copy.143
  242.5 3.1 reshape.487
  245.6 0.7 dynamic_slice.14
  246.2 29.5 %all-to-all-done.1 = bf16[8,392,512]{2,1,0:T(8,128)(2,1)} async-done(((bf16[8,392,512]{2,1,0:T(8,128)(2,1)}), bf16[8,392,512]{2,1,0:T(8,128)(2,1)}, u32[]{:S(2)}, u32[]{:S(2)}) %all-to-all-start.1) | async-done | bytes 3211296 | tf_op jit(solution)/shard_map/all_to_all | solution.py:178
  275.7 2.5 convert_reduce_fusion
  278.6 0.7 collective-permute-start.1
  280.0 15.7 %collective-permute-done.1 = bf16[2,192,512]{2,1,0:T(8,128)(2,1)S(1)} collective-permute-done((bf16[2,192,512]{2,1,0:T(8,128)(2,1)S(1)}, bf16[2,192,512]{2,1,0:T(8,128)(2,1)S(1)}, u32[]{:S(2)}, u32[]{:S(2)}) %collective-permute-start.1) | collective-permute-done | bytes 393248 | tf_op jit(solution)/shard_map/ppermute | solution.py:192
  295.8 0.8 pad_maximum_fusion.4
  296.6 0.8 pad_maximum_fusion.3
  297.4 56.5 %reduce-scatter.2.cloned.1.call-done = bf16[1,1288,128]{1,2,0:T(8,128)(2,1)} async-done(((bf16[32,1288,128]{1,2,0:T(8,128)(2,1)}), bf16[1,1288,128]{1,2,0:T(8,128)(2,1)}) %reduce-scatter.2.cloned.1.call-update) | async-done | bytes 329744 | tf_op jit(solution)/shard_map/reduce_scatter | solution.py:207
  353.8 1.0 convert_element_type.233
  355.7 4.9 %all-to-all-start.2 = ((f32[8,1,128]{2,1,0:T(1,128)}), f32[8,1,128]{2,1,0:T(1,128)S(1)}, u32[]{:S(2)}, u32[]{:S(2)}) async-start(f32[8,1,128]{2,1,0:T(1,128)} %broadcast_in_dim.21), calls=%async_computation.3 | async-start | bytes 8192 | tf_op jit(solution)/shard_map/all_to_all | solution.py:209
  360.7 1.0 slice.136
  361.9 0.7 reshape.482
  362.6 0.8 copy.156
  363.5 0.7 copy.155
  364.2 0.7 copy.154
  364.9 1.9 all-to-all-done.2
  (93 shorter events, 10.2 us)
Async XLA Ops:
  7.2 126.1 %all-gather.3.cloned.1.call-start = ((), (), s32[]{:S(2)}) async-start(), calls=%async_computation.5 | async-start | bytes 10881024 | tf_op jit(solution)/shard_map/all_gather | solution.py:75
  11.4 0.7 copy-start.19
  14.0 12.4 %collective-permute-start = (bf16[2,192,512]{2,1,0:T(8,128)(2,1)S(1)}, bf16[2,192,512]{2,1,0:T(8,128)(2,1)S(1)}, u32[]{:S(2)}, u32[]{:S(2)}) collective-permute-start(bf16[2,192,512]{2,1,0:T(8,128)(2,1)S(1)} %pad_maximum_fusion.1), channel_id=1, source_target_pairs={{0,128},{8,136},{16,144},{24,152},{32,160},{40,168},{48,176},{56,1... | collective-permute-start | bytes 1179656 | tf_op jit(solution)/shard_map/ppermute | solution.py:89
  26.5 3.2 copy-start.15
  29.7 89.9 %all-to-all-start = ((bf16[8,2,1,192,512]{4,3,2,1,0:T(8,128)(2,1)}), bf16[8,2,1,192,512]{4,3,2,1,0:T(8,128)(2,1)S(1)}, u32[]{:S(2)}, u32[]{:S(2)}) async-start(bf16[8,2,1,192,512]{4,3,2,1,0:T(8,128)(2,1)} %broadcast_in_dim.17), calls=%async_computation | async-start | bytes 6291456 | tf_op jit(solution)/shard_map/all_to_all | solution.py:99
  35.6 318.2 %reduce-scatter.2.cloned.1.call-start = ((), (), s32[]{:S(2)}) async-start(), calls=%async_computation.4 | async-start | bytes 11894784 | tf_op jit(solution)/shard_map/reduce_scatter | solution.py:207
  119.6 1.7 copy-start.2
  123.8 5.9 %copy-start = (f32[1,1,192,8,512]{4,2,1,0,3:T(8,128)}, f32[1,1,192,8,512]{4,2,1,0,3:T(8,128)S(1)}, u32[]{:S(2)}) copy-start(f32[1,1,192,8,512]{4,2,1,0,3:T(8,128)S(1)} %get-tuple-element.57) | copy-start | bytes 9437188
  129.8 3.0 copy-start.3
  133.2 34.7 %copy-start.21 = (f32[192]{0:T(256)}, f32[192]{0:T(256)S(1)}, u32[]{:S(2)}) copy-start(f32[192]{0:T(256)S(1)} %add_rsqrt_fusion) | copy-start | bytes 2308
  138.1 6.2 %copy-start.4 = (bf16[8,2,1,192,512]{4,3,2,1,0:T(8,128)(2,1)S(1)}, bf16[8,2,1,192,512]{4,3,2,1,0:T(8,128)(2,1)}, u32[]{:S(2)}) copy-start(bf16[8,2,1,192,512]{4,3,2,1,0:T(8,128)(2,1)} %copy-done.2) | copy-start | bytes 9437188
  144.3 1.2 copy-start.7
  144.8 1.3 copy-start.9
  145.0 1.7 copy-start.11
  162.3 2.2 copy-start.5
  164.5 1.5 copy-start.8
  166.1 1.2 copy-start.10
  167.3 1.9 copy-start.6
  177.8 2.6 copy-start.14
  177.8 3.9 %copy-start.20 = (bf16[4096]{0:T(1024)(128)(2,1)S(1)}, bf16[4096]{0:T(1024)(128)(2,1)}, u32[]{:S(2)}) copy-start(bf16[4096]{0:T(1024)(128)(2,1)} %get-tuple-element.49) | copy-start | bytes 24580
  190.7 6.7 %copy-start.12 = (bf16[192,32,128]{2,1,0:T(8,128)(2,1)S(1)}, bf16[192,32,128]{2,1,0:T(8,128)(2,1)}, u32[]{:S(2)}) copy-start(bf16[192,32,128]{2,1,0:T(8,128)(2,1)} %reshape.472) | copy-start | bytes 4718596
  197.3 3.4 copy-start.13
  221.3 6.5 %copy-start.24 = (bf16[192]{0:T(256)(128)(2,1)S(1)}, bf16[192]{0:T(256)(128)(2,1)}, u32[]{:S(2)}) copy-start(bf16[192]{0:T(256)(128)(2,1)} %get-tuple-element.50) | copy-start | bytes 1156
  234.2 4.8 %copy-start.1 = (f32[1,1,192,8,512]{4,2,1,0,3:T(8,128)S(1)}, f32[1,1,192,8,512]{4,2,1,0,3:T(8,128)}, u32[]{:S(2)}) copy-start(f32[1,1,192,8,512]{4,2,1,0,3:T(8,128)} %copy-done) | copy-start | bytes 9437188
  234.2 41.5 %all-to-all-start.1 = ((bf16[8,392,512]{2,1,0:T(8,128)(2,1)}), bf16[8,392,512]{2,1,0:T(8,128)(2,1)}, u32[]{:S(2)}, u32[]{:S(2)}) async-start(bf16[8,392,512]{2,1,0:T(8,128)(2,1)} %pad_maximum_fusion), calls=%async_computation.1 | async-start | bytes 6422528 | tf_op jit(solution)/shard_map/all_to_all | solution.py:178
  245.6 32.7 %copy-start.16 = (bf16[2,192,512]{2,1,0:T(8,128)(2,1)S(1)}, bf16[2,192,512]{2,1,0:T(8,128)(2,1)}, u32[]{:S(2)}) copy-start(bf16[2,192,512]{2,1,0:T(8,128)(2,1)} %copy-done.15) | copy-start | bytes 1179652
  246.2 32.1 %copy-start.22 = (f32[192]{0:T(256)S(1)}, f32[192]{0:T(256)}, u32[]{:S(2)}) copy-start(f32[192]{0:T(256)} %copy-done.21) | copy-start | bytes 2308
  246.2 32.1 %copy-start.23 = (f32[512]{0:T(512)S(1)}, f32[512]{0:T(512)}, u32[]{:S(2)}) copy-start(f32[512]{0:T(512)} %dynamic_slice.14) | copy-start | bytes 6148
  275.7 2.5 copy-start.17
  275.7 2.7 copy-start.18
  278.6 17.1 %collective-permute-start.1 = (bf16[2,192,512]{2,1,0:T(8,128)(2,1)S(1)}, bf16[2,192,512]{2,1,0:T(8,128)(2,1)S(1)}, u32[]{:S(2)}, u32[]{:S(2)}) collective-permute-start(bf16[2,192,512]{2,1,0:T(8,128)(2,1)S(1)} %get-tuple-element.65), channel_id=1, source_target_pairs={{0,128},{8,136},{16,144},{24,152},{32,160},{40,168},{48,176},{56,1... | collective-permute-start | bytes 1179656 | tf_op jit(solution)/shard_map/ppermute | solution.py:192
  355.7 11.1 %all-to-all-start.2 = ((f32[8,1,128]{2,1,0:T(1,128)}), f32[8,1,128]{2,1,0:T(1,128)S(1)}, u32[]{:S(2)}, u32[]{:S(2)}) async-start(f32[8,1,128]{2,1,0:T(1,128)} %broadcast_in_dim.21), calls=%async_computation.3 | async-start | bytes 8192 | tf_op jit(solution)/shard_map/all_to_all | solution.py:209
Sparse Core Ops, SparseCore 0:
  12.2 111.0 all-gather.2
  221.5 132.3 reduce-scatter.1
where the time goes:
time: 376 us; the launch traced here: 374 us
  waiting for transfers between devices  194 us (52%)
  local copies, waits for them, and re-layouts  101 us (27%)
  matrix products  26.8 us (7%)
  starting transfers between devices  18.6 us (5%)
  between operations  17.2 us (5%)
  other arithmetic  16.6 us (4%)
    all_to_all x1, waiting for transfers between devices, on_device(): gathered = lax.all_to_all(spread, 'tensor', 0, 0, tiled=True)  84 us
    reduce_scatter x1, waiting for transfers between devices, on_device(): lax.psum_scatter(gpack, 'dp', scatter_dimension=0, tiled=True)[0]  56.5 us
    all_to_all x1, waiting for transfers between devices, on_device(): received = lax.all_to_all(payload, 'tensor', 0, 0, tiled=True)  29.5 us
    concatenate x1, local copies, waits for them, and re-layouts, on_device(): jnp.concatenate([jnp.pad(gain_part.reshape(dp_size, 1, d_local), ((0, 0),...  20.3 us
    ppermute x1, waiting for transfers between devices, on_device(): returned = lax.ppermute(work_out, 'dp', pair)  15.7 us
    reshape x2, local copies, waits for them, and re-layouts, on_device(): grad_query_proj.reshape(dp_size, d_local * q_cols // lane, lane)  14.2 us
    unnamed x59, local copies, waits for them, and re-layouts  13.5 us
    dot_general x2, local copies, waits for them, and re-layouts, on_device(): jnp.einsum('btk,jkl->btjl', context_flat, wo_blk, preferred_element_type=...  12.7 us
  transfers between devices with their start and end apart: 7, of which 6 were waited for; matrix products, arithmetic and copies ran while one was open for 12% of the time, Pallas kernels for 0%

commit v1 on v0

--- a/solution.py
+++ b/solution.py
@@ -64,7 +64,7 @@
     lane = wo.shape[1]
     pack = jnp.concatenate(
         [
-            jnp.pad(gain.reshape(1, d_local), ((0, 7), (0, 0))),
+            jnp.pad(gain.reshape(1, d_local), ((0, 15), (0, 0))),
             wq.reshape(d_local * q_cols // lane, lane),
             wk.reshape(d_local * k_cols // lane, lane),
             wv.reshape(d_local * k_cols // lane, lane),
@@ -73,7 +73,7 @@
         axis=0,
     )
     packed = lax.all_gather(pack, "dp", axis=0, tiled=False)
-    r0 = 8
+    r0 = 16
     r1 = r0 + d_local * q_cols // lane
     r2 = r1 + d_local * k_cols // lane
     r3 = r2 + d_local * k_cols // lane
@@ -162,7 +162,7 @@
     row_dot = jnp.sum(term_float * normed_float, axis=-1).reshape(rows)
     gain_part = jnp.sum(term_float * unit_rows, axis=(0, 1))
     extra = jnp.pad(row_dot, (0, shard_width - rows)).reshape(1, shard_width)
-    extra = jnp.pad(extra, ((0, 7), (0, 0))).astype(jnp.bfloat16)
+    extra = jnp.pad(extra, ((0, 15), (0, 0))).astype(jnp.bfloat16)
 
     def by_chunk(x):
         return x.reshape(rows, groups, shard_width).transpose(1, 0, 2)
@@ -196,7 +196,7 @@
     grad_block = jnp.stack([first[1], second[1]])
     gpack = jnp.concatenate(
         [
-            jnp.pad(gain_part.reshape(dp_size, 1, d_local), ((0, 0), (0, 7), (0, 0))),
+            jnp.pad(gain_part.reshape(dp_size, 1, d_local), ((0, 0), (0, 15), (0, 0))),
             grad_query_proj.reshape(dp_size, d_local * q_cols // lane, lane),
             grad_key_proj.reshape(dp_size, d_local * k_cols // lane, lane),
             grad_value_proj.reshape(dp_size, d_local * k_cols // lane, lane),

time: 376 us -> 377 us (level)
  no operation moved by 1% of the time
where the time goes in v1:
time: 377 us; the launch traced here: 374 us
  waiting for transfers between devices  196 us (52%)
  local copies, waits for them, and re-layouts  101 us (27%)
  matrix products  26.8 us (7%)
  starting transfers between devices  17.8 us (5%)
  between operations  17.2 us (5%)
  other arithmetic  16.4 us (4%)
    all_to_all x1, waiting for transfers between devices, on_device(): gathered = lax.all_to_all(spread, 'tensor', 0, 0, tiled=True)  84.2 us
    reduce_scatter x1, waiting for transfers between devices, on_device(): lax.psum_scatter(gpack, 'dp', scatter_dimension=0, tiled=True)[0]  57.1 us
    all_to_all x1, waiting for transfers between devices, on_device(): received = lax.all_to_all(payload, 'tensor', 0, 0, tiled=True)  30.2 us
    concatenate x1, local copies, waits for them, and re-layouts, on_device(): jnp.concatenate([jnp.pad(gain_part.reshape(dp_size, 1, d_local), ((0, 0),...  20.3 us
    ppermute x1, waiting for transfers between devices, on_device(): returned = lax.ppermute(work_out, 'dp', pair)  15.4 us
    reshape x2, local copies, waits for them, and re-layouts, on_device(): grad_query_proj.reshape(dp_size, d_local * q_cols // lane, lane)  14.2 us
    unnamed x59, local copies, waits for them, and re-layouts  13.5 us
    dot_general x2, local copies, waits for them, and re-layouts, on_device(): jnp.einsum('btk,jkl->btjl', context_flat, wo_blk, preferred_element_type=...  12.7 us
  transfers between devices with their start and end apart: 7, of which 6 were waited for; matrix products, arithmetic and copies ran while one was open for 12% of the time, Pallas kernels for 0%

profile of v1, /device:TPU:4, one launch (start us, length us, event | category | flops | bytes accessed | tf_op | source)
XLA Modules:
  0.0 374.4 jit_solution(14372701700268846164)
XLA Ops:
  7.2 1.0 reshape.464
  8.2 0.7 constant_dynamic-update-slice_fusion.4
  8.9 0.8 constant_dynamic-update-slice_fusion.2
  9.7 0.8 constant_dynamic-update-slice_fusion.1
  10.4 0.9 constant_dynamic-update-slice_fusion
  11.4 0.7 copy-done.19
  12.1 0.9 slice.90
  13.1 0.9 slice.91
  14.0 2.3 collective-permute-start
  16.3 1.3 fusion.89
  19.6 6.9 %collective-permute-done = bf16[2,192,512]{2,1,0:T(8,128)(2,1)S(1)} collective-permute-done((bf16[2,192,512]{2,1,0:T(8,128)(2,1)S(1)}, bf16[2,192,512]{2,1,0:T(8,128)(2,1)S(1)}, u32[]{:S(2)}, u32[]{:S(2)}) %collective-permute-start) | collective-permute-done | bytes 393248 | tf_op jit(solution)/shard_map/ppermute | solution.py:89
  26.5 1.2 fusion.80
  27.8 2.0 broadcast_in_dim.17
  29.7 5.8 %all-to-all-start = ((bf16[8,2,1,192,512]{4,3,2,1,0:T(8,128)(2,1)}), bf16[8,2,1,192,512]{4,3,2,1,0:T(8,128)(2,1)S(1)}, u32[]{:S(2)}, u32[]{:S(2)}) async-start(bf16[8,2,1,192,512]{4,3,2,1,0:T(8,128)(2,1)} %broadcast_in_dim.17), calls=%async_computation | async-start | bytes 6291456 | tf_op jit(solution)/shard_map/all_to_all | solution.py:99
  35.6 84.2 %all-to-all-done = bf16[8,2,1,192,512]{4,3,2,1,0:T(8,128)(2,1)S(1)} async-done(((bf16[8,2,1,192,512]{4,3,2,1,0:T(8,128)(2,1)}), bf16[8,2,1,192,512]{4,3,2,1,0:T(8,128)(2,1)S(1)}, u32[]{:S(2)}, u32[]{:S(2)}) %all-to-all-start) | async-done | bytes 3145760 | tf_op jit(solution)/shard_map/all_to_all | solution.py:99
  119.8 1.7 copy-done.2
  121.5 2.5 fusion.86
  124.0 2.1 copy.135
  126.1 3.8 %reshape.472 = bf16[192,32,128]{2,1,0:T(8,128)(2,1)} reshape(bf16[1,1,192,8,512]{4,3,2,1,0:T(8,128)(2,1)} %copy.135) | data formatting | bytes 3145728 | tf_op jit(solution)/shard_map/reshape.24
  129.9 2.1 copy.167
  132.1 0.9 copy-done.3
  133.4 0.9 fusion.82
  134.3 0.9 slice_convert_fusion.1
  135.1 3.1 fusion.85
  138.3 6.2 %slice_bitcast_fusion = (bf16[32,128,512]{1,2,0:T(8,128)(2,1)}, bf16[32,512,128]{2,1,0:T(8,128)(2,1)}) fusion(bf16[32,1296,128]{2,1,0:T(8,128)(2,1)} %bitcast.207), kind=kLoop, calls=%fused_computation.11 | loop fusion | bytes 16777216 | tf_op jit(solution)/shard_map/btk,jkl->btjl/dot_general | solution.py:124
  146.9 3.7 fusion.35
  150.6 7.6 %reshape.467 = bf16[4096,512]{1,0:T(8,128)(2,1)} reshape(bf16[32,512,128]{2,1,0:T(8,128)(2,1)} %get-tuple-element.52) | data formatting | bytes 8388608 | tf_op jit(solution)/shard_map/reshape | solution.py:82
  158.2 3.2 fusion.34
  163.8 0.9 copy-done.5
  164.7 1.5 fusion.59
  166.8 0.6 copy-done.10
  168.0 1.3 copy-done.6
  169.3 1.8 fusion.4
  171.1 1.8 fusion.13
  172.8 1.8 fusion.10
  174.6 3.4 convolution_convert_fusion
  178.2 2.3 copy.150
  180.6 1.3 copy.151
  181.9 1.4 copy.145
  183.3 7.6 %reshape.481 = bf16[32,512,128]{2,1,0:T(8,128)(2,1)} reshape(bf16[4096,512]{1,0:T(8,128)(2,1)} %convolution_convert_fusion) | data formatting | bytes 8388608 | tf_op jit(solution)/shard_map/reshape | solution.py:200
  190.8 6.7 %copy.149 = bf16[32,512,128]{1,2,0:T(8,128)(2,1)} copy(bf16[32,512,128]{2,1,0:T(8,128)(2,1)} %reshape.481) | data formatting | bytes 8388608 | tf_op jit(solution)/shard_map/reshape | solution.py:200
  197.5 3.4 convert_bitcast_fusion
  201.2 20.3 %concatenate.12 = bf16[32,1296,128]{1,2,0:T(8,128)(2,1)} concatenate(bf16[32,16,128]{1,2,0:T(8,128)(2,1)S(1)} %pad.22, bf16[32,512,128]{1,2,0:T(8,128)(2,1)} %copy.149, bf16[32,128,128]{1,2,0:T(8,128)(2,1)} %copy.150, bf16[32,128,128]{1,2,0:T(8,128)(2,1)} %copy.151, bf16[32,512,128]{1,2,0:T(8,128)(2,1)} %convert_bitcast_fusion), dimensions={1} | concatenate | bytes 21233664 | tf_op jit(solution)/shard_map/concatenate | solution.py:197
  221.5 6.5 %copy.133 = bf16[32,128,512]{2,1,0:T(8,128)(2,1)} copy(bf16[32,128,512]{1,2,0:T(8,128)(2,1)} %get-tuple-element.51) | data formatting | bytes 8388608 | tf_op jit(solution)/shard_map/btk,jkl->btjl/dot_general | solution.py:124
  228.0 4.0 %convolution_convert_fusion.1 = bf16[192,4096]{1,0:T(8,128)(2,1)S(1)} fusion(bf16[4096,512]{1,0:T(8,128)(2,1)} %bitcast.201, bf16[24,8,4,128]{3,2,1,0:T(4,128)(2,1)S(1)} %bitcast.216), kind=kOutput, calls=%fused_computation.5 | convolution fusion | flops 806092800 | bytes 5963776 | tf_op jit(solution)/shard_map/btk,jkl->btjl/dot_general | solution.py:124
  232.3 1.9 pad_maximum_fusion
  234.2 4.8 %all-to-all-start.1 = ((bf16[8,400,512]{2,1,0:T(8,128)(2,1)}), bf16[8,400,512]{2,1,0:T(8,128)(2,1)}, u32[]{:S(2)}, u32[]{:S(2)}) async-start(bf16[8,400,512]{2,1,0:T(8,128)(2,1)} %pad_maximum_fusion), calls=%async_computation.1 | async-start | bytes 6553600 | tf_op jit(solution)/shard_map/all_to_all | solution.py:178
  239.0 3.5 copy.143
  242.5 3.0 reshape.487
  245.5 0.7 dynamic_slice.14
  246.2 30.2 %all-to-all-done.1 = bf16[8,400,512]{2,1,0:T(8,128)(2,1)} async-done(((bf16[8,400,512]{2,1,0:T(8,128)(2,1)}), bf16[8,400,512]{2,1,0:T(8,128)(2,1)}, u32[]{:S(2)}, u32[]{:S(2)}) %all-to-all-start.1) | async-done | bytes 3276832 | tf_op jit(solution)/shard_map/all_to_all | solution.py:178
  276.4 2.6 convert_reduce_fusion
  280.7 15.4 %collective-permute-done.1 = bf16[2,192,512]{2,1,0:T(8,128)(2,1)S(1)} collective-permute-done((bf16[2,192,512]{2,1,0:T(8,128)(2,1)S(1)}, bf16[2,192,512]{2,1,0:T(8,128)(2,1)S(1)}, u32[]{:S(2)}, u32[]{:S(2)}) %collective-permute-start.1) | collective-permute-done | bytes 393248 | tf_op jit(solution)/shard_map/ppermute | solution.py:192
  296.1 0.8 pad_maximum_fusion.4
  296.9 0.8 pad_maximum_fusion.3
  297.7 57.1 %reduce-scatter.2.cloned.1.call-done = bf16[1,1296,128]{1,2,0:T(8,128)(2,1)} async-done(((bf16[32,1296,128]{1,2,0:T(8,128)(2,1)}), bf16[1,1296,128]{1,2,0:T(8,128)(2,1)}) %reduce-scatter.2.cloned.1.call-update) | async-done | bytes 331792 | tf_op jit(solution)/shard_map/reduce_scatter | solution.py:207
  354.8 1.0 convert_element_type.233
  356.7 4.2 %all-to-all-start.2 = ((f32[8,1,128]{2,1,0:T(1,128)}), f32[8,1,128]{2,1,0:T(1,128)S(1)}, u32[]{:S(2)}, u32[]{:S(2)}) async-start(f32[8,1,128]{2,1,0:T(1,128)} %broadcast_in_dim.21), calls=%async_computation.3 | async-start | bytes 8192 | tf_op jit(solution)/shard_map/all_to_all | solution.py:209
  361.0 1.0 slice.136
  362.1 0.7 reshape.482
  362.9 0.8 copy.156
  363.7 0.7 copy.155
  364.5 0.7 copy.154
  365.2 1.9 all-to-all-done.2
  (93 shorter events, 10.1 us)
Async XLA Ops:
  7.2 126.2 %all-gather.3.cloned.1.call-start = ((), (), s32[]{:S(2)}) async-start(), calls=%async_computation.5 | async-start | bytes 10948608 | tf_op jit(solution)/shard_map/all_gather | solution.py:75
  11.4 0.7 copy-start.19
  14.0 12.4 %collective-permute-start = (bf16[2,192,512]{2,1,0:T(8,128)(2,1)S(1)}, bf16[2,192,512]{2,1,0:T(8,128)(2,1)S(1)}, u32[]{:S(2)}, u32[]{:S(2)}) collective-permute-start(bf16[2,192,512]{2,1,0:T(8,128)(2,1)S(1)} %pad_maximum_fusion.1), channel_id=1, source_target_pairs={{0,128},{8,136},{16,144},{24,152},{32,160},{40,168},{48,176},{56,1... | collective-permute-start | bytes 1179656 | tf_op jit(solution)/shard_map/ppermute | solution.py:89
  26.5 3.2 copy-start.15
  29.7 90.1 %all-to-all-start = ((bf16[8,2,1,192,512]{4,3,2,1,0:T(8,128)(2,1)}), bf16[8,2,1,192,512]{4,3,2,1,0:T(8,128)(2,1)S(1)}, u32[]{:S(2)}, u32[]{:S(2)}) async-start(bf16[8,2,1,192,512]{4,3,2,1,0:T(8,128)(2,1)} %broadcast_in_dim.17), calls=%async_computation | async-start | bytes 6291456 | tf_op jit(solution)/shard_map/all_to_all | solution.py:99
  35.6 319.2 %reduce-scatter.2.cloned.1.call-start = ((), (), s32[]{:S(2)}) async-start(), calls=%async_computation.4 | async-start | bytes 11894784 | tf_op jit(solution)/shard_map/reduce_scatter | solution.py:207
  119.8 1.7 copy-start.2
  124.0 5.9 %copy-start = (f32[1,1,192,8,512]{4,2,1,0,3:T(8,128)}, f32[1,1,192,8,512]{4,2,1,0,3:T(8,128)S(1)}, u32[]{:S(2)}) copy-start(f32[1,1,192,8,512]{4,2,1,0,3:T(8,128)S(1)} %get-tuple-element.57) | copy-start | bytes 9437188
  129.9 3.0 copy-start.3
  133.4 34.7 %copy-start.21 = (f32[192]{0:T(256)}, f32[192]{0:T(256)S(1)}, u32[]{:S(2)}) copy-start(f32[192]{0:T(256)S(1)} %add_rsqrt_fusion) | copy-start | bytes 2308
  138.3 6.2 %copy-start.4 = (bf16[8,2,1,192,512]{4,3,2,1,0:T(8,128)(2,1)S(1)}, bf16[8,2,1,192,512]{4,3,2,1,0:T(8,128)(2,1)}, u32[]{:S(2)}) copy-start(bf16[8,2,1,192,512]{4,3,2,1,0:T(8,128)(2,1)} %copy-done.2) | copy-start | bytes 9437188
  144.5 1.2 copy-start.7
  144.9 1.3 copy-start.9
  145.1 1.7 copy-start.11
  162.5 2.2 copy-start.5
  164.7 1.5 copy-start.8
  166.2 1.2 copy-start.10
  167.4 1.9 copy-start.6
  178.0 2.6 copy-start.14
  178.0 3.9 %copy-start.20 = (bf16[4096]{0:T(1024)(128)(2,1)S(1)}, bf16[4096]{0:T(1024)(128)(2,1)}, u32[]{:S(2)}) copy-start(bf16[4096]{0:T(1024)(128)(2,1)} %get-tuple-element.49) | copy-start | bytes 24580
  190.8 6.7 %copy-start.12 = (bf16[192,32,128]{2,1,0:T(8,128)(2,1)S(1)}, bf16[192,32,128]{2,1,0:T(8,128)(2,1)}, u32[]{:S(2)}) copy-start(bf16[192,32,128]{2,1,0:T(8,128)(2,1)} %reshape.472) | copy-start | bytes 4718596
  197.5 3.4 copy-start.13
  221.5 6.5 %copy-start.24 = (bf16[192]{0:T(256)(128)(2,1)S(1)}, bf16[192]{0:T(256)(128)(2,1)}, u32[]{:S(2)}) copy-start(bf16[192]{0:T(256)(128)(2,1)} %get-tuple-element.50) | copy-start | bytes 1156
  234.2 4.8 %copy-start.1 = (f32[1,1,192,8,512]{4,2,1,0,3:T(8,128)S(1)}, f32[1,1,192,8,512]{4,2,1,0,3:T(8,128)}, u32[]{:S(2)}) copy-start(f32[1,1,192,8,512]{4,2,1,0,3:T(8,128)} %copy-done) | copy-start | bytes 9437188
  234.2 42.2 %all-to-all-start.1 = ((bf16[8,400,512]{2,1,0:T(8,128)(2,1)}), bf16[8,400,512]{2,1,0:T(8,128)(2,1)}, u32[]{:S(2)}, u32[]{:S(2)}) async-start(bf16[8,400,512]{2,1,0:T(8,128)(2,1)} %pad_maximum_fusion), calls=%async_computation.1 | async-start | bytes 6553600 | tf_op jit(solution)/shard_map/all_to_all | solution.py:178
  245.5 33.5 %copy-start.16 = (bf16[2,192,512]{2,1,0:T(8,128)(2,1)S(1)}, bf16[2,192,512]{2,1,0:T(8,128)(2,1)}, u32[]{:S(2)}) copy-start(bf16[2,192,512]{2,1,0:T(8,128)(2,1)} %copy-done.15) | copy-start | bytes 1179652
  246.2 32.9 %copy-start.22 = (f32[192]{0:T(256)S(1)}, f32[192]{0:T(256)}, u32[]{:S(2)}) copy-start(f32[192]{0:T(256)} %copy-done.21) | copy-start | bytes 2308
  246.2 32.9 %copy-start.23 = (f32[512]{0:T(512)S(1)}, f32[512]{0:T(512)}, u32[]{:S(2)}) copy-start(f32[512]{0:T(512)} %dynamic_slice.14) | copy-start | bytes 6148
  276.4 2.6 copy-start.17
  276.4 2.7 copy-start.18
  279.4 16.6 %collective-permute-start.1 = (bf16[2,192,512]{2,1,0:T(8,128)(2,1)S(1)}, bf16[2,192,512]{2,1,0:T(8,128)(2,1)S(1)}, u32[]{:S(2)}, u32[]{:S(2)}) collective-permute-start(bf16[2,192,512]{2,1,0:T(8,128)(2,1)S(1)} %get-tuple-element.65), channel_id=1, source_target_pairs={{0,128},{8,136},{16,144},{24,152},{32,160},{40,168},{48,176},{56,1... | collective-permute-start | bytes 1179656 | tf_op jit(solution)/shard_map/ppermute | solution.py:192
  356.7 10.4 %all-to-all-start.2 = ((f32[8,1,128]{2,1,0:T(1,128)}), f32[8,1,128]{2,1,0:T(1,128)S(1)}, u32[]{:S(2)}, u32[]{:S(2)}) async-start(f32[8,1,128]{2,1,0:T(1,128)} %broadcast_in_dim.21), calls=%async_computation.3 | async-start | bytes 8192 | tf_op jit(solution)/shard_map/all_to_all | solution.py:209
Sparse Core Ops, SparseCore 0:
  12.2 111.3 all-gather.2
  221.6 133.1 reduce-scatter.1

commit v2 on v1

--- a/solution.py
+++ b/solution.py
@@ -1,7 +1,7 @@
 import jax
 import jax.numpy as jnp
 from jax import lax
-from jax.sharding import PartitionSpec as P
+from jax.sharding import Mesh, PartitionSpec as P
 
 HEADS = 32
 KV = 8
@@ -52,8 +52,8 @@
 
 def on_device(tokens, grad_out, counts, gain, wq, wk, wv, wo):
     groups = lax.axis_size("tensor")
-    dp_size = lax.axis_size("dp")
-    replica = lax.axis_index("dp")
+    dp_size = lax.axis_size("dq") * lax.axis_size("dc")
+    replica = lax.axis_index(("dq", "dc"))
     own_count = counts[replica]
     blocks, length, shard_width = tokens.shape
     full_width = shard_width * groups
@@ -72,7 +72,12 @@
         ],
         axis=0,
     )
-    packed = lax.all_gather(pack, "dp", axis=0, tiled=False)
+    half_gather = lax.all_gather(pack, "dq", axis=0, tiled=False)
+    other_half = lax.ppermute(half_gather, "dc", [(0, 1), (1, 0)])
+    core = lax.axis_index("dc")
+    lower = jnp.where(core == 0, half_gather, other_half)
+    upper = jnp.where(core == 0, other_half, half_gather)
+    packed = jnp.stack([lower, upper], axis=1).reshape((dp_size,) + pack.shape)
     r0 = 16
     r1 = r0 + d_local * q_cols // lane
     r2 = r1 + d_local * k_cols // lane
@@ -86,7 +91,7 @@
     half = dp_size // 2
     pair = [(i, (i + half) % dp_size) for i in range(dp_size)]
     partner_count = counts[(replica + half) % dp_size]
-    lent = lax.ppermute(jnp.stack([tokens[1], grad_out[1]]), "dp", pair)
+    lent = lax.ppermute(jnp.stack([tokens[1], grad_out[1]]), ("dq", "dc"), pair)
     borrow = own_count == 0
     work_live = jnp.where(borrow, partner_count >= 2, own_count >= 1)
     live_mask = work_live.astype(jnp.bfloat16)
@@ -189,7 +194,7 @@
     own_grad = inverse_rms * (grad_normed * own_gain - own_unit * row_mean)
     grad_block = (block_grad.astype(jnp.float32) + own_grad).astype(jnp.bfloat16)
     work_out = jnp.stack([mixed_block[0], grad_block[0]])
-    returned = lax.ppermute(work_out, "dp", pair)
+    returned = lax.ppermute(work_out, ("dq", "dc"), pair)
     first = jnp.where(own_count >= 1, work_out, jnp.zeros_like(work_out))
     second = jnp.where(own_count >= 2, returned, jnp.zeros_like(returned))
     mixed_block = jnp.stack([first[0], second[0]])
@@ -204,7 +209,13 @@
         ],
         axis=1,
     ).astype(jnp.bfloat16)
-    greduced = lax.psum_scatter(gpack, "dp", scatter_dimension=0, tiled=True)[0].astype(jnp.float32)
+    by_core = gpack.reshape((dp_size // 2, 2) + gpack.shape[1:])
+    core = lax.axis_index("dc")
+    keep = lax.dynamic_index_in_dim(by_core, core, 1, keepdims=False)
+    give = lax.dynamic_index_in_dim(by_core, 1 - core, 1, keepdims=False)
+    got = lax.ppermute(give, "dc", [(0, 1), (1, 0)])
+    pair_sum = (keep.astype(jnp.float32) + got.astype(jnp.float32)).astype(jnp.bfloat16)
+    greduced = lax.psum_scatter(pair_sum, "dq", scatter_dimension=0, tiled=True)[0].astype(jnp.float32)
     gain_spread = jnp.broadcast_to(greduced[0][None], (groups, d_local))
     grad_gain = jnp.sum(lax.all_to_all(gain_spread, "tensor", 0, 0, tiled=True), axis=0)
     grad_wq = greduced[r0:r1].reshape(d_local, q_cols)
@@ -215,27 +226,30 @@
 
 
 def solution(mesh):
+    split = Mesh(
+        mesh.devices.reshape(mesh.shape["dp"] // 2, 2, mesh.shape["tensor"]), ("dq", "dc", "tensor")
+    )
     return jax.shard_map(
         on_device,
-        mesh=mesh,
+        mesh=split,
         in_specs=(
-            P("dp", None, "tensor"),
-            P("dp", None, "tensor"),
+            P(("dq", "dc"), None, "tensor"),
+            P(("dq", "dc"), None, "tensor"),
             P(),
-            P("dp"),
-            P("dp", "tensor"),
-            P("dp", "tensor"),
-            P("dp", "tensor"),
-            P("tensor", "dp"),
+            P(("dq", "dc")),
+            P(("dq", "dc"), "tensor"),
+            P(("dq", "dc"), "tensor"),
+            P(("dq", "dc"), "tensor"),
+            P("tensor", ("dq", "dc")),
         ),
         out_specs=(
-            P("dp", None, "tensor"),
-            P("dp", None, "tensor"),
-            P("dp"),
-            P("dp", "tensor"),
-            P("dp", "tensor"),
-            P("dp", "tensor"),
-            P("tensor", "dp"),
+            P(("dq", "dc"), None, "tensor"),
+            P(("dq", "dc"), None, "tensor"),
+            P(("dq", "dc")),
+            P(("dq", "dc"), "tensor"),
+            P(("dq", "dc"), "tensor"),
+            P(("dq", "dc"), "tensor"),
+            P("tensor", ("dq", "dc")),
         ),
         check_vma=False,
     )

time: 377 us -> 380 us (level)
  other arithmetic: 16.4 us -> 37.7 us
  local copies, waits for them, and re-layouts: 101 us -> 86.6 us
  waiting for transfers between devices: 196 us -> 189 us
    all_gather x1, waiting for transfers between devices: 0.02 us -> 86.5 us  [on_device(): half_gather = lax.all_gather(pack, 'dq', axis=0, tiled=False)]
    all_to_all x1, waiting for transfers between devices: 84.2 us -> 0.01 us  [on_device(): gathered = lax.all_to_all(spread, 'tensor', 0, 0, tiled=True)]
    reduce_scatter x1, waiting for transfers between devices: 57.1 us -> 0.01 us  [on_device(): lax.psum_scatter(pair_sum, 'dq', scatter_dimension=0, tiled=True)[0]]
    all_to_all x1, waiting for transfers between devices: 30.2 us -> 70 us  [on_device(): received = lax.all_to_all(payload, 'tensor', 0, 0, tiled=True)]
    reshape x3 -> x0, local copies, waits for them, and re-layouts: 15.6 us -> none  [the longest x2 14.2 us: on_device(): grad_query_proj.reshape(dp_size, d_local * q_cols // lane, lane)]
    another operation x2 -> x4, other arithmetic: 0.25 us -> 14.5 us  [the longest x2 14.3 us: on_device(): packed = jnp.stack([lower, upper], axis=1).reshape((dp_size,) + pack.shape)]
    unnamed x59 -> x74, local copies, waits for them, and re-layouts: 13.5 us -> 21.7 us
    convert_element_type x1 -> x2, other arithmetic: 1.03 us -> 8.77 us  [the longest x1 7.75 us: on_device(): (keep.astype(jnp.float32) + got.astype(jnp.float32)).astype(jnp.bfloat16)]
  transfers between devices with their start and end apart: 7 -> 9, of which waited for: 6 -> 6; matrix products, arithmetic and copies ran while one was open for 12% -> 12% of each run, Pallas kernels for 0% -> 0%
where the time goes in v2:
time: 380 us; the launch traced here: 377 us
  waiting for transfers between devices  189 us (50%)
  local copies, waits for them, and re-layouts  86.6 us (23%)
  other arithmetic  37.7 us (10%)
  matrix products  29.4 us (8%)
  starting transfers between devices  17.6 us (5%)
  between operations  17.2 us (5%)
    all_gather x1, waiting for transfers between devices, on_device(): half_gather = lax.all_gather(pack, 'dq', axis=0, tiled=False)  86.5 us
    all_to_all x1, waiting for transfers between devices, on_device(): received = lax.all_to_all(payload, 'tensor', 0, 0, tiled=True)  70 us
    unnamed x74, local copies, waits for them, and re-layouts  21.7 us
    concatenate x3, local copies, waits for them, and re-layouts, on_device(): jnp.concatenate([jnp.pad(gain_part.reshape(dp_size, 1, d_local), ((0, 0),...  14.5 us
    another operation x2, other arithmetic, on_device(): packed = jnp.stack([lower, upper], axis=1).reshape((dp_size,) + pack.shape)  14.3 us
    ppermute x1, waiting for transfers between devices, on_device(): returned = lax.ppermute(work_out, ('dq', 'dc'), pair)  12.8 us
    dot_general x2, local copies, waits for them, and re-layouts, on_device(): jnp.einsum('btk,jkl->btjl', context_flat, wo_blk, preferred_element_type=...  10.3 us
    ppermute x1, waiting for transfers between devices, on_device(): got = lax.ppermute(give, 'dc', [(0, 1), (1, 0)])  8.72 us
  transfers between devices with their start and end apart: 9, of which 6 were waited for; matrix products, arithmetic and copies ran while one was open for 12% of the time, Pallas kernels for 0%

profile of v2, /device:TPU:4, one launch (start us, length us, event | category | flops | bytes accessed | tf_op | source)
XLA Modules:
  0.0 377.3 jit_solution(7477443803842224724)
XLA Ops:
  7.2 1.0 reshape.480
  8.2 0.7 constant_dynamic-update-slice_fusion.4
  8.9 0.8 constant_dynamic-update-slice_fusion.2
  9.7 0.8 constant_dynamic-update-slice_fusion.1
  10.4 0.9 constant_dynamic-update-slice_fusion
  11.4 0.7 copy-done.23
  12.1 0.9 slice.90
  13.1 0.9 slice.91
  14.0 2.3 collective-permute-start
  16.3 1.4 fusion.80
  19.6 6.9 %collective-permute-done = bf16[2,192,512]{2,1,0:T(8,128)(2,1)S(1)} collective-permute-done((bf16[2,192,512]{2,1,0:T(8,128)(2,1)S(1)}, bf16[2,192,512]{2,1,0:T(8,128)(2,1)S(1)}, u32[]{:S(2)}, u32[]{:S(2)}) %collective-permute-start) | collective-permute-done | bytes 393248 | tf_op jit(solution)/shard_map/ppermute | solution.py:94
  26.5 1.2 fusion.71
  27.8 2.0 broadcast_in_dim.17
  29.8 5.8 %all-to-all-start = ((bf16[8,2,1,192,512]{4,3,2,1,0:T(8,128)(2,1)}), bf16[8,2,1,192,512]{4,3,2,1,0:T(8,128)(2,1)S(1)}, u32[]{:S(2)}, u32[]{:S(2)}) async-start(bf16[8,2,1,192,512]{4,3,2,1,0:T(8,128)(2,1)} %broadcast_in_dim.17), calls=%async_computation | async-start | bytes 6291456 | tf_op jit(solution)/shard_map/all_to_all | solution.py:104
  35.7 86.5 %all-gather.3.cloned.1.call-done = bf16[20736,128]{1,0:T(8,128)(2,1)} async-done(((bf16[1296,128]{1,0:T(8,128)(2,1)}), bf16[20736,128]{1,0:T(8,128)(2,1)}) %all-gather.3.cloned.1.call-update) | async-done | bytes 5308432 | tf_op jit(solution)/shard_map/all_gather | solution.py:75
  122.3 1.6 copy-done.3
  123.9 2.4 fusion.77
  126.3 2.2 copy.131
  128.5 3.7 reshape.489
  132.3 2.1 copy.164
  134.4 0.9 copy-done.4
  135.7 8.7 %select_bitcast_fusion.1 = (bf16[16,1,1296,128]{3,2,1,0:T(8,128)(2,1)}, bf16[16,1,1296,128]{3,2,1,0:T(8,128)(2,1)}) fusion(bf16[16,1296,128]{2,1,0:T(8,128)(2,1)} %bitcast.228, bf16[16,1296,128]{2,1,0:T(8,128)(2,1)} %collective-permute-done.1, pred[]{:T(512)S(6)} %eq.14), kind=kLoop, calls=%fused_computation.7 | loop fusion | flops 5308416 | bytes 21233664 | tf_op jit(solution)/shard_map/stack | solution.py:80
  144.4 5.6 %pad_maximum_fusion = bf16[16,2,1296,128]{3,2,1,0:T(8,128)(2,1)S(1)} fusion(bf16[16,1,1296,128]{3,2,1,0:T(8,128)(2,1)} %get-tuple-element.14, bf16[16,1,1296,128]{3,2,1,0:T(8,128)(2,1)} %get-tuple-element.13), kind=kLoop, calls=%fused_computation | loop fusion | flops 5308416 | bytes 21233664 | tf_op jit(solution)/shard_map/stack | solution.py:80
  150.1 1.8 fusion.76
  151.9 2.9 copy-done
  154.8 3.8 %slice_bitcast_fusion = (bf16[32,128,512]{1,2,0:T(8,128)(2,1)}, bf16[32,512,128]{2,1,0:T(8,128)(2,1)}) fusion(bf16[32,1296,128]{2,1,0:T(8,128)(2,1)S(1)} %bitcast.208), kind=kLoop, calls=%fused_computation.17 | loop fusion | bytes 16777216 | tf_op jit(solution)/shard_map/btk,jkl->btjl/dot_general | solution.py:129
  159.3 0.8 copy-done.15
  160.0 3.9 %fusion.26 = bf16[24,4,8,128]{3,2,1,0:T(8,128)(2,1)S(1)} fusion(bf16[32,1296,128]{2,1,0:T(8,128)(2,1)} %bitcast.209, bf16[192,32,128]{2,1,0:T(8,128)(2,1)S(1)} %copy-done.15), kind=kOutput, calls=%fused_computation.47 | convolution fusion | flops 805404672 | bytes 5963776 | tf_op jit(solution)/shard_map/btjl,jkl->btk/dot_general | solution.py:133
  165.1 7.5 %reshape.484 = bf16[4096,512]{1,0:T(8,128)(2,1)} reshape(bf16[32,512,128]{2,1,0:T(8,128)(2,1)} %get-tuple-element.10) | data formatting | bytes 8388608 | tf_op jit(solution)/shard_map/reshape | solution.py:87
  172.6 3.2 fusion.25
  178.3 0.9 copy-done.6
  179.1 1.5 fusion.50
  182.5 1.9 copy-done.10
  184.3 2.8 fusion.5
  187.2 3.0 dot_general.83
  190.2 3.1 convolution_convert_fusion.3
  193.3 3.1 convolution_convert_fusion.4
  196.4 3.3 convolution_convert_fusion
  200.0 7.6 %concatenate.20 = bf16[16,2,512,128]{3,2,1,0:T(8,128)(2,1)} reshape(bf16[4096,512]{1,0:T(8,128)(2,1)} %convolution_convert_fusion) | data formatting | bytes 8388608 | tf_op jit(solution)/shard_map/concatenate | solution.py:202
  207.6 3.4 convolution_convert_fusion.2
  211.0 6.3 %copy.149 = bf16[16,2,512,128]{3,2,0,1:T(8,128)(2,1)} copy(bf16[16,2,512,128]{2,3,1,0:T(8,128)(2,1)} %bitcast.219) | data formatting | bytes 8388608 | tf_op jit(solution)/shard_map/concatenate | solution.py:202
  217.4 3.1 copy_dynamic-update-slice_fusion
  220.8 0.7 copy-done.7
  222.1 2.9 dynamic-slice_bitcast_fusion
  225.0 2.7 copy-done.11
  228.3 8.7 %collective-permute-done.3 = bf16[16,1296,128]{2,1,0:T(8,128)(2,1)} collective-permute-done((bf16[16,1296,128]{2,1,0:T(8,128)(2,1)}, bf16[16,1296,128]{2,1,0:T(8,128)(2,1)}, u32[]{:S(2)}, u32[]{:S(2)}) %collective-permute-start.3) | collective-permute-done | bytes 5308448 | tf_op jit(solution)/shard_map/ppermute | solution.py:216
  237.0 7.8 %fusion = bf16[16,1296,128]{2,1,0:T(8,128)(2,1)} fusion(bf16[16,1296,128]{2,1,0:T(8,128)(2,1)} %collective-permute-done.3, bf16[16,2,1296,128]{3,2,0,1:T(8,128)(2,1)} %copy-done.11, s32[]{:T(128)S(6)} %select_n.107), kind=kLoop, calls=%fused_computation.2 | loop fusion | flops 10616832 | bytes 15925252 | tf_op jit(solution)/shard_map/convert_element_type | solution.py:217
  244.8 6.5 %copy.129 = bf16[32,128,512]{2,1,0:T(8,128)(2,1)} copy(bf16[32,128,512]{1,2,0:T(8,128)(2,1)} %get-tuple-element.9) | data formatting | bytes 8388608 | tf_op jit(solution)/shard_map/btk,jkl->btjl/dot_general | solution.py:129
  251.4 3.8 %convolution_convert_fusion.1 = bf16[192,4096]{1,0:T(8,128)(2,1)S(1)} fusion(bf16[4096,512]{1,0:T(8,128)(2,1)} %bitcast.218, bf16[24,8,4,128]{3,2,1,0:T(4,128)(2,1)S(1)} %bitcast.231), kind=kOutput, calls=%fused_computation.11 | convolution fusion | flops 806092800 | bytes 5963776 | tf_op jit(solution)/shard_map/btk,jkl->btjl/dot_general | solution.py:129
  255.5 1.8 pad_maximum_fusion.1
  257.4 5.0 %all-to-all-start.1 = ((bf16[8,400,512]{2,1,0:T(8,128)(2,1)}), bf16[8,400,512]{2,1,0:T(8,128)(2,1)}, u32[]{:S(2)}, u32[]{:S(2)}) async-start(bf16[8,400,512]{2,1,0:T(8,128)(2,1)} %pad_maximum_fusion.1), calls=%async_computation.1 | async-start | bytes 6553600 | tf_op jit(solution)/shard_map/all_to_all | solution.py:183
  262.4 3.5 copy.139
  265.9 2.9 reshape.503
  269.5 70.0 %all-to-all-done.1 = bf16[8,400,512]{2,1,0:T(8,128)(2,1)} async-done(((bf16[8,400,512]{2,1,0:T(8,128)(2,1)}), bf16[8,400,512]{2,1,0:T(8,128)(2,1)}, u32[]{:S(2)}, u32[]{:S(2)}) %all-to-all-start.1) | async-done | bytes 3276832 | tf_op jit(solution)/shard_map/all_to_all | solution.py:183
  339.5 2.6 convert_reduce_fusion
  343.7 12.8 %collective-permute-done.2 = bf16[2,192,512]{2,1,0:T(8,128)(2,1)S(1)} collective-permute-done((bf16[2,192,512]{2,1,0:T(8,128)(2,1)S(1)}, bf16[2,192,512]{2,1,0:T(8,128)(2,1)S(1)}, u32[]{:S(2)}, u32[]{:S(2)}) %collective-permute-start.2) | collective-permute-done | bytes 393248 | tf_op jit(solution)/shard_map/ppermute | solution.py:197
  356.6 0.8 pad_maximum_fusion.5
  357.4 0.8 pad_maximum_fusion.4
  358.2 1.0 convert_element_type.250
  359.2 0.7 slice_bitcast_fusion.1
  360.5 3.2 all-to-all-start.2
  364.4 0.9 slice.136
  365.4 0.7 reshape.498
  366.1 3.8 %all-to-all-done.2 = f32[8,1,128]{2,1,0:T(1,128)S(1)} async-done(((f32[8,1,128]{2,1,0:T(1,128)}), f32[8,1,128]{2,1,0:T(1,128)S(1)}, u32[]{:S(2)}, u32[]{:S(2)}) %all-to-all-start.2) | async-done | bytes 4128 | tf_op jit(solution)/shard_map/all_to_all | solution.py:220
  (113 shorter events, 12.2 us)
Async XLA Ops:
  7.2 115.0 %all-gather.3.cloned.1.call-start = ((), (), s32[]{:S(2)}) async-start(), calls=%async_computation.5 | async-start | bytes 5640192 | tf_op jit(solution)/shard_map/all_gather | solution.py:75
  11.4 0.7 copy-start.23
  14.0 12.4 %collective-permute-start = (bf16[2,192,512]{2,1,0:T(8,128)(2,1)S(1)}, bf16[2,192,512]{2,1,0:T(8,128)(2,1)S(1)}, u32[]{:S(2)}, u32[]{:S(2)}) collective-permute-start(bf16[2,192,512]{2,1,0:T(8,128)(2,1)S(1)} %pad_maximum_fusion.2), channel_id=1, source_target_pairs={{0,128},{8,136},{16,144},{24,152},{32,160},{40,168},{48,176},{56,1... | collective-permute-start | bytes 1179656 | tf_op jit(solution)/shard_map/ppermute | solution.py:94
  26.5 3.3 copy-start.19
  29.8 92.4 %all-to-all-start = ((bf16[8,2,1,192,512]{4,3,2,1,0:T(8,128)(2,1)}), bf16[8,2,1,192,512]{4,3,2,1,0:T(8,128)(2,1)S(1)}, u32[]{:S(2)}, u32[]{:S(2)}) async-start(bf16[8,2,1,192,512]{4,3,2,1,0:T(8,128)(2,1)} %broadcast_in_dim.17), calls=%async_computation | async-start | bytes 6291456 | tf_op jit(solution)/shard_map/all_to_all | solution.py:104
  35.7 322.5 %reduce-scatter.2.cloned.1.call-start = ((), (), s32[]{:S(2)}) async-start(), calls=%async_computation.4 | async-start | bytes 5640192 | tf_op jit(solution)/shard_map/reduce_scatter | solution.py:218
  122.2 13.5 %collective-permute-start.1 = (bf16[16,1296,128]{2,1,0:T(8,128)(2,1)}, bf16[16,1296,128]{2,1,0:T(8,128)(2,1)}, u32[]{:S(2)}, u32[]{:S(2)}) collective-permute-start(bf16[16,1296,128]{2,1,0:T(8,128)(2,1)} %bitcast.227), channel_id=1, source_target_pairs={{0,8},{8,0},{1,9},{9,1},{2,10},{10,2},{3,11},{11,3},{4,12},{12,4},... | collective-permute-start | bytes 15925256 | tf_op jit(solution)/shard_map/ppermute | solution.py:76
  122.2 1.6 copy-start.3
  126.3 6.0 %copy-start.1 = (f32[1,1,192,8,512]{4,2,1,0,3:T(8,128)}, f32[1,1,192,8,512]{4,2,1,0,3:T(8,128)S(1)}, u32[]{:S(2)}) copy-start(f32[1,1,192,8,512]{4,2,1,0,3:T(8,128)S(1)} %get-tuple-element.17) | copy-start | bytes 9437188
  132.3 3.0 copy-start.4
  135.7 22.9 %copy-start.27 = (f32[192]{0:T(256)}, f32[192]{0:T(256)S(1)}, u32[]{:S(2)}) copy-start(f32[192]{0:T(256)S(1)} %add_rsqrt_fusion) | copy-start | bytes 2308
  150.0 4.8 %copy-start = (bf16[16,2,1296,128]{3,2,1,0:T(8,128)(2,1)}, bf16[16,2,1296,128]{3,2,1,0:T(8,128)(2,1)S(1)}, u32[]{:S(2)}) copy-start(bf16[16,2,1296,128]{3,2,1,0:T(8,128)(2,1)S(1)} %pad_maximum_fusion) | copy-start | bytes 31850500
  154.8 3.8 %copy-start.5 = (bf16[8,2,1,192,512]{4,3,2,1,0:T(8,128)(2,1)S(1)}, bf16[8,2,1,192,512]{4,3,2,1,0:T(8,128)(2,1)}, u32[]{:S(2)}) copy-start(bf16[8,2,1,192,512]{4,3,2,1,0:T(8,128)(2,1)} %copy-done.3) | copy-start | bytes 9437188
  158.6 1.4 copy-start.15
  160.0 3.9 %copy-start.12 = (bf16[32,128,128]{2,1,0:T(8,128)(2,1)S(1)}, bf16[32,128,128]{2,1,0:T(8,128)(2,1)}, u32[]{:S(2)}) copy-start(bf16[32,128,128]{2,1,0:T(8,128)(2,1)} %get-tuple-element.12) | copy-start | bytes 3145732
  160.0 4.5 %copy-start.13 = (bf16[32,128,128]{2,1,0:T(8,128)(2,1)S(1)}, bf16[32,128,128]{2,1,0:T(8,128)(2,1)}, u32[]{:S(2)}) copy-start(bf16[32,128,128]{2,1,0:T(8,128)(2,1)} %get-tuple-element.11) | copy-start | bytes 3145732
  176.6 4.7 %copy-start.24 = (bf16[128,192]{0,1:T(8,128)(2,1)}, bf16[128,192]{0,1:T(8,128)(2,1)S(1)}, u32[]{:S(2)}) copy-start(bf16[128,192]{0,1:T(8,128)(2,1)S(1)} %fusion.32) | copy-start | bytes 147460
  176.9 2.2 copy-start.6
  177.7 2.9 copy-start.25
  180.7 1.2 copy-start.14
  181.9 2.5 copy-start.10
  181.9 2.5 copy-start.28
  182.5 4.7 %copy-start.8 = (bf16[192,4096]{1,0:T(8,128)(2,1)}, bf16[192,4096]{1,0:T(8,128)(2,1)S(1)}, u32[]{:S(2)}) copy-start(bf16[192,4096]{1,0:T(8,128)(2,1)S(1)} %fusion.1) | copy-start | bytes 4718596
  200.0 7.7 %copy-start.16 = (bf16[192,32,128]{2,1,0:T(8,128)(2,1)S(1)}, bf16[192,32,128]{2,1,0:T(8,128)(2,1)}, u32[]{:S(2)}) copy-start(bf16[192,32,128]{2,1,0:T(8,128)(2,1)} %reshape.489) | copy-start | bytes 4718596
  211.0 6.3 %copy-start.26 = (bf16[4096]{0:T(1024)(128)(2,1)S(1)}, bf16[4096]{0:T(1024)(128)(2,1)}, u32[]{:S(2)}) copy-start(bf16[4096]{0:T(1024)(128)(2,1)} %get-tuple-element.7) | copy-start | bytes 24580
  217.4 3.1 copy-start.18
  217.4 3.2 copy-start.17
  217.4 4.1 %copy-start.7 = (bf16[16,2,512,128]{3,2,0,1:T(8,128)(2,1)S(1)}, bf16[16,2,512,128]{3,2,0,1:T(8,128)(2,1)}, u32[]{:S(2)}) copy-start(bf16[16,2,512,128]{3,2,0,1:T(8,128)(2,1)} %copy.149) | copy-start | bytes 12582916
  222.1 5.7 %copy-start.11 = (bf16[16,2,1296,128]{3,2,0,1:T(8,128)(2,1)}, bf16[16,2,1296,128]{3,2,0,1:T(8,128)(2,1)S(1)}, u32[]{:S(2)}) copy-start(bf16[16,2,1296,128]{3,2,0,1:T(8,128)(2,1)S(1)} %constant_dynamic-update-slice_fusion.5) | copy-start | bytes 31850500
  227.8 9.2 %collective-permute-start.3 = (bf16[16,1296,128]{2,1,0:T(8,128)(2,1)}, bf16[16,1296,128]{2,1,0:T(8,128)(2,1)}, u32[]{:S(2)}, u32[]{:S(2)}) collective-permute-start(bf16[16,1296,128]{2,1,0:T(8,128)(2,1)} %dynamic-slice_bitcast_fusion), channel_id=1, source_target_pairs={{0,8},{8,0},{1,9},{9,1},{2,10},{10,2},{3,11},{11,3},{4,12},{12,4},... | collective-permute-start | bytes 15925256 | tf_op jit(solution)/shard_map/ppermute | solution.py:216
  244.8 6.5 %copy-start.31 = (bf16[192]{0:T(256)(128)(2,1)S(1)}, bf16[192]{0:T(256)(128)(2,1)}, u32[]{:S(2)}) copy-start(bf16[192]{0:T(256)(128)(2,1)} %get-tuple-element.8) | copy-start | bytes 1156
  251.3 3.9 %copy-start.9 = (bf16[192,4096]{1,0:T(8,128)(2,1)S(1)}, bf16[192,4096]{1,0:T(8,128)(2,1)}, u32[]{:S(2)}) copy-start(bf16[192,4096]{1,0:T(8,128)(2,1)} %copy-done.8) | copy-start | bytes 4718596
  257.4 5.0 %copy-start.2 = (f32[1,1,192,8,512]{4,2,1,0,3:T(8,128)S(1)}, f32[1,1,192,8,512]{4,2,1,0,3:T(8,128)}, u32[]{:S(2)}) copy-start(f32[1,1,192,8,512]{4,2,1,0,3:T(8,128)} %copy-done.1) | copy-start | bytes 9437188
  257.4 82.1 %all-to-all-start.1 = ((bf16[8,400,512]{2,1,0:T(8,128)(2,1)}), bf16[8,400,512]{2,1,0:T(8,128)(2,1)}, u32[]{:S(2)}, u32[]{:S(2)}) async-start(bf16[8,400,512]{2,1,0:T(8,128)(2,1)} %pad_maximum_fusion.1), calls=%async_computation.1 | async-start | bytes 6553600 | tf_op jit(solution)/shard_map/all_to_all | solution.py:183
  268.8 73.2 %copy-start.20 = (bf16[2,192,512]{2,1,0:T(8,128)(2,1)S(1)}, bf16[2,192,512]{2,1,0:T(8,128)(2,1)}, u32[]{:S(2)}) copy-start(bf16[2,192,512]{2,1,0:T(8,128)(2,1)} %copy-done.19) | copy-start | bytes 1179652
  269.5 72.7 %copy-start.29 = (f32[192]{0:T(256)S(1)}, f32[192]{0:T(256)}, u32[]{:S(2)}) copy-start(f32[192]{0:T(256)} %copy-done.27) | copy-start | bytes 2308
  269.5 72.7 %copy-start.30 = (f32[512]{0:T(512)S(1)}, f32[512]{0:T(512)}, u32[]{:S(2)}) copy-start(f32[512]{0:T(512)} %dynamic_slice.21) | copy-start | bytes 6148
  339.5 2.6 copy-start.21
  339.5 2.7 copy-start.22
  342.4 14.1 %collective-permute-start.2 = (bf16[2,192,512]{2,1,0:T(8,128)(2,1)S(1)}, bf16[2,192,512]{2,1,0:T(8,128)(2,1)S(1)}, u32[]{:S(2)}, u32[]{:S(2)}) collective-permute-start(bf16[2,192,512]{2,1,0:T(8,128)(2,1)S(1)} %get-tuple-element.25), channel_id=1, source_target_pairs={{0,128},{8,136},{16,144},{24,152},{32,160},{40,168},{48,176},{56,1... | collective-permute-start | bytes 1179656 | tf_op jit(solution)/shard_map/ppermute | solution.py:197
  360.5 9.4 %all-to-all-start.2 = ((f32[8,1,128]{2,1,0:T(1,128)}), f32[8,1,128]{2,1,0:T(1,128)S(1)}, u32[]{:S(2)}, u32[]{:S(2)}) async-start(f32[8,1,128]{2,1,0:T(1,128)} %broadcast_in_dim.21), calls=%async_computation.3 | async-start | bytes 8192 | tf_op jit(solution)/shard_map/all_to_all | solution.py:220
Sparse Core Ops, SparseCore 0:
  12.2 109.9 all-gather.2
  244.9 112.7 reduce-scatter.1

commit v3 on v1

v3 whole, which is shorter than its diff:
```python
import jax
import jax.numpy as jnp
from jax import lax
from jax.sharding import PartitionSpec as P

HEADS = 32
KV = 8
HD = 128


epsilon = 1e-05


def attention_forward(query_heads, key_heads, value_heads):
    length = query_heads.shape[1]
    score_scale = query_heads.shape[-1] ** (-0.5)
    position = jnp.arange(length)
    causal = position[None, :] <= position[:, None]
    scores = (
        jnp.einsum("btgrh,bugh->bgrtu", query_heads, key_heads, preferred_element_type=jnp.float32)
        * score_scale
    )
    scores = jnp.where(causal, scores, -1e30)
    row_max = jnp.max(scores, axis=-1, keepdims=True)
    exp_scores = jnp.exp(scores - row_max)
    softmax_out = exp_scores / jnp.sum(exp_scores, axis=-1, keepdims=True)
    softmax_low = softmax_out.astype(jnp.bfloat16)
    context = jnp.einsum(
        "bgrtu,bugh->btgrh", softmax_low, value_heads, preferred_element_type=jnp.float32
    ).astype(jnp.bfloat16)
    return (softmax_out, softmax_low, context)


def attention_backward(grad_context, query_heads, key_heads, value_heads, softmax_out, softmax_low):
    score_scale = query_heads.shape[-1] ** (-0.5)
    grad_soft = jnp.einsum(
        "btgrh,bugh->bgrtu", grad_context, value_heads, preferred_element_type=jnp.float32
    )
    row_inner = jnp.sum(grad_soft * softmax_out, axis=-1, keepdims=True)
    grad_scores = (softmax_out * (grad_soft - row_inner) * score_scale).astype(jnp.bfloat16)
    grad_query = jnp.einsum(
        "bgrtu,bugh->btgrh", grad_scores, key_heads, preferred_element_type=jnp.float32
    ).astype(jnp.bfloat16)
    grad_key = jnp.einsum(
        "bgrtu,btgrh->bugh", grad_scores, query_heads, preferred_element_type=jnp.float32
    ).astype(jnp.bfloat16)
    grad_value = jnp.einsum(
        "bgrtu,btgrh->bugh", softmax_low, grad_context, preferred_element_type=jnp.float32
    ).astype(jnp.bfloat16)
    return (grad_query, grad_key, grad_value)


def on_device(tokens, grad_out, counts, gain, wq, wk, wv, wo):
    groups = lax.axis_size("tensor")
    dp_size = lax.axis_size("dp")
    replica = lax.axis_index("dp")
    own_count = counts[replica]
    blocks, length, shard_width = tokens.shape
    full_width = shard_width * groups
    d_local = gain.shape[0]
    q_cols = wq.shape[1]
    k_cols = wk.shape[1]
    o_rows = wo.shape[0]
    c1 = q_cols
    c2 = c1 + k_cols
    c3 = c2 + k_cols
    c4 = c3 + o_rows
    pack = jnp.concatenate(
        [wq, wk, wv, wo.T, jnp.pad(gain.reshape(d_local, 1), ((0, 0), (0, 127)))], axis=1
    )
    packed = lax.all_gather(pack, "dp", axis=0, tiled=False)
    w_qkv = packed[:, :, :c3].reshape(dp_size * d_local, c3)
    wo_blk = packed[:, :, c3:c4]
    gain_all = packed[:, :, c4].reshape(full_width)
    half = dp_size // 2
    pair = [(i, (i + half) % dp_size) for i in range(dp_size)]
    partner_count = counts[(replica + half) % dp_size]
    lent = lax.ppermute(jnp.stack([tokens[1], grad_out[1]]), "dp", pair)
    borrow = own_count == 0
    work_live = jnp.where(borrow, partner_count >= 2, own_count >= 1)
    live_mask = work_live.astype(jnp.bfloat16)
    work_tokens = jnp.where(borrow, lent[0], tokens[0])
    work_grad = jnp.where(borrow, lent[1], grad_out[0]) * live_mask
    piece = jnp.stack([work_tokens, work_grad])
    spread = jnp.broadcast_to(piece[None], (groups,) + piece.shape)
    gathered = lax.all_to_all(spread, "tensor", 0, 0, tiled=True)
    both = jnp.moveaxis(gathered, 0, 2).reshape(2, length, full_width)
    wide_in, upstream = both[0], both[1]
    repeat = HEADS // KV
    kv_local = k_cols // HD
    wide_float = wide_in.astype(jnp.float32)
    inverse_rms = lax.rsqrt(jnp.mean(wide_float * wide_float, axis=-1, keepdims=True) + epsilon)
    unit_rows = wide_float * inverse_rms
    gain_float = gain_all.astype(jnp.float32)
    normed_float = unit_rows * gain_float
    normed = normed_float.astype(jnp.bfloat16)
    qkv = jnp.einsum("td,dk->tk", normed, w_qkv, preferred_element_type=jnp.float32).astype(
        jnp.bfloat16
    )
    query_heads = qkv[:, :c1].reshape(1, length, kv_local, repeat, HD)
    key_heads = qkv[:, c1:c2].reshape(1, length, kv_local, HD)
    value_heads = qkv[:, c2:c3].reshape(1, length, kv_local, HD)
    softmax_out, softmax_low, context = attention_forward(query_heads, key_heads, value_heads)
    context_flat = context.reshape(length, kv_local * repeat * HD)
    partial_value = jnp.einsum(
        "tk,jlk->tjl", context_flat, wo_blk, preferred_element_type=jnp.float32
    ).reshape(length, full_width)
    upstream_blk = upstream.reshape(length, dp_size, d_local)
    grad_context = jnp.einsum(
        "tjl,jlk->tk", upstream_blk, wo_blk, preferred_element_type=jnp.float32
    ).astype(jnp.bfloat16)
    grad_query, grad_key, grad_value = attention_backward(
        grad_context.reshape(1, length, kv_local, repeat, HD),
        query_heads,
        key_heads,
        value_heads,
        softmax_out,
        softmax_low,
    )
    grad_qkv = jnp.concatenate(
        [
            grad_query.reshape(length, c1),
            grad_key.reshape(length, k_cols),
            grad_value.reshape(length, k_cols),
        ],
        axis=1,
    )
    normed_terms = jnp.einsum("tk,dk->td", grad_qkv, w_qkv, preferred_element_type=jnp.float32)
    grad_w_qkv = jnp.einsum(
        "tjl,tk->jlk", normed.reshape(length, dp_size, d_local), grad_qkv,
        preferred_element_type=jnp.float32,
    )
    grad_output_t = jnp.einsum(
        "tjl,tk->jlk", upstream_blk, context_flat, preferred_element_type=jnp.float32
    )
    term_low = normed_terms.astype(jnp.bfloat16)
    term_float = term_low.astype(jnp.float32)
    row_dot = jnp.sum(term_float * normed_float, axis=-1)
    gain_part = jnp.sum(term_float * unit_rows, axis=0)
    extra = jnp.pad(row_dot, (0, shard_width - length)).reshape(1, shard_width)
    extra = jnp.pad(extra, ((0, 15), (0, 0))).astype(jnp.bfloat16)

    def by_chunk(x):
        return x.reshape(length, groups, shard_width).transpose(1, 0, 2)

    payload = jnp.concatenate(
        [
            by_chunk(partial_value.astype(jnp.bfloat16)),
            by_chunk(term_low),
            jnp.broadcast_to(extra[None], (groups,) + extra.shape),
        ],
        axis=1,
    )
    received = lax.all_to_all(payload, "tensor", 0, 0, tiled=True)
    reduced = jnp.sum(received.astype(jnp.float32), axis=0)
    attn_sum = reduced[:length]
    grad_normed = reduced[length : 2 * length]
    row_mean = (reduced[2 * length, :length] / full_width)[:, None]
    work_mixed = ((work_tokens.astype(jnp.float32) + attn_sum) * live_mask.astype(jnp.float32)).astype(
        jnp.bfloat16
    )
    shard_start = lax.axis_index("tensor") * shard_width
    own_unit = lax.dynamic_slice_in_dim(unit_rows, shard_start, shard_width, 1)
    own_gain = lax.dynamic_slice_in_dim(gain_float, shard_start, shard_width, 0)
    own_grad = inverse_rms * (grad_normed * own_gain - own_unit * row_mean)
    work_grad_tokens = (work_grad.astype(jnp.float32) + own_grad).astype(jnp.bfloat16)
    work_out = jnp.stack([work_mixed, work_grad_tokens])
    returned = lax.ppermute(work_out, "dp", pair)
    first = jnp.where(own_count >= 1, work_out, jnp.zeros_like(work_out))
    second = jnp.where(own_count >= 2, returned, jnp.zeros_like(returned))
    mixed_block = jnp.stack([first[0], second[0]])
    grad_block = jnp.stack([first[1], second[1]])
    gpack = jnp.concatenate(
        [
            grad_w_qkv.astype(jnp.bfloat16),
            grad_output_t.astype(jnp.bfloat16),
            jnp.pad(gain_part.reshape(dp_size, d_local, 1), ((0, 0), (0, 0), (0, 127))).astype(
                jnp.bfloat16
            ),
        ],
        axis=2,
    )
    greduced = lax.psum_scatter(gpack, "dp", scatter_dimension=0, tiled=True)[0].astype(jnp.float32)
    grad_wq = greduced[:, :c1]
    grad_wk = greduced[:, c1:c2]
    grad_wv = greduced[:, c2:c3]
    grad_wo = greduced[:, c3:c4].T
    gain_spread = jnp.broadcast_to(greduced[:, c4][None], (groups, d_local))
    grad_gain = jnp.sum(lax.all_to_all(gain_spread, "tensor", 0, 0, tiled=True), axis=0)
    return (mixed_block, grad_block, grad_gain, grad_wq, grad_wk, grad_wv, grad_wo)


def solution(mesh):
    return jax.shard_map(
        on_device,
        mesh=mesh,
        in_specs=(
            P("dp", None, "tensor"),
            P("dp", None, "tensor"),
            P(),
            P("dp"),
            P("dp", "tensor"),
            P("dp", "tensor"),
            P("dp", "tensor"),
            P("tensor", "dp"),
        ),
        out_specs=(
            P("dp", None, "tensor"),
            P("dp", None, "tensor"),
            P("dp"),
            P("dp", "tensor"),
            P("dp", "tensor"),
            P("dp", "tensor"),
            P("tensor", "dp"),
        ),
        check_vma=False,
    )
```

time: 377 us -> 351 us (0.931)
  local copies, waits for them, and re-layouts: 101 us -> 61.2 us
  waiting for transfers between devices: 196 us -> 212 us
    reshape x7 -> x3, local copies, waits for them, and re-layouts: 24.9 us -> 1.97 us  [the longest x1 1.21 us: on_device(): gain_part.reshape(dp_size, d_local, 1)]
    concatenate x2 -> x1, local copies, waits for them, and re-layouts: 21.2 us -> 0.67 us  [on_device(): jnp.concatenate([wq, wk, wv, wo.T, jnp.pad(gain.reshape(d_local, 1), ((0,...]
    all_gather x0 -> x1, local copies, waits for them, and re-layouts: none -> 15.2 us  [on_device(): packed = lax.all_gather(pack, 'dp', axis=0, tiled=False)]
    dot_general x2 -> x0, local copies, waits for them, and re-layouts: 12.7 us -> none  [on_device(): jnp.einsum('btk,jkl->btjl', context_flat, wo_blk, preferred_element_type=...]
    all_to_all x1, waiting for transfers between devices: 84.2 us -> 72 us  [on_device(): gathered = lax.all_to_all(spread, 'tensor', 0, 0, tiled=True)]
    all_to_all x1, waiting for transfers between devices: 30.2 us -> 39.9 us  [on_device(): received = lax.all_to_all(payload, 'tensor', 0, 0, tiled=True)]
    all_gather x1, waiting for transfers between devices: 0.02 us -> 8.6 us  [on_device(): packed = lax.all_gather(pack, 'dp', axis=0, tiled=False)]
    concatenate x0 -> x1, other arithmetic: none -> 5.39 us  [on_device(): jnp.concatenate([grad_w_qkv.astype(jnp.bfloat16), grad_output_t.astype(jn...]
  transfers between devices with their start and end apart: 7 -> 7, of which waited for: 6 -> 7; matrix products, arithmetic and copies ran while one was open for 12% -> 11% of each run, Pallas kernels for 0% -> 0%
where the time goes in v3:
time: 351 us; the launch traced here: 350 us
  waiting for transfers between devices  212 us (60%)
  local copies, waits for them, and re-layouts  61.2 us (17%)
  matrix products  23.5 us (7%)
  other arithmetic  18.9 us (5%)
  between operations  17.1 us (5%)
  starting transfers between devices  17 us (5%)
    all_to_all x1, waiting for transfers between devices, on_device(): gathered = lax.all_to_all(spread, 'tensor', 0, 0, tiled=True)  72 us
    reduce_scatter x1, waiting for transfers between devices, on_device(): lax.psum_scatter(gpack, 'dp', scatter_dimension=0, tiled=True)[0]  60.3 us
    all_to_all x1, waiting for transfers between devices, on_device(): received = lax.all_to_all(payload, 'tensor', 0, 0, tiled=True)  39.9 us
    ppermute x1, waiting for transfers between devices, on_device(): returned = lax.ppermute(work_out, 'dp', pair)  20 us
    all_gather x1, local copies, waits for them, and re-layouts, on_device(): packed = lax.all_gather(pack, 'dp', axis=0, tiled=False)  15.2 us
    convert_element_type x2, local copies, waits for them, and re-layouts, on_device(): wide_float = wide_in.astype(jnp.float32)  10.2 us
    unnamed x51, local copies, waits for them, and re-layouts  9.52 us
    all_gather x1, waiting for transfers between devices, on_device(): packed = lax.all_gather(pack, 'dp', axis=0, tiled=False)  8.6 us
  transfers between devices with their start and end apart: 7, of which 7 were waited for; matrix products, arithmetic and copies ran while one was open for 11% of the time, Pallas kernels for 0%

profile of v3, /device:TPU:4, one launch (start us, length us, event | category | flops | bytes accessed | tf_op | source)
XLA Modules:
  0.0 350.2 jit_solution(970154985376414719)
XLA Ops:
  7.2 0.9 copy.112
  8.2 0.9 copy.113
  9.0 1.0 copy.111
  10.1 0.9 bitcast_dynamic-update-slice_fusion
  11.1 0.7 pad_dynamic-update-slice_fusion
  11.7 0.7 copy-done.10
  12.5 0.9 slice.80
  13.4 0.9 slice.81
  14.4 2.3 collective-permute-start
  16.7 1.3 fusion.60
  20.0 6.9 %collective-permute-done = bf16[2,192,512]{2,1,0:T(8,128)(2,1)S(1)} collective-permute-done((bf16[2,192,512]{2,1,0:T(8,128)(2,1)S(1)}, bf16[2,192,512]{2,1,0:T(8,128)(2,1)S(1)}, u32[]{:S(2)}, u32[]{:S(2)}) %collective-permute-start) | collective-permute-done | bytes 393248 | tf_op jit(solution)/shard_map/ppermute | solution.py:78
  26.9 0.7 copy-done.6
  27.6 2.0 broadcast_in_dim.16
  29.7 5.8 %all-to-all-start = ((bf16[8,2,192,512]{3,2,1,0:T(8,128)(2,1)}), bf16[8,2,192,512]{3,2,1,0:T(8,128)(2,1)S(1)}, u32[]{:S(2)}, u32[]{:S(2)}) async-start(bf16[8,2,192,512]{3,2,1,0:T(8,128)(2,1)} %broadcast_in_dim.16), calls=%async_computation | async-start | bytes 6291456 | tf_op jit(solution)/shard_map/all_to_all | solution.py:86
  35.6 72.0 %all-to-all-done = bf16[8,2,192,512]{3,2,1,0:T(8,128)(2,1)S(1)} async-done(((bf16[8,2,192,512]{3,2,1,0:T(8,128)(2,1)}), bf16[8,2,192,512]{3,2,1,0:T(8,128)(2,1)S(1)}, u32[]{:S(2)}, u32[]{:S(2)}) %all-to-all-start) | async-done | bytes 3145760 | tf_op jit(solution)/shard_map/all_to_all | solution.py:86
  107.6 2.3 slice_convert_fusion
  109.9 2.0 copy.120
  111.9 3.7 %reshape_squeeze.4 = bf16[192,32,128]{2,1,0:T(8,128)(2,1)} reshape(bf16[1,192,8,512]{3,2,1,0:T(8,128)(2,1)} %copy.120) | data formatting | bytes 3145728 | tf_op jit(solution)/shard_map/reshape;squeeze | solution.py:108
  115.6 5.5 %copy.128 = f32[1,192,8,512]{3,2,1,0:T(8,128)} copy(f32[1,192,8,512]{3,1,0,2:T(8,128)} %get-tuple-element.52) | data formatting | bytes 6291456 | tf_op jit(solution)/shard_map/convert_element_type | solution.py:91
  121.2 2.0 copy.143
  123.2 4.7 %reshape.220 = f32[192,32,128]{2,1,0:T(8,128)} reshape(f32[1,192,8,512]{3,2,1,0:T(8,128)} %copy.128) | data formatting | bytes 6291456 | tf_op jit(solution)/shard_map/convert_element_type | solution.py:91
  127.9 0.4 multiply_reduce_fusion
  128.3 8.6 %all-gather.3.cloned.1.call-done = bf16[4096,1408]{0,1:T(8,128)(2,1)} async-done(((bf16[128,1408]{0,1:T(8,128)(2,1)}), bf16[4096,1408]{0,1:T(8,128)(2,1)}) %all-gather.3.cloned.1.call-update) | async-done | bytes 11534352 | tf_op jit(solution)/shard_map/all_gather | solution.py:71
  136.9 15.2 %copy.114 = bf16[4096,1408]{1,0:T(8,128)(2,1)} copy(bf16[4096,1408]{0,1:T(8,128)(2,1)} %all-gather.3.cloned.1.call-done) | data formatting | bytes 23068672 | tf_op jit(solution)/shard_map/all_gather | solution.py:71
  152.1 1.6 convert_reduce_fusion.1
  153.7 6.1 %slice.110 = bf16[32,128,768]{2,1,0:T(8,128)(2,1)} slice(bf16[32,128,1408]{2,1,0:T(8,128)(2,1)} %bitcast.169), slice={[0:32], [0:128], [0:768]} | slice | bytes 12582912 | tf_op jit(solution)/shard_map/slice | solution.py:72
  159.8 0.4 fusion.62
  160.5 0.8 copy-done.4
  161.2 3.5 fusion.18
  164.7 1.4 convolution_convert_fusion.4
  166.1 0.3 fusion.61
  166.6 0.4 fusion.16
  167.0 0.9 fusion.23
  168.4 0.9 fusion.24
  169.3 1.0 fusion.17
  170.3 1.6 multiply_convert_fusion
  172.1 0.8 reshape.230
  172.9 1.1 copy.124
  174.0 7.9 %fusion.3 = (bf16[4096]{0:T(1024)(128)(2,1)}, bf16[192]{0:T(256)(128)(2,1)}, f32[192,4096]{1,0:T(8,128)}, bf16[192,4096]{1,0:T(8,128)(2,1)}) fusion(f32[4096]{0:T(1024)S(1)} %bitcast.189, f32[192,4096]{1,0:T(8,128)S(1)} %bitcast.180, f32[192]{0:T(256)} %copy-done.15, bf16[4096,768]{1,0:T(8,128)(2,1)} %bitcast.176, bf16[192,128]{1,0:T(8,128)(2,1)} %fusion.23, ...), kind=kOutput, calls=%fused_computation.11 | convolution fusion | flops 1215131392 | bytes 14476416 | tf_op jit(solution)/shard_map/tk,dk->td/dot_general | solution.py:128
  181.9 1.2 copy.132
  183.2 2.9 convolution_convert_fusion.3
  186.1 2.5 convolution_convert_fusion.2
  188.6 5.4 %fusion.1 = bf16[32,128,1408]{2,1,0:T(8,128)(2,1)} fusion(bf16[32,128,1]{2,1,0:T(8,128)(2,1)S(1)} %copy.132, bf16[32,128,512]{2,1,0:T(8,128)(2,1)S(1)} %convolution_convert_fusion.3, bf16[32,128,768]{2,1,0:T(8,128)(2,1)S(1)} %convolution_convert_fusion.2), kind=kLoop, calls=%fused_computation.2 | loop fusion | flops 46137344 | bytes 22028288 | tf_op jit(solution)/shard_map/concatenate | solution.py:173
  194.0 2.6 slice.114
  196.7 1.5 convolution_convert_fusion.1
  198.6 1.9 pad_maximum_fusion
  200.5 3.9 %all-to-all-start.1 = ((bf16[8,400,512]{2,1,0:T(8,128)(2,1)}), bf16[8,400,512]{2,1,0:T(8,128)(2,1)S(1)}, u32[]{:S(2)}, u32[]{:S(2)}) async-start(bf16[8,400,512]{2,1,0:T(8,128)(2,1)} %pad_maximum_fusion), calls=%async_computation.1 | async-start | bytes 6553600 | tf_op jit(solution)/shard_map/all_to_all | solution.py:154
  204.5 39.9 %all-to-all-done.1 = bf16[8,400,512]{2,1,0:T(8,128)(2,1)S(1)} async-done(((bf16[8,400,512]{2,1,0:T(8,128)(2,1)}), bf16[8,400,512]{2,1,0:T(8,128)(2,1)S(1)}, u32[]{:S(2)}, u32[]{:S(2)}) %all-to-all-start.1) | async-done | bytes 3276832 | tf_op jit(solution)/shard_map/all_to_all | solution.py:154
  244.4 0.5 convert_reduce_fusion
  244.9 0.4 copy-done.7
  245.4 1.2 fusion.37
  246.6 0.6 collective-permute-start.1
  247.9 20.0 %collective-permute-done.1 = bf16[2,192,512]{2,1,0:T(8,128)(2,1)S(1)} collective-permute-done((bf16[2,192,512]{2,1,0:T(8,128)(2,1)S(1)}, bf16[2,192,512]{2,1,0:T(8,128)(2,1)S(1)}, u32[]{:S(2)}, u32[]{:S(2)}) %collective-permute-start.1) | collective-permute-done | bytes 393248 | tf_op jit(solution)/shard_map/ppermute | solution.py:168
  267.9 0.8 pad_maximum_fusion.5
  268.7 0.8 pad_maximum_fusion.4
  269.5 60.3 %reduce-scatter.2.cloned.1.call-done = bf16[1,128,1408]{2,1,0:T(8,128)(2,1)} async-done(((bf16[32,128,1408]{2,1,0:T(8,128)(2,1)}), bf16[1,128,1408]{2,1,0:T(8,128)(2,1)}) %reduce-scatter.2.cloned.1.call-update) | async-done | bytes 360464 | tf_op jit(solution)/shard_map/reduce_scatter | solution.py:183
  329.8 1.0 bitcast_convert_fusion
  330.9 0.8 slice_bitcast_fusion
  331.7 0.6 broadcast_in_dim.21
  332.3 4.3 %all-to-all-start.2 = ((f32[8,1,128]{2,1,0:T(1,128)}), f32[8,1,128]{2,1,0:T(1,128)S(1)}, u32[]{:S(2)}, u32[]{:S(2)}) async-start(f32[8,1,128]{2,1,0:T(1,128)} %broadcast_in_dim.21), calls=%async_computation.3 | async-start | bytes 8192 | tf_op jit(solution)/shard_map/all_to_all | solution.py:189
  336.6 0.7 fusion.57
  337.3 0.8 copy.134
  338.1 4.7 %all-to-all-done.2 = f32[8,1,128]{2,1,0:T(1,128)S(1)} async-done(((f32[8,1,128]{2,1,0:T(1,128)}), f32[8,1,128]{2,1,0:T(1,128)S(1)}, u32[]{:S(2)}, u32[]{:S(2)}) %all-to-all-start.2) | async-done | bytes 4128 | tf_op jit(solution)/shard_map/all_to_all | solution.py:189
  342.8 0.5 reduce_sum.69
  (68 shorter events, 2.1 us)
Async XLA Ops:
  7.2 19.7 %copy-start.12 = (bf16[2,192,512]{2,1,0:T(8,128)(2,1)S(1)}, bf16[2,192,512]{2,1,0:T(8,128)(2,1)}, u32[]{:S(2)}) copy-start(bf16[2,192,512]{2,1,0:T(8,128)(2,1)} %param.8) | copy-start | bytes 1179652
  7.2 19.7 %copy-start.11 = (bf16[2,192,512]{2,1,0:T(8,128)(2,1)S(1)}, bf16[2,192,512]{2,1,0:T(8,128)(2,1)}, u32[]{:S(2)}) copy-start(bf16[2,192,512]{2,1,0:T(8,128)(2,1)} %param.9) | copy-start | bytes 1179652
  7.2 129.7 %all-gather.3.cloned.1.call-start = ((), (), s32[]{:S(2)}) async-start(), calls=%async_computation.5 | async-start | bytes 11894784 | tf_op jit(solution)/shard_map/all_gather | solution.py:71
  11.7 0.7 copy-start.10
  14.4 12.4 %collective-permute-start = (bf16[2,192,512]{2,1,0:T(8,128)(2,1)S(1)}, bf16[2,192,512]{2,1,0:T(8,128)(2,1)S(1)}, u32[]{:S(2)}, u32[]{:S(2)}) collective-permute-start(bf16[2,192,512]{2,1,0:T(8,128)(2,1)S(1)} %pad_maximum_fusion.1), channel_id=1, source_target_pairs={{0,128},{8,136},{16,144},{24,152},{32,160},{40,168},{48,176},{56,1... | collective-permute-start | bytes 1179656 | tf_op jit(solution)/shard_map/ppermute | solution.py:78
  26.9 0.7 copy-start.6
  29.7 77.9 %all-to-all-start = ((bf16[8,2,192,512]{3,2,1,0:T(8,128)(2,1)}), bf16[8,2,192,512]{3,2,1,0:T(8,128)(2,1)S(1)}, u32[]{:S(2)}, u32[]{:S(2)}) async-start(bf16[8,2,192,512]{3,2,1,0:T(8,128)(2,1)} %broadcast_in_dim.16), calls=%async_computation | async-start | bytes 6291456 | tf_op jit(solution)/shard_map/all_to_all | solution.py:86
  35.5 294.3 %reduce-scatter.2.cloned.1.call-start = ((), (), s32[]{:S(2)}) async-start(), calls=%async_computation.4 | async-start | bytes 11894784 | tf_op jit(solution)/shard_map/reduce_scatter | solution.py:183
  115.6 5.5 %copy-start = (f32[1,192,8,512]{3,1,0,2:T(8,128)S(1)}, f32[1,192,8,512]{3,1,0,2:T(8,128)}, u32[]{:S(2)}) copy-start(f32[1,192,8,512]{3,1,0,2:T(8,128)} %get-tuple-element.52) | copy-start | bytes 9437188
  128.3 42.1 %copy-start.15 = (f32[192]{0:T(256)}, f32[192]{0:T(256)S(1)}, u32[]{:S(2)}) copy-start(f32[192]{0:T(256)S(1)} %add_rsqrt_fusion) | copy-start | bytes 2308
  159.8 1.4 copy-start.4
  160.3 4.4 %slice-start = ((s8[6291456]{0:T(1024)(128)(4,1)}), s8[4194304]{0:T(1024)(128)(4,1)S(1)}, s32[]{:S(2)}) async-start(s8[6291456]{0:T(1024)(128)(4,1)} %bitcast.177), calls=%async_computation.6 | async-start | bytes 8388608
  161.2 3.5 slice-start.1
  167.9 2.5 copy-start.2
  170.3 3.7 %copy-start.1 = (f32[24,8,8,512]{3,1,2,0:T(8,128)S(1)}, f32[24,8,8,512]{3,1,2,0:T(8,128)}, u32[]{:S(2)}) copy-start(f32[24,8,8,512]{3,1,2,0:T(8,128)} %copy.143) | copy-start | bytes 9437188
  174.0 8.0 %copy-start.8 = (bf16[24,8,4,128]{3,1,2,0:T(8,128)(2,1)}, bf16[24,8,4,128]{3,1,2,0:T(8,128)(2,1)S(1)}, u32[]{:S(2)}) copy-start(bf16[24,8,4,128]{3,1,2,0:T(8,128)(2,1)S(1)} %copy.186) | copy-start | bytes 589828
  183.2 2.9 copy-start.5
  183.2 2.9 copy-start.9
  183.2 2.9 copy-start.13
  183.2 2.9 copy-start.14
  194.0 2.7 copy-start.17
  196.7 1.6 copy-start.3
  200.5 43.9 %all-to-all-start.1 = ((bf16[8,400,512]{2,1,0:T(8,128)(2,1)}), bf16[8,400,512]{2,1,0:T(8,128)(2,1)S(1)}, u32[]{:S(2)}, u32[]{:S(2)}) async-start(bf16[8,400,512]{2,1,0:T(8,128)(2,1)} %pad_maximum_fusion), calls=%async_computation.1 | async-start | bytes 6553600 | tf_op jit(solution)/shard_map/all_to_all | solution.py:154
  204.4 40.5 %copy-start.16 = (f32[192]{0:T(256)S(1)}, f32[192]{0:T(256)}, u32[]{:S(2)}) copy-start(f32[192]{0:T(256)} %copy-done.15) | copy-start | bytes 2308
  244.4 0.9 copy-start.7
  246.6 21.2 %collective-permute-start.1 = (bf16[2,192,512]{2,1,0:T(8,128)(2,1)S(1)}, bf16[2,192,512]{2,1,0:T(8,128)(2,1)S(1)}, u32[]{:S(2)}, u32[]{:S(2)}) collective-permute-start(bf16[2,192,512]{2,1,0:T(8,128)(2,1)S(1)} %get-tuple-element.65), channel_id=1, source_target_pairs={{0,128},{8,136},{16,144},{24,152},{32,160},{40,168},{48,176},{56,1... | collective-permute-start | bytes 1179656 | tf_op jit(solution)/shard_map/ppermute | solution.py:168
  332.3 10.5 %all-to-all-start.2 = ((f32[8,1,128]{2,1,0:T(1,128)}), f32[8,1,128]{2,1,0:T(1,128)S(1)}, u32[]{:S(2)}, u32[]{:S(2)}) async-start(f32[8,1,128]{2,1,0:T(1,128)} %broadcast_in_dim.21), calls=%async_computation.3 | async-start | bytes 8192 | tf_op jit(solution)/shard_map/all_to_all | solution.py:189
Sparse Core Ops, SparseCore 0:
  12.6 124.2 all-gather.2
  194.1 135.6 reduce-scatter.1

commit v4 on v3

--- a/solution.py
+++ b/solution.py
@@ -68,10 +68,9 @@
     pack = jnp.concatenate(
         [wq, wk, wv, wo.T, jnp.pad(gain.reshape(d_local, 1), ((0, 0), (0, 127)))], axis=1
     )
-    packed = lax.all_gather(pack, "dp", axis=0, tiled=False)
-    w_qkv = packed[:, :, :c3].reshape(dp_size * d_local, c3)
-    wo_blk = packed[:, :, c3:c4]
-    gain_all = packed[:, :, c4].reshape(full_width)
+    packed = lax.all_gather(pack, "dp", axis=0, tiled=True)
+    width = packed.shape[1]
+    gain_all = packed[:, c4]
     half = dp_size // 2
     pair = [(i, (i + half) % dp_size) for i in range(dp_size)]
     partner_count = counts[(replica + half) % dp_size]
@@ -94,7 +93,7 @@
     gain_float = gain_all.astype(jnp.float32)
     normed_float = unit_rows * gain_float
     normed = normed_float.astype(jnp.bfloat16)
-    qkv = jnp.einsum("td,dk->tk", normed, w_qkv, preferred_element_type=jnp.float32).astype(
+    qkv = jnp.einsum("td,dk->tk", normed, packed, preferred_element_type=jnp.float32).astype(
         jnp.bfloat16
     )
     query_heads = qkv[:, :c1].reshape(1, length, kv_local, repeat, HD)
@@ -102,13 +101,14 @@
     value_heads = qkv[:, c2:c3].reshape(1, length, kv_local, HD)
     softmax_out, softmax_low, context = attention_forward(query_heads, key_heads, value_heads)
     context_flat = context.reshape(length, kv_local * repeat * HD)
+    context_wide = jnp.pad(context_flat, ((0, 0), (c3, width - c4)))
     partial_value = jnp.einsum(
-        "tk,jlk->tjl", context_flat, wo_blk, preferred_element_type=jnp.float32
-    ).reshape(length, full_width)
+        "tk,dk->td", context_wide, packed, preferred_element_type=jnp.float32
+    )
     upstream_blk = upstream.reshape(length, dp_size, d_local)
     grad_context = jnp.einsum(
-        "tjl,jlk->tk", upstream_blk, wo_blk, preferred_element_type=jnp.float32
-    ).astype(jnp.bfloat16)
+        "td,dk->tk", upstream, packed, preferred_element_type=jnp.float32
+    )[:, c3:c4].astype(jnp.bfloat16)
     grad_query, grad_key, grad_value = attention_backward(
         grad_context.reshape(1, length, kv_local, repeat, HD),
         query_heads,
@@ -125,7 +125,8 @@
         ],
         axis=1,
     )
-    normed_terms = jnp.einsum("tk,dk->td", grad_qkv, w_qkv, preferred_element_type=jnp.float32)
+    grad_wide = jnp.pad(grad_qkv, ((0, 0), (0, width - c3)))
+    normed_terms = jnp.einsum("tk,dk->td", grad_wide, packed, preferred_element_type=jnp.float32)
     grad_w_qkv = jnp.einsum(
         "tjl,tk->jlk", normed.reshape(length, dp_size, d_local), grad_qkv,
         preferred_element_type=jnp.float32,

time: 351 us -> 339 us (0.966)
  local copies, waits for them, and re-layouts: 61.2 us -> 39.4 us
  matrix products: 23.5 us -> 39.4 us
  waiting for transfers between devices: 212 us -> 205 us
    dot_general x4, matrix products: 14.3 us -> 33.7 us  [the longest x1 10.2 us: on_device(): jnp.einsum('tk,dk->td', grad_wide, packed, preferred_element_type=jnp.flo...]
    all_gather x1 -> x0, local copies, waits for them, and re-layouts: 15.2 us -> none  [on_device(): packed = lax.all_gather(pack, 'dp', axis=0, tiled=False)]
    slice x2 -> x0, local copies, waits for them, and re-layouts: 8.75 us -> none  [the longest x1 6.11 us: on_device(): w_qkv = packed[:, :, :c3].reshape(dp_size * d_local, c3)]
    unnamed x51 -> x58, local copies, waits for them, and re-layouts: 9.52 us -> 13.6 us
    all_gather x1, waiting for transfers between devices: 8.6 us -> 4.62 us  [on_device(): packed = lax.all_gather(pack, 'dp', axis=0, tiled=True)]
  transfers between devices with their start and end apart: 7 -> 7, of which waited for: 7 -> 7; matrix products, arithmetic and copies ran while one was open for 11% -> 13% of each run, Pallas kernels for 0% -> 0%
where the time goes in v4:
time: 339 us; the launch traced here: 338 us
  waiting for transfers between devices  205 us (60%)
  local copies, waits for them, and re-layouts  39.4 us (12%)
  matrix products  39.4 us (12%)
  other arithmetic  19.9 us (6%)
  between operations  16.9 us (5%)
  starting transfers between devices  16.8 us (5%)
    all_to_all x1, waiting for transfers between devices, on_device(): gathered = lax.all_to_all(spread, 'tensor', 0, 0, tiled=True)  72 us
    reduce_scatter x1, waiting for transfers between devices, on_device(): lax.psum_scatter(gpack, 'dp', scatter_dimension=0, tiled=True)[0]  57.2 us
    all_to_all x1, waiting for transfers between devices, on_device(): received = lax.all_to_all(payload, 'tensor', 0, 0, tiled=True)  40.1 us
    ppermute x1, waiting for transfers between devices, on_device(): returned = lax.ppermute(work_out, 'dp', pair)  19.4 us
    unnamed x58, local copies, waits for them, and re-layouts  13.6 us
    dot_general x1, matrix products, on_device(): jnp.einsum('tk,dk->td', grad_wide, packed, preferred_element_type=jnp.flo...  10.2 us
    convert_element_type x2, local copies, waits for them, and re-layouts, on_device(): wide_float = wide_in.astype(jnp.float32)  8.38 us
    dot_general x1, matrix products, on_device(): jnp.einsum('td,dk->tk', upstream, packed, preferred_element_type=jnp.floa...  8.27 us
  transfers between devices with their start and end apart: 7, of which 7 were waited for; matrix products, arithmetic and copies ran while one was open for 13% of the time, Pallas kernels for 0%

profile of v4, /device:TPU:4, one launch (start us, length us, event | category | flops | bytes accessed | tf_op | source)
XLA Modules:
  0.0 337.5 jit_solution(8838600003846409743)
XLA Ops:
  7.2 0.9 copy.104
  8.2 0.9 copy.105
  9.0 1.0 copy.103
  10.1 0.9 bitcast_dynamic-update-slice_fusion
  11.1 0.7 pad_dynamic-update-slice_fusion
  11.7 0.7 copy-done.13
  12.5 0.9 slice.78
  13.4 0.9 slice.79
  14.4 2.3 collective-permute-start
  16.7 1.3 fusion.51
  19.8 7.0 %collective-permute-done = bf16[2,192,512]{2,1,0:T(8,128)(2,1)S(1)} collective-permute-done((bf16[2,192,512]{2,1,0:T(8,128)(2,1)S(1)}, bf16[2,192,512]{2,1,0:T(8,128)(2,1)S(1)}, u32[]{:S(2)}, u32[]{:S(2)}) %collective-permute-start) | collective-permute-done | bytes 393248 | tf_op jit(solution)/shard_map/ppermute | solution.py:77
  26.9 0.7 copy-done.6
  27.6 2.0 broadcast_in_dim.16
  29.7 5.8 %all-to-all-start = ((bf16[8,2,192,512]{3,2,1,0:T(8,128)(2,1)}), bf16[8,2,192,512]{3,2,1,0:T(8,128)(2,1)S(1)}, u32[]{:S(2)}, u32[]{:S(2)}) async-start(bf16[8,2,192,512]{3,2,1,0:T(8,128)(2,1)} %broadcast_in_dim.16), calls=%async_computation | async-start | bytes 6291456 | tf_op jit(solution)/shard_map/all_to_all | solution.py:85
  35.6 72.0 %all-to-all-done = bf16[8,2,192,512]{3,2,1,0:T(8,128)(2,1)S(1)} async-done(((bf16[8,2,192,512]{3,2,1,0:T(8,128)(2,1)}), bf16[8,2,192,512]{3,2,1,0:T(8,128)(2,1)S(1)}, u32[]{:S(2)}, u32[]{:S(2)}) %all-to-all-start) | async-done | bytes 3145760 | tf_op jit(solution)/shard_map/all_to_all | solution.py:85
  107.6 1.7 copy-done
  109.4 2.5 fusion.47
  111.9 2.0 copy.110
  113.9 1.3 copy.131
  115.2 3.7 %reshape_squeeze.3 = bf16[192,32,128]{2,1,0:T(8,128)(2,1)} reshape(bf16[1,192,8,512]{3,2,1,0:T(8,128)(2,1)} %copy.110) | data formatting | bytes 3145728 | tf_op jit(solution)/shard_map/reshape;squeeze | solution.py:108
  119.0 3.6 %copy.102 = f32[1,192,8,512]{3,2,1,0:T(8,128)} copy(f32[1,192,8,512]{3,1,0,2:T(8,128)S(1)} %get-tuple-element.52) | data formatting | bytes 6291456 | tf_op jit(solution)/shard_map/convert_element_type | solution.py:90
  122.5 2.1 copy.130
  124.7 4.8 %reshape.196 = f32[192,32,128]{2,1,0:T(8,128)} reshape(f32[1,192,8,512]{3,2,1,0:T(8,128)} %copy.102) | data formatting | bytes 6291456 | tf_op jit(solution)/shard_map/convert_element_type | solution.py:90
  129.5 0.4 multiply_reduce_fusion
  129.9 2.4 broadcast_multiply_fusion
  132.3 4.6 %all-gather.2.cloned.1.call-done = bf16[4096,1408]{0,1:T(8,128)(2,1)} async-done(((bf16[128,1408]{0,1:T(8,128)(2,1)}), bf16[4096,1408]{0,1:T(8,128)(2,1)}) %all-gather.2.cloned.1.call-update) | async-done | bytes 11534352 | tf_op jit(solution)/shard_map/all_gather | solution.py:71
  136.9 0.8 slice_convert_fusion.2
  137.7 8.2 %convolution_convert_fusion.4 = bf16[192,1408]{1,0:T(8,128)(2,1)S(1)} fusion(bf16[4096,1408]{0,1:T(8,128)(2,1)} %all-gather.2.cloned.1.call-done, f32[192,4096]{1,0:T(8,128)S(1)} %broadcast_multiply_fusion, f32[4096]{0:T(1024)S(1)} %bitcast.178), kind=kOutput, calls=%fused_computation.16 | convolution fusion | flops 2216435712 | bytes 15237120 | tf_op jit(solution)/shard_map/td,dk->tk/dot_general | solution.py:96
  146.0 0.3 fusion.52
  146.4 0.4 fusion.9
  146.8 0.6 copy-done.10
  147.4 8.3 %fusion.53 = bf16[192,1408]{1,0:T(8,128)(2,1)S(1)} fusion(bf16[192,4096]{1,0:T(8,128)(2,1)S(1)} %bitcast.173, bf16[4096,1408]{0,1:T(8,128)(2,1)} %all-gather.2.cloned.1.call-done), kind=kOutput, calls=%fused_computation.109 | convolution fusion | flops 2214592512 | bytes 13647872 | tf_op jit(solution)/shard_map/td,dk->tk/dot_general | solution.py:109
  156.0 0.3 multiply_reduce_fusion.1
  156.8 0.3 fusion.10
  157.3 0.8 reshape.204
  158.3 0.6 copy-done.8
  159.0 10.2 %fusion.3 = (bf16[4096]{0:T(1024)(128)(2,1)}, bf16[192]{0:T(256)(128)(2,1)}, bf16[192,4096]{1,0:T(8,128)(2,1)}) fusion(f32[192,4096]{1,0:T(8,128)} %copy-done.5, f32[4096]{0:T(1024)S(1)} %bitcast.179, bf16[4096,1408]{0,1:T(8,128)(2,1)} %all-gather.2.cloned.1.call-done, bf16[192,768]{1,0:T(8,128)(2,1)S(1)} %pad_maximum_fusion.6), kind=kOutput, calls=%fused_computation.11 | convolution fusion | flops 2220093184 | bytes 16572800 | tf_op jit(solution)/shard_map/tk,dk->td/dot_general | solution.py:129
  169.2 2.1 copy.121
  171.3 1.3 multiply_convert_fusion
  172.6 2.5 convolution_convert_fusion.2
  175.1 1.4 convolution_convert_fusion.3
  176.5 5.1 %fusion.1 = bf16[32,128,1408]{2,1,0:T(8,128)(2,1)} fusion(bf16[32,128,1]{2,1,0:T(8,128)(2,1)S(1)} %copy-done.4, bf16[32,128,512]{2,1,0:T(8,128)(2,1)S(1)} %convolution_convert_fusion.3, bf16[32,128,768]{2,1,0:T(8,128)(2,1)S(1)} %convolution_convert_fusion.2), kind=kLoop, calls=%fused_computation.2 | loop fusion | flops 46137344 | bytes 22028288 | tf_op jit(solution)/shard_map/concatenate | solution.py:174
  181.7 0.6 copy-done.22
  182.3 7.1 %convolution_convert_fusion.1 = bf16[192,4096]{1,0:T(8,128)(2,1)S(1)} fusion(bf16[4096,1408]{0,1:T(8,128)(2,1)} %all-gather.2.cloned.1.call-done, bf16[192,512]{1,0:T(8,128)(2,1)S(1)} %bitcast.177), kind=kOutput, calls=%fused_computation.5 | convolution fusion | flops 2215378944 | bytes 13303808 | tf_op jit(solution)/shard_map/tk,dk->td/dot_general | solution.py:105
  189.4 0.3 bitcast_bitcast_fusion
  189.7 1.8 pad_maximum_fusion
  191.5 3.8 %all-to-all-start.1 = ((bf16[8,400,512]{2,1,0:T(8,128)(2,1)}), bf16[8,400,512]{2,1,0:T(8,128)(2,1)S(1)}, u32[]{:S(2)}, u32[]{:S(2)}) async-start(bf16[8,400,512]{2,1,0:T(8,128)(2,1)} %pad_maximum_fusion), calls=%async_computation.1 | async-start | bytes 6553600 | tf_op jit(solution)/shard_map/all_to_all | solution.py:155
  195.4 40.1 %all-to-all-done.1 = bf16[8,400,512]{2,1,0:T(8,128)(2,1)S(1)} async-done(((bf16[8,400,512]{2,1,0:T(8,128)(2,1)}), bf16[8,400,512]{2,1,0:T(8,128)(2,1)S(1)}, u32[]{:S(2)}, u32[]{:S(2)}) %all-to-all-start.1) | async-done | bytes 3276832 | tf_op jit(solution)/shard_map/all_to_all | solution.py:155
  235.5 0.5 convert_reduce_fusion
  236.0 0.4 copy-done.7
  236.4 1.3 fusion.30
  237.8 0.5 collective-permute-start.1
  238.9 19.4 %collective-permute-done.1 = bf16[2,192,512]{2,1,0:T(8,128)(2,1)S(1)} collective-permute-done((bf16[2,192,512]{2,1,0:T(8,128)(2,1)S(1)}, bf16[2,192,512]{2,1,0:T(8,128)(2,1)S(1)}, u32[]{:S(2)}, u32[]{:S(2)}) %collective-permute-start.1) | collective-permute-done | bytes 393248 | tf_op jit(solution)/shard_map/ppermute | solution.py:169
  258.4 0.8 pad_maximum_fusion.5
  259.2 0.8 pad_maximum_fusion.4
  260.0 57.2 %reduce-scatter.2.cloned.1.call-done = bf16[1,128,1408]{2,1,0:T(8,128)(2,1)} async-done(((bf16[32,128,1408]{2,1,0:T(8,128)(2,1)}), bf16[1,128,1408]{2,1,0:T(8,128)(2,1)}) %reduce-scatter.2.cloned.1.call-update) | async-done | bytes 360464 | tf_op jit(solution)/shard_map/reduce_scatter | solution.py:184
  317.2 1.0 bitcast_convert_fusion
  318.4 0.8 slice_bitcast_fusion
  319.2 0.6 broadcast_in_dim.21
  319.8 4.2 %all-to-all-start.2 = ((f32[8,1,128]{2,1,0:T(1,128)}), f32[8,1,128]{2,1,0:T(1,128)S(1)}, u32[]{:S(2)}, u32[]{:S(2)}) async-start(f32[8,1,128]{2,1,0:T(1,128)} %broadcast_in_dim.21), calls=%async_computation.3 | async-start | bytes 8192 | tf_op jit(solution)/shard_map/all_to_all | solution.py:190
  324.0 0.7 fusion.48
  324.6 0.8 copy.123
  325.5 4.7 %all-to-all-done.2 = f32[8,1,128]{2,1,0:T(1,128)S(1)} async-done(((f32[8,1,128]{2,1,0:T(1,128)}), f32[8,1,128]{2,1,0:T(1,128)S(1)}, u32[]{:S(2)}, u32[]{:S(2)}) %all-to-all-start.2) | async-done | bytes 4128 | tf_op jit(solution)/shard_map/all_to_all | solution.py:190
  330.1 0.5 reduce_sum.69
  (71 shorter events, 2.0 us)
Async XLA Ops:
  7.2 19.7 %copy-start.15 = (bf16[2,192,512]{2,1,0:T(8,128)(2,1)S(1)}, bf16[2,192,512]{2,1,0:T(8,128)(2,1)}, u32[]{:S(2)}) copy-start(bf16[2,192,512]{2,1,0:T(8,128)(2,1)} %param.8) | copy-start | bytes 1179652
  7.2 19.7 %copy-start.14 = (bf16[2,192,512]{2,1,0:T(8,128)(2,1)S(1)}, bf16[2,192,512]{2,1,0:T(8,128)(2,1)}, u32[]{:S(2)}) copy-start(bf16[2,192,512]{2,1,0:T(8,128)(2,1)} %param.9) | copy-start | bytes 1179652
  7.2 129.7 %all-gather.2.cloned.1.call-start = ((), (), s32[]{:S(2)}) async-start(), calls=%async_computation.4 | async-start | bytes 11894784 | tf_op jit(solution)/shard_map/all_gather | solution.py:71
  11.7 0.7 copy-start.13
  14.4 12.4 %collective-permute-start = (bf16[2,192,512]{2,1,0:T(8,128)(2,1)S(1)}, bf16[2,192,512]{2,1,0:T(8,128)(2,1)S(1)}, u32[]{:S(2)}, u32[]{:S(2)}) collective-permute-start(bf16[2,192,512]{2,1,0:T(8,128)(2,1)S(1)} %pad_maximum_fusion.1), channel_id=1, source_target_pairs={{0,128},{8,136},{16,144},{24,152},{32,160},{40,168},{48,176},{56,1... | collective-permute-start | bytes 1179656 | tf_op jit(solution)/shard_map/ppermute | solution.py:77
  26.9 0.7 copy-start.6
  29.7 77.9 %all-to-all-start = ((bf16[8,2,192,512]{3,2,1,0:T(8,128)(2,1)}), bf16[8,2,192,512]{3,2,1,0:T(8,128)(2,1)S(1)}, u32[]{:S(2)}, u32[]{:S(2)}) async-start(bf16[8,2,192,512]{3,2,1,0:T(8,128)(2,1)} %broadcast_in_dim.16), calls=%async_computation | async-start | bytes 6291456 | tf_op jit(solution)/shard_map/all_to_all | solution.py:85
  35.5 281.7 %reduce-scatter.2.cloned.1.call-start = ((), (), s32[]{:S(2)}) async-start(), calls=%async_computation.5 | async-start | bytes 11894784 | tf_op jit(solution)/shard_map/reduce_scatter | solution.py:184
  107.6 1.7 copy-start
  124.7 4.8 %copy-start.1 = (bf16[8,2,192,512]{3,2,1,0:T(8,128)(2,1)S(1)}, bf16[8,2,192,512]{3,2,1,0:T(8,128)(2,1)}, u32[]{:S(2)}) copy-start(bf16[8,2,192,512]{3,2,1,0:T(8,128)(2,1)} %copy-done) | copy-start | bytes 9437188
  129.9 2.4 copy-start.20
  132.3 13.7 %copy-start.5 = (f32[192,4096]{1,0:T(8,128)}, f32[192,4096]{1,0:T(8,128)S(1)}, u32[]{:S(2)}) copy-start(f32[192,4096]{1,0:T(8,128)S(1)} %broadcast_multiply_fusion) | copy-start | bytes 9437188
  146.0 1.4 copy-start.10
  156.0 2.3 copy-start.16
  156.8 1.5 copy-start.18
  158.3 0.7 copy-start.8
  159.0 12.3 %copy-start.2 = (f32[192,32,128]{2,1,0:T(8,128)S(1)}, f32[192,32,128]{2,1,0:T(8,128)}, u32[]{:S(2)}) copy-start(f32[192,32,128]{2,1,0:T(8,128)} %reshape.196) | copy-start | bytes 9437188
  171.2 1.3 copy-start.9
  171.2 1.3 copy-start.17
  171.3 1.3 copy-start.19
  172.6 2.5 copy-start.3
  172.6 2.5 copy-start.12
  175.1 1.4 copy-start.4
  181.6 0.7 copy-start.22
  182.3 7.1 %copy-start.11 = (bf16[192,4096]{1,0:T(8,128)(2,1)S(1)}, bf16[192,4096]{1,0:T(8,128)(2,1)}, u32[]{:S(2)}) copy-start(bf16[192,4096]{1,0:T(8,128)(2,1)} %get-tuple-element.73) | copy-start | bytes 4718596
  191.5 43.9 %all-to-all-start.1 = ((bf16[8,400,512]{2,1,0:T(8,128)(2,1)}), bf16[8,400,512]{2,1,0:T(8,128)(2,1)S(1)}, u32[]{:S(2)}, u32[]{:S(2)}) async-start(bf16[8,400,512]{2,1,0:T(8,128)(2,1)} %pad_maximum_fusion), calls=%async_computation.1 | async-start | bytes 6553600 | tf_op jit(solution)/shard_map/all_to_all | solution.py:155
  195.4 40.6 %copy-start.21 = (f32[192]{0:T(256)S(1)}, f32[192]{0:T(256)}, u32[]{:S(2)}) copy-start(f32[192]{0:T(256)} %copy-done.20) | copy-start | bytes 2308
  235.5 0.9 copy-start.7
  237.8 20.6 %collective-permute-start.1 = (bf16[2,192,512]{2,1,0:T(8,128)(2,1)S(1)}, bf16[2,192,512]{2,1,0:T(8,128)(2,1)S(1)}, u32[]{:S(2)}, u32[]{:S(2)}) collective-permute-start(bf16[2,192,512]{2,1,0:T(8,128)(2,1)S(1)} %get-tuple-element.64), channel_id=1, source_target_pairs={{0,128},{8,136},{16,144},{24,152},{32,160},{40,168},{48,176},{56,1... | collective-permute-start | bytes 1179656 | tf_op jit(solution)/shard_map/ppermute | solution.py:169
  319.8 10.4 %all-to-all-start.2 = ((f32[8,1,128]{2,1,0:T(1,128)}), f32[8,1,128]{2,1,0:T(1,128)S(1)}, u32[]{:S(2)}, u32[]{:S(2)}) async-start(f32[8,1,128]{2,1,0:T(1,128)} %broadcast_in_dim.21), calls=%async_computation.3 | async-start | bytes 8192 | tf_op jit(solution)/shard_map/all_to_all | solution.py:190
Sparse Core Ops, SparseCore 0:
  12.6 124.2 all-gather.1
  181.7 135.4 reduce-scatter.1

commit v5 on v4

--- a/solution.py
+++ b/solution.py
@@ -93,22 +93,19 @@
     gain_float = gain_all.astype(jnp.float32)
     normed_float = unit_rows * gain_float
     normed = normed_float.astype(jnp.bfloat16)
-    qkv = jnp.einsum("td,dk->tk", normed, packed, preferred_element_type=jnp.float32).astype(
+    lhs = jnp.concatenate([normed, upstream], axis=0)
+    proj = jnp.einsum("td,dk->tk", lhs, packed, preferred_element_type=jnp.float32).astype(
         jnp.bfloat16
     )
+    qkv = proj[:length]
     query_heads = qkv[:, :c1].reshape(1, length, kv_local, repeat, HD)
     key_heads = qkv[:, c1:c2].reshape(1, length, kv_local, HD)
     value_heads = qkv[:, c2:c3].reshape(1, length, kv_local, HD)
     softmax_out, softmax_low, context = attention_forward(query_heads, key_heads, value_heads)
     context_flat = context.reshape(length, kv_local * repeat * HD)
     context_wide = jnp.pad(context_flat, ((0, 0), (c3, width - c4)))
-    partial_value = jnp.einsum(
-        "tk,dk->td", context_wide, packed, preferred_element_type=jnp.float32
-    )
     upstream_blk = upstream.reshape(length, dp_size, d_local)
-    grad_context = jnp.einsum(
-        "td,dk->tk", upstream, packed, preferred_element_type=jnp.float32
-    )[:, c3:c4].astype(jnp.bfloat16)
+    grad_context = proj[length:, c3:c4]
     grad_query, grad_key, grad_value = attention_backward(
         grad_context.reshape(1, length, kv_local, repeat, HD),
         query_heads,
@@ -126,7 +123,14 @@
         axis=1,
     )
     grad_wide = jnp.pad(grad_qkv, ((0, 0), (0, width - c3)))
-    normed_terms = jnp.einsum("tk,dk->td", grad_wide, packed, preferred_element_type=jnp.float32)
+    back = jnp.einsum(
+        "tk,dk->td",
+        jnp.concatenate([context_wide, grad_wide], axis=0),
+        packed,
+        preferred_element_type=jnp.float32,
+    )
+    partial_value = back[:length]
+    normed_terms = back[length:]
     grad_w_qkv = jnp.einsum(
         "tjl,tk->jlk", normed.reshape(length, dp_size, d_local), grad_qkv,
         preferred_element_type=jnp.float32,

time: 339 us -> 340 us (level)
  matrix products: 39.4 us -> 26.5 us
  waiting for transfers between devices: 205 us -> 214 us
  other arithmetic: 19.9 us -> 23.3 us
    dot_general x4 -> x2, matrix products: 33.7 us -> 19.5 us  [the longest x1 11.5 us: on_device(): jnp.einsum('tk,dk->td', jnp.concatenate([context_wide, grad_wide], axis=0...]
    all_gather x1, waiting for transfers between devices: 4.62 us -> 11.2 us  [on_device(): packed = lax.all_gather(pack, 'dp', axis=0, tiled=True)]
    convert_element_type x1 -> x2, other arithmetic: 1.3 us -> 4.87 us  [on_device(): normed = normed_float.astype(jnp.bfloat16)]
    unnamed x58 -> x49, local copies, waits for them, and re-layouts: 13.6 us -> 12.6 us
  transfers between devices with their start and end apart: 7 -> 7, of which waited for: 7 -> 7; matrix products, arithmetic and copies ran while one was open for 13% -> 10% of each run, Pallas kernels for 0% -> 0%
where the time goes in v5:
time: 340 us; the launch traced here: 339 us
  waiting for transfers between devices  214 us (63%)
  local copies, waits for them, and re-layouts  40.9 us (12%)
  matrix products  26.5 us (8%)
  other arithmetic  23.3 us (7%)
  starting transfers between devices  17.6 us (5%)
  between operations  17 us (5%)
    all_to_all x1, waiting for transfers between devices, on_device(): gathered = lax.all_to_all(spread, 'tensor', 0, 0, tiled=True)  71.4 us
    reduce_scatter x1, waiting for transfers between devices, on_device(): lax.psum_scatter(gpack, 'dp', scatter_dimension=0, tiled=True)[0]  60.1 us
    all_to_all x1, waiting for transfers between devices, on_device(): received = lax.all_to_all(payload, 'tensor', 0, 0, tiled=True)  39.7 us
    ppermute x1, waiting for transfers between devices, on_device(): returned = lax.ppermute(work_out, 'dp', pair)  20.1 us
    unnamed x49, local copies, waits for them, and re-layouts  12.6 us
    dot_general x1, matrix products, on_device(): jnp.einsum('tk,dk->td', jnp.concatenate([context_wide, grad_wide], axis=0...  11.5 us
    all_gather x1, waiting for transfers between devices, on_device(): packed = lax.all_gather(pack, 'dp', axis=0, tiled=True)  11.2 us
    dot_general x1, matrix products, on_device(): jnp.einsum('td,dk->tk', lhs, packed, preferred_element_type=jnp.float32)  8.04 us
  transfers between devices with their start and end apart: 7, of which 7 were waited for; matrix products, arithmetic and copies ran while one was open for 10% of the time, Pallas kernels for 0%

profile of v5, /device:TPU:4, one launch (start us, length us, event | category | flops | bytes accessed | tf_op | source)
XLA Modules:
  0.0 339.4 jit_solution(8294448720089710706)
XLA Ops:
  7.2 1.1 copy.83
  8.3 0.9 copy.84
  9.2 0.9 copy.85
  10.1 0.9 bitcast_dynamic-update-slice_fusion
  11.0 0.7 pad_dynamic-update-slice_fusion
  11.7 0.7 copy-done.8
  12.5 0.9 slice.90
  13.4 0.9 slice.89
  14.4 2.3 collective-permute-start
  16.7 1.3 fusion.66
  19.9 6.9 %collective-permute-done = bf16[2,192,512]{2,1,0:T(8,128)(2,1)S(1)} collective-permute-done((bf16[2,192,512]{2,1,0:T(8,128)(2,1)S(1)}, bf16[2,192,512]{2,1,0:T(8,128)(2,1)S(1)}, u32[]{:S(2)}, u32[]{:S(2)}) %collective-permute-start) | collective-permute-done | bytes 393248 | tf_op jit(solution)/shard_map/ppermute | solution.py:77
  26.9 0.7 copy-done.3
  27.6 2.0 broadcast_in_dim.16
  29.7 5.8 %all-to-all-start = ((bf16[8,2,192,512]{3,2,1,0:T(8,128)(2,1)}), bf16[8,2,192,512]{3,2,1,0:T(8,128)(2,1)S(1)}, u32[]{:S(2)}, u32[]{:S(2)}) async-start(bf16[8,2,192,512]{3,2,1,0:T(8,128)(2,1)} %broadcast_in_dim.16), calls=%async_computation | async-start | bytes 6291456 | tf_op jit(solution)/shard_map/all_to_all | solution.py:85
  35.6 0.6 iota_compare_fusion.3
  36.2 71.4 %all-to-all-done = bf16[8,2,192,512]{3,2,1,0:T(8,128)(2,1)S(1)} async-done(((bf16[8,2,192,512]{3,2,1,0:T(8,128)(2,1)}), bf16[8,2,192,512]{3,2,1,0:T(8,128)(2,1)S(1)}, u32[]{:S(2)}, u32[]{:S(2)}) %all-to-all-start) | async-done | bytes 3145760 | tf_op jit(solution)/shard_map/all_to_all | solution.py:85
  107.6 0.5 fusion.62
  108.1 3.5 %copy.82 = f32[1,192,8,512]{3,2,1,0:T(8,128)} copy(f32[1,192,8,512]{3,1,0,2:T(8,128)S(1)} %get-tuple-element.49) | data formatting | bytes 6291456 | tf_op jit(solution)/shard_map/convert_element_type | solution.py:90
  111.6 2.1 copy.110
  113.7 2.0 copy.86
  115.7 1.3 copy.111
  117.1 3.8 %reshape_squeeze.3 = bf16[192,32,128]{2,1,0:T(8,128)(2,1)} reshape(bf16[1,192,8,512]{3,2,1,0:T(8,128)(2,1)} %copy.86) | data formatting | bytes 3145728 | tf_op jit(solution)/shard_map/reshape;squeeze | solution.py:107
  120.8 4.4 %reshape.196 = f32[192,32,128]{2,1,0:T(8,128)} reshape(f32[1,192,8,512]{3,2,1,0:T(8,128)} %copy.82) | data formatting | bytes 6291456 | tf_op jit(solution)/shard_map/convert_element_type | solution.py:90
  125.3 0.4 multiply_reduce_fusion
  125.7 11.2 %all-gather.2.cloned.1.call-done = bf16[4096,1408]{0,1:T(8,128)(2,1)} async-done(((bf16[128,1408]{0,1:T(8,128)(2,1)}), bf16[4096,1408]{0,1:T(8,128)(2,1)}) %all-gather.2.cloned.1.call-update) | async-done | bytes 11534352 | tf_op jit(solution)/shard_map/all_gather | solution.py:71
  136.9 0.8 slice_convert_fusion.1
  137.7 2.5 multiply_convert_fusion.1
  140.3 8.0 %fusion.8 = bf16[384,1408]{1,0:T(8,128)(2,1)S(1)} fusion(bf16[4096,1408]{0,1:T(8,128)(2,1)} %all-gather.2.cloned.1.call-done, bf16[192,4096]{1,0:T(8,128)(2,1)S(1)} %bitcast.164, bf16[192,4096]{1,0:T(8,128)(2,1)S(1)} %get-tuple-element.44), kind=kOutput, calls=%fused_computation.18 | convolution fusion | flops 4436017152 | bytes 15761408 | tf_op jit(solution)/shard_map/td,dk->tk/dot_general | solution.py:97
  148.9 0.9 fusion.21
  150.3 0.9 fusion.22
  151.2 0.3 fusion.18
  151.6 0.4 fusion.17
  152.1 0.7 copy.144
  153.0 0.8 reshape.204
  153.8 1.0 pad_maximum_fusion.6
  154.8 11.5 %convolution_convert_fusion = bf16[384,4096]{1,0:T(8,128)(2,1)S(1)} fusion(bf16[4096,1408]{0,1:T(8,128)(2,1)} %all-gather.2.cloned.1.call-done, bf16[192,768]{1,0:T(8,128)(2,1)S(1)} %pad_maximum_fusion.6, bf16[192,512]{1,0:T(8,128)(2,1)S(1)} %bitcast.169), kind=kOutput, calls=%fused_computation.4 | convolution fusion | flops 4435083264 | bytes 15171584 | tf_op jit(solution)/shard_map/tk,dk->td/dot_general | solution.py:126
  166.3 1.7 copy-done
  168.0 1.6 fusion.3
  169.6 2.2 copy.101
  171.7 2.3 multiply_convert_fusion
  174.1 2.4 convolution_convert_fusion.1
  176.6 1.4 convolution_convert_fusion.2
  178.0 5.2 %fusion.1 = bf16[32,128,1408]{2,1,0:T(8,128)(2,1)} fusion(bf16[32,128,1]{2,1,0:T(8,128)(2,1)S(1)} %copy-done.2, bf16[32,128,512]{2,1,0:T(8,128)(2,1)S(1)} %convolution_convert_fusion.2, bf16[32,128,768]{2,1,0:T(8,128)(2,1)S(1)} %convolution_convert_fusion.1), kind=kLoop, calls=%fused_computation.2 | loop fusion | flops 46137344 | bytes 22028288 | tf_op jit(solution)/shard_map/concatenate | solution.py:178
  183.2 0.6 copy-done.17
  183.8 2.2 fusion.61
  186.1 0.3 bitcast_bitcast_fusion
  186.4 1.8 pad_maximum_fusion
  188.3 4.5 %all-to-all-start.1 = ((bf16[8,400,512]{2,1,0:T(8,128)(2,1)}), bf16[8,400,512]{2,1,0:T(8,128)(2,1)}, u32[]{:S(2)}, u32[]{:S(2)}) async-start(bf16[8,400,512]{2,1,0:T(8,128)(2,1)} %pad_maximum_fusion), calls=%async_computation.1 | async-start | bytes 6553600 | tf_op jit(solution)/shard_map/all_to_all | solution.py:159
  192.8 0.6 constant_dynamic-slice_fusion
  193.4 39.7 %all-to-all-done.1 = bf16[8,400,512]{2,1,0:T(8,128)(2,1)} async-done(((bf16[8,400,512]{2,1,0:T(8,128)(2,1)}), bf16[8,400,512]{2,1,0:T(8,128)(2,1)}, u32[]{:S(2)}, u32[]{:S(2)}) %all-to-all-start.1) | async-done | bytes 3276832 | tf_op jit(solution)/shard_map/all_to_all | solution.py:159
  233.1 2.5 convert_reduce_fusion
  235.9 0.6 collective-permute-start.1
  237.1 20.1 %collective-permute-done.1 = bf16[2,192,512]{2,1,0:T(8,128)(2,1)S(1)} collective-permute-done((bf16[2,192,512]{2,1,0:T(8,128)(2,1)S(1)}, bf16[2,192,512]{2,1,0:T(8,128)(2,1)S(1)}, u32[]{:S(2)}, u32[]{:S(2)}) %collective-permute-start.1) | collective-permute-done | bytes 393248 | tf_op jit(solution)/shard_map/ppermute | solution.py:173
  257.3 0.8 pad_maximum_fusion.4
  258.1 0.8 pad_maximum_fusion.5
  258.9 60.1 %reduce-scatter.2.cloned.1.call-done = bf16[1,128,1408]{2,1,0:T(8,128)(2,1)} async-done(((bf16[32,128,1408]{2,1,0:T(8,128)(2,1)}), bf16[1,128,1408]{2,1,0:T(8,128)(2,1)}) %reduce-scatter.2.cloned.1.call-update) | async-done | bytes 360464 | tf_op jit(solution)/shard_map/reduce_scatter | solution.py:188
  319.0 1.0 bitcast_convert_fusion
  320.1 0.8 slice_bitcast_fusion
  320.9 0.6 broadcast_in_dim.21
  321.5 4.3 %all-to-all-start.2 = ((f32[8,1,128]{2,1,0:T(1,128)}), f32[8,1,128]{2,1,0:T(1,128)S(1)}, u32[]{:S(2)}, u32[]{:S(2)}) async-start(f32[8,1,128]{2,1,0:T(1,128)} %broadcast_in_dim.21), calls=%async_computation.3 | async-start | bytes 8192 | tf_op jit(solution)/shard_map/all_to_all | solution.py:194
  325.8 0.7 fusion.63
  326.5 0.8 copy.103
  327.3 4.7 %all-to-all-done.2 = f32[8,1,128]{2,1,0:T(1,128)S(1)} async-done(((f32[8,1,128]{2,1,0:T(1,128)}), f32[8,1,128]{2,1,0:T(1,128)S(1)}, u32[]{:S(2)}, u32[]{:S(2)}) %all-to-all-start.2) | async-done | bytes 4128 | tf_op jit(solution)/shard_map/all_to_all | solution.py:194
  332.0 0.5 reduce_sum.69
  (62 shorter events, 2.2 us)
Async XLA Ops:
  7.2 19.7 %copy-start.9 = (bf16[2,192,512]{2,1,0:T(8,128)(2,1)S(1)}, bf16[2,192,512]{2,1,0:T(8,128)(2,1)}, u32[]{:S(2)}) copy-start(bf16[2,192,512]{2,1,0:T(8,128)(2,1)} %param.9) | copy-start | bytes 1179652
  7.2 19.7 %copy-start.10 = (bf16[2,192,512]{2,1,0:T(8,128)(2,1)S(1)}, bf16[2,192,512]{2,1,0:T(8,128)(2,1)}, u32[]{:S(2)}) copy-start(bf16[2,192,512]{2,1,0:T(8,128)(2,1)} %param.8) | copy-start | bytes 1179652
  7.2 129.7 %all-gather.2.cloned.1.call-start = ((), (), s32[]{:S(2)}) async-start(), calls=%async_computation.4 | async-start | bytes 11894784 | tf_op jit(solution)/shard_map/all_gather | solution.py:71
  11.7 0.7 copy-start.8
  14.4 12.4 %collective-permute-start = (bf16[2,192,512]{2,1,0:T(8,128)(2,1)S(1)}, bf16[2,192,512]{2,1,0:T(8,128)(2,1)S(1)}, u32[]{:S(2)}, u32[]{:S(2)}) collective-permute-start(bf16[2,192,512]{2,1,0:T(8,128)(2,1)S(1)} %pad_maximum_fusion.1), channel_id=1, source_target_pairs={{0,128},{8,136},{16,144},{24,152},{32,160},{40,168},{48,176},{56,1... | collective-permute-start | bytes 1179656 | tf_op jit(solution)/shard_map/ppermute | solution.py:77
  26.9 0.7 copy-start.3
  29.7 77.9 %all-to-all-start = ((bf16[8,2,192,512]{3,2,1,0:T(8,128)(2,1)}), bf16[8,2,192,512]{3,2,1,0:T(8,128)(2,1)S(1)}, u32[]{:S(2)}, u32[]{:S(2)}) async-start(bf16[8,2,192,512]{3,2,1,0:T(8,128)(2,1)} %broadcast_in_dim.16), calls=%async_computation | async-start | bytes 6291456 | tf_op jit(solution)/shard_map/all_to_all | solution.py:85
  35.5 283.5 %reduce-scatter.2.cloned.1.call-start = ((), (), s32[]{:S(2)}) async-start(), calls=%async_computation.5 | async-start | bytes 11894784 | tf_op jit(solution)/shard_map/reduce_scatter | solution.py:188
  125.7 14.6 %copy-start.14 = (f32[192]{0:T(256)}, f32[192]{0:T(256)S(1)}, u32[]{:S(2)}) copy-start(f32[192]{0:T(256)S(1)} %add_rsqrt_fusion) | copy-start | bytes 2308
  137.7 2.6 copy-start.6
  140.3 8.1 %copy-start.13 = (pred[192,192]{0,1:T(8,128)(4,1)S(1)}, pred[192,192]{0,1:T(8,128)(4,1)}, u32[]{:S(2)}) copy-start(pred[192,192]{0,1:T(8,128)(4,1)} %iota_compare_fusion.3) | copy-start | bytes 110596
  166.3 1.7 copy-start
  169.6 4.5 %copy-start.5 = (bf16[24,8,4,128]{3,1,2,0:T(8,128)(2,1)S(1)}, bf16[24,8,4,128]{3,1,2,0:T(8,128)(2,1)}, u32[]{:S(2)}) copy-start(bf16[24,8,4,128]{3,1,2,0:T(8,128)(2,1)} %copy.144) | copy-start | bytes 589828
  171.7 2.3 copy-start.11
  171.7 2.3 copy-start.12
  174.1 2.5 copy-start.1
  174.1 2.5 copy-start.7
  176.6 1.4 copy-start.2
  183.2 0.7 copy-start.17
  188.3 44.8 %all-to-all-start.1 = ((bf16[8,400,512]{2,1,0:T(8,128)(2,1)}), bf16[8,400,512]{2,1,0:T(8,128)(2,1)}, u32[]{:S(2)}, u32[]{:S(2)}) async-start(bf16[8,400,512]{2,1,0:T(8,128)(2,1)} %pad_maximum_fusion), calls=%async_computation.1 | async-start | bytes 6553600 | tf_op jit(solution)/shard_map/all_to_all | solution.py:159
  192.7 42.8 %copy-start.4 = (bf16[1,192,512]{2,1,0:T(8,128)(2,1)S(1)}, bf16[1,192,512]{2,1,0:T(8,128)(2,1)}, u32[]{:S(2)}) copy-start(bf16[1,192,512]{2,1,0:T(8,128)(2,1)} %copy-done.3) | copy-start | bytes 589828
  193.4 42.2 %copy-start.15 = (f32[192]{0:T(256)S(1)}, f32[192]{0:T(256)}, u32[]{:S(2)}) copy-start(f32[192]{0:T(256)} %copy-done.14) | copy-start | bytes 2308
  193.4 42.3 %copy-start.16 = (f32[512,1]{0,1:T(1,128)S(1)}, f32[512,1]{0,1:T(1,128)}, u32[]{:S(2)}) copy-start(f32[512,1]{0,1:T(1,128)} %constant_dynamic-slice_fusion) | copy-start | bytes 6148
  235.9 21.4 %collective-permute-start.1 = (bf16[2,192,512]{2,1,0:T(8,128)(2,1)S(1)}, bf16[2,192,512]{2,1,0:T(8,128)(2,1)S(1)}, u32[]{:S(2)}, u32[]{:S(2)}) collective-permute-start(bf16[2,192,512]{2,1,0:T(8,128)(2,1)S(1)} %get-tuple-element.63), channel_id=1, source_target_pairs={{0,128},{8,136},{16,144},{24,152},{32,160},{40,168},{48,176},{56,1... | collective-permute-start | bytes 1179656 | tf_op jit(solution)/shard_map/ppermute | solution.py:173
  321.5 10.5 %all-to-all-start.2 = ((f32[8,1,128]{2,1,0:T(1,128)}), f32[8,1,128]{2,1,0:T(1,128)S(1)}, u32[]{:S(2)}, u32[]{:S(2)}) async-start(f32[8,1,128]{2,1,0:T(1,128)} %broadcast_in_dim.21), calls=%async_computation.3 | async-start | bytes 8192 | tf_op jit(solution)/shard_map/all_to_all | solution.py:194
Sparse Core Ops, SparseCore 0:
  12.6 124.2 all-gather.1
  183.3 135.6 reduce-scatter.1

commit v6 on v5

--- a/solution.py
+++ b/solution.py
@@ -65,12 +65,11 @@
     c2 = c1 + k_cols
     c3 = c2 + k_cols
     c4 = c3 + o_rows
-    pack = jnp.concatenate(
-        [wq, wk, wv, wo.T, jnp.pad(gain.reshape(d_local, 1), ((0, 0), (0, 127)))], axis=1
-    )
+    pack = jnp.concatenate([wq, wk, wv, wo.T], axis=1)
     packed = lax.all_gather(pack, "dp", axis=0, tiled=True)
     width = packed.shape[1]
-    gain_all = packed[:, c4]
+    gain_spread = jnp.broadcast_to(gain[None], (dp_size, d_local))
+    gain_all = lax.all_to_all(gain_spread, "dp", 0, 0, tiled=True).reshape(full_width)
     half = dp_size // 2
     pair = [(i, (i + half) % dp_size) for i in range(dp_size)]
     partner_count = counts[(replica + half) % dp_size]
@@ -179,9 +178,6 @@
         [
             grad_w_qkv.astype(jnp.bfloat16),
             grad_output_t.astype(jnp.bfloat16),
-            jnp.pad(gain_part.reshape(dp_size, d_local, 1), ((0, 0), (0, 0), (0, 127))).astype(
-                jnp.bfloat16
-            ),
         ],
         axis=2,
     )
@@ -190,8 +186,9 @@
     grad_wk = greduced[:, c1:c2]
     grad_wv = greduced[:, c2:c3]
     grad_wo = greduced[:, c3:c4].T
-    gain_spread = jnp.broadcast_to(greduced[:, c4][None], (groups, d_local))
-    grad_gain = jnp.sum(lax.all_to_all(gain_spread, "tensor", 0, 0, tiled=True), axis=0)
+    gain_replicas = lax.all_to_all(gain_part.reshape(dp_size, d_local), "dp", 0, 0, tiled=True)
+    gain_groups = jnp.broadcast_to(jnp.sum(gain_replicas, axis=0)[None], (groups, d_local))
+    grad_gain = jnp.sum(lax.all_to_all(gain_groups, "tensor", 0, 0, tiled=True), axis=0)
     return (mixed_block, grad_block, grad_gain, grad_wq, grad_wk, grad_wv, grad_wo)
 
 

time: 340 us -> 309 us (0.909)
  waiting for transfers between devices: 214 us -> 151 us
  blocking collectives: 0 us -> 20.5 us
  starting transfers between devices: 17.6 us -> 30.5 us
  local copies, waits for them, and re-layouts: 40.9 us -> 33.3 us
  other arithmetic: 23.3 us -> 27 us
    reduce_scatter x1, waiting for transfers between devices: 60.1 us -> 19.7 us  [on_device(): lax.psum_scatter(gpack, 'dp', scatter_dimension=0, tiled=True)[0]]
    all_to_all x0 -> x1, blocking collectives: none -> 20.5 us  [on_device(): lax.all_to_all(gain_part.reshape(dp_size, d_local), 'dp', 0, 0, tiled=True)]
    ppermute x1, waiting for transfers between devices: 20.1 us -> 0.01 us  [on_device(): returned = lax.ppermute(work_out, 'dp', pair)]
    all_to_all x1, waiting for transfers between devices: 39.7 us -> 51.7 us  [on_device(): received = lax.all_to_all(payload, 'tensor', 0, 0, tiled=True)]
    all_to_all x1 -> x2, starting transfers between devices: 4.34 us -> 15.8 us  [the longest x1 10.5 us: on_device(): lax.all_to_all(gain_spread, 'dp', 0, 0, tiled=True).reshape(full_width)]
    all_gather x1, waiting for transfers between devices: 11.2 us -> 0.01 us  [on_device(): packed = lax.all_gather(pack, 'dp', axis=0, tiled=True)]
    ppermute x1, waiting for transfers between devices: 6.92 us -> 0.01 us  [on_device(): lent = lax.ppermute(jnp.stack([tokens[1], grad_out[1]]), 'dp', pair)]
    all_to_all x1 -> x2, waiting for transfers between devices: 4.69 us -> 9.04 us  [the longest x1 5.47 us: on_device(): lax.all_to_all(gain_groups, 'tensor', 0, 0, tiled=True)]
  transfers between devices with their start and end apart: 7 -> 8, of which waited for: 7 -> 5; matrix products, arithmetic and copies ran while one was open for 10% -> 17% of each run, Pallas kernels for 0% -> 0%
where the time goes in v6:
time: 309 us; the launch traced here: 307 us
  waiting for transfers between devices  151 us (49%)
  local copies, waits for them, and re-layouts  33.3 us (11%)
  starting transfers between devices  30.5 us (10%)
  matrix products  27.6 us (9%)
  other arithmetic  27 us (9%)
  blocking collectives  20.5 us (7%)
  between operations  17 us (6%)
    all_to_all x1, waiting for transfers between devices, on_device(): gathered = lax.all_to_all(spread, 'tensor', 0, 0, tiled=True)  70.6 us
    all_to_all x1, waiting for transfers between devices, on_device(): received = lax.all_to_all(payload, 'tensor', 0, 0, tiled=True)  51.7 us
    all_to_all x1, blocking collectives, on_device(): lax.all_to_all(gain_part.reshape(dp_size, d_local), 'dp', 0, 0, tiled=True)  20.5 us
    reduce_scatter x1, waiting for transfers between devices, on_device(): lax.psum_scatter(gpack, 'dp', scatter_dimension=0, tiled=True)[0]  19.7 us
    all_to_all x1, starting transfers between devices, on_device(): lax.all_to_all(gain_spread, 'dp', 0, 0, tiled=True).reshape(full_width)  10.5 us
    dot_general x1, matrix products, on_device(): jnp.einsum('tk,dk->td', jnp.concatenate([context_wide, grad_wide], axis=0...  9.87 us
    dot_general x1, matrix products, on_device(): jnp.einsum('td,dk->tk', lhs, packed, preferred_element_type=jnp.float32)  9.2 us
    unnamed x37, local copies, waits for them, and re-layouts  8.63 us
  transfers between devices with their start and end apart: 8, of which 5 were waited for; matrix products, arithmetic and copies ran while one was open for 17% of the time, Pallas kernels for 0%

profile of v6, /device:TPU:4, one launch (start us, length us, event | category | flops | bytes accessed | tf_op | source)
XLA Modules:
  0.0 306.9 jit_solution(5701665756184554641)
XLA Ops:
  7.2 0.9 copy.83
  8.2 0.9 copy.82
  9.0 1.0 copy.81
  10.1 1.7 pad_maximum_fusion.7
  11.8 0.9 slice.84
  12.7 0.9 slice.83
  13.7 2.3 collective-permute-start
  16.0 1.3 broadcast_in_dim.17
  17.3 10.5 %all-to-all-start.1 = ((bf16[32,1,128]{2,1,0:T(2,128)(2,1)}), bf16[32,1,128]{2,1,0:T(2,128)(2,1)S(1)}, u32[]{:S(2)}, u32[]{:S(2)}) async-start(bf16[32,1,128]{2,1,0:T(2,128)(2,1)} %broadcast_in_dim.17), calls=%async_computation.1 | async-start | bytes 32768 | tf_op jit(solution)/shard_map/all_to_all | solution.py:72
  27.8 1.3 fusion.64
  31.2 0.7 copy-done.2
  31.9 3.6 %all-to-all-done.1 = bf16[32,1,128]{2,1,0:T(2,128)(2,1)S(1)} async-done(((bf16[32,1,128]{2,1,0:T(2,128)(2,1)}), bf16[32,1,128]{2,1,0:T(2,128)(2,1)S(1)}, u32[]{:S(2)}, u32[]{:S(2)}) %all-to-all-start.1) | async-done | bytes 8224 | tf_op jit(solution)/shard_map/all_to_all | solution.py:72
  35.5 2.1 broadcast_in_dim.16
  37.5 4.9 %all-to-all-start = ((bf16[8,2,192,512]{3,2,1,0:T(8,128)(2,1)}), bf16[8,2,192,512]{3,2,1,0:T(8,128)(2,1)S(1)}, u32[]{:S(2)}, u32[]{:S(2)}) async-start(bf16[8,2,192,512]{3,2,1,0:T(8,128)(2,1)} %broadcast_in_dim.16), calls=%async_computation | async-start | bytes 6291456 | tf_op jit(solution)/shard_map/all_to_all | solution.py:84
  42.5 0.6 iota_compare_fusion.2
  43.2 70.6 %all-to-all-done = bf16[8,2,192,512]{3,2,1,0:T(8,128)(2,1)S(1)} async-done(((bf16[8,2,192,512]{3,2,1,0:T(8,128)(2,1)}), bf16[8,2,192,512]{3,2,1,0:T(8,128)(2,1)S(1)}, u32[]{:S(2)}, u32[]{:S(2)}) %all-to-all-start) | async-done | bytes 3145760 | tf_op jit(solution)/shard_map/all_to_all | solution.py:84
  113.8 0.5 fusion.60
  114.3 3.4 %copy.79 = f32[1,192,8,512]{3,2,1,0:T(8,128)} copy(f32[1,192,8,512]{3,1,0,2:T(8,128)S(1)} %get-tuple-element.49) | data formatting | bytes 6291456 | tf_op jit(solution)/shard_map/convert_element_type | solution.py:89
  117.8 2.1 copy.107
  119.9 2.0 copy.80
  121.9 1.4 copy.108
  123.3 3.8 %reshape_squeeze.3 = bf16[192,32,128]{2,1,0:T(8,128)(2,1)} reshape(bf16[1,192,8,512]{3,2,1,0:T(8,128)(2,1)} %copy.80) | data formatting | bytes 3145728 | tf_op jit(solution)/shard_map/reshape;squeeze | solution.py:106
  127.1 4.4 %reshape.199 = f32[192,32,128]{2,1,0:T(8,128)} reshape(f32[1,192,8,512]{3,2,1,0:T(8,128)} %copy.79) | data formatting | bytes 6291456 | tf_op jit(solution)/shard_map/convert_element_type | solution.py:89
  131.5 0.4 multiply_reduce_fusion
  131.9 3.7 %multiply_convert_fusion = bf16[192,32,128]{2,1,0:T(8,128)(2,1)} fusion(f32[192,32,128]{2,1,0:T(8,128)} %reshape.199, f32[32,128]{1,0:T(8,128)S(1)} %bitcast.162, f32[192]{0:T(256)S(1)} %add_rsqrt_fusion), kind=kLoop, calls=%fused_computation.13 | loop fusion | flops 2359296 | bytes 4735744 | tf_op jit(solution)/shard_map/convert_element_type | solution.py:94
  135.6 1.8 multiply_convert_fusion.1
  137.4 9.2 %fusion.6 = bf16[384,1280]{1,0:T(8,128)(2,1)S(1)} fusion(bf16[4096,1280]{0,1:T(8,128)(2,1)} %all-gather.2.cloned.1.call-done, bf16[192,4096]{1,0:T(8,128)(2,1)} %bitcast.160, bf16[192,4096]{1,0:T(8,128)(2,1)} %get-tuple-element.44), kind=kOutput, calls=%fused_computation.16 | convolution fusion | flops 4033314816 | bytes 14614528 | tf_op jit(solution)/shard_map/td,dk->tk/dot_general | solution.py:96
  146.7 0.3 fusion.65
  147.1 0.9 fusion.19
  148.0 0.3 multiply_reduce_fusion.1
  148.3 0.2 fusion.30
  148.6 0.9 fusion.20
  149.5 0.3 fusion.16
  149.8 0.4 fusion.15
  150.2 0.2 copy.89
  150.3 0.7 copy.141
  151.2 0.8 reshape.207
  152.0 2.9 convolution_convert_fusion.2
  154.9 2.5 convolution_convert_fusion.1
  157.4 7.4 %pad_maximum_fusion = bf16[32,128,1280]{2,1,0:T(8,128)(2,1)} fusion(bf16[32,128,512]{2,1,0:T(8,128)(2,1)S(1)} %convolution_convert_fusion.2, bf16[32,128,768]{2,1,0:T(8,128)(2,1)S(1)} %convolution_convert_fusion.1), kind=kLoop, calls=%fused_computation | loop fusion | flops 20971520 | bytes 20971520 | tf_op jit(solution)/shard_map/concatenate | solution.py:177
  164.8 1.0 pad_maximum_fusion.8
  165.8 9.9 %convolution_convert_fusion = bf16[384,4096]{1,0:T(8,128)(2,1)S(1)} fusion(bf16[4096,1280]{0,1:T(8,128)(2,1)} %all-gather.2.cloned.1.call-done, bf16[192,768]{1,0:T(8,128)(2,1)S(1)} %pad_maximum_fusion.8, bf16[192,512]{1,0:T(8,128)(2,1)S(1)} %bitcast.166), kind=kOutput, calls=%fused_computation.2 | convolution fusion | flops 4032036864 | bytes 14123008 | tf_op jit(solution)/shard_map/tk,dk->td/dot_general | solution.py:125
  175.7 1.5 fusion.1
  177.3 0.2 fusion.59
  177.5 0.3 bitcast_bitcast_fusion
  177.8 1.9 pad_maximum_fusion.1
  179.7 7.1 %all-to-all-start.2 = ((bf16[8,400,512]{2,1,0:T(8,128)(2,1)}), bf16[8,400,512]{2,1,0:T(8,128)(2,1)}, u32[]{:S(2)}, u32[]{:S(2)}) async-start(bf16[8,400,512]{2,1,0:T(8,128)(2,1)} %pad_maximum_fusion.1), calls=%async_computation.2 | async-start | bytes 6553600 | tf_op jit(solution)/shard_map/all_to_all | solution.py:158
  186.8 0.7 dynamic_slice.14
  187.5 51.7 %all-to-all-done.2 = bf16[8,400,512]{2,1,0:T(8,128)(2,1)} async-done(((bf16[8,400,512]{2,1,0:T(8,128)(2,1)}), bf16[8,400,512]{2,1,0:T(8,128)(2,1)}, u32[]{:S(2)}, u32[]{:S(2)}) %all-to-all-start.2) | async-done | bytes 3276832 | tf_op jit(solution)/shard_map/all_to_all | solution.py:158
  239.2 2.6 convert_reduce_fusion
  241.8 0.2 fusion.40
  242.1 0.3 collective-permute-start.1
  242.4 20.5 %all_to_all.31 = f32[32,1,128]{2,1,0:T(1,128)S(1)} all-to-all(f32[32,1,128]{2,1,0:T(1,128)S(1)} %bitcast.168), channel_id=1, replica_groups=mesh['dp'=32,'tensor'=8] {'dp'}, dimensions={0} | all-to-all | bytes 32768 | tf_op jit(solution)/shard_map/all_to_all | solution.py:189
  262.9 0.6 broadcast_in_dim.21
  263.5 5.3 %all-to-all-start.4 = ((f32[8,1,128]{2,1,0:T(1,128)}), f32[8,1,128]{2,1,0:T(1,128)S(1)}, u32[]{:S(2)}, u32[]{:S(2)}) async-start(f32[8,1,128]{2,1,0:T(1,128)} %broadcast_in_dim.21), calls=%async_computation.4 | async-start | bytes 8192 | tf_op jit(solution)/shard_map/all_to_all | solution.py:191
  269.4 5.5 %all-to-all-done.4 = f32[8,1,128]{2,1,0:T(1,128)S(1)} async-done(((f32[8,1,128]{2,1,0:T(1,128)}), f32[8,1,128]{2,1,0:T(1,128)S(1)}, u32[]{:S(2)}, u32[]{:S(2)}) %all-to-all-start.4) | async-done | bytes 4128 | tf_op jit(solution)/shard_map/all_to_all | solution.py:191
  274.9 0.5 reduce_sum.79
  275.5 0.8 pad_maximum_fusion.5
  276.3 0.8 pad_maximum_fusion.6
  277.1 19.7 %reduce-scatter.2.cloned.1.call-done = bf16[1,128,1280]{2,1,0:T(8,128)(2,1)} async-done(((bf16[32,128,1280]{2,1,0:T(8,128)(2,1)}), bf16[1,128,1280]{2,1,0:T(8,128)(2,1)}) %reduce-scatter.2.cloned.1.call-update) | async-done | bytes 327696 | tf_op jit(solution)/shard_map/reduce_scatter | solution.py:184
  296.8 1.0 bitcast_convert_fusion
  297.8 0.8 slice_bitcast_fusion
  298.6 0.7 fusion.61
  299.2 0.8 copy.100
  (53 shorter events, 0.9 us)
Async XLA Ops:
  7.2 23.9 %copy-start.5 = (bf16[2,192,512]{2,1,0:T(8,128)(2,1)S(1)}, bf16[2,192,512]{2,1,0:T(8,128)(2,1)}, u32[]{:S(2)}) copy-start(bf16[2,192,512]{2,1,0:T(8,128)(2,1)} %param.9) | copy-start | bytes 1179652
  7.2 23.9 %copy-start.6 = (bf16[2,192,512]{2,1,0:T(8,128)(2,1)S(1)}, bf16[2,192,512]{2,1,0:T(8,128)(2,1)}, u32[]{:S(2)}) copy-start(bf16[2,192,512]{2,1,0:T(8,128)(2,1)} %param.8) | copy-start | bytes 1179652
  7.2 130.2 %all-gather.2.cloned.1.call-start = ((), (), s32[]{:S(2)}) async-start(), calls=%async_computation.6 | async-start | bytes 10813440 | tf_op jit(solution)/shard_map/all_gather | solution.py:69
  13.7 17.4 %collective-permute-start = (bf16[2,192,512]{2,1,0:T(8,128)(2,1)S(1)}, bf16[2,192,512]{2,1,0:T(8,128)(2,1)S(1)}, u32[]{:S(2)}, u32[]{:S(2)}) collective-permute-start(bf16[2,192,512]{2,1,0:T(8,128)(2,1)S(1)} %pad_maximum_fusion.2), channel_id=1, source_target_pairs={{0,128},{8,136},{16,144},{24,152},{32,160},{40,168},{48,176},{56,1... | collective-permute-start | bytes 1179656 | tf_op jit(solution)/shard_map/ppermute | solution.py:76
  17.3 18.2 %all-to-all-start.1 = ((bf16[32,1,128]{2,1,0:T(2,128)(2,1)}), bf16[32,1,128]{2,1,0:T(2,128)(2,1)S(1)}, u32[]{:S(2)}, u32[]{:S(2)}) async-start(bf16[32,1,128]{2,1,0:T(2,128)(2,1)} %broadcast_in_dim.17), calls=%async_computation.1 | async-start | bytes 32768 | tf_op jit(solution)/shard_map/all_to_all | solution.py:72
  31.2 0.7 copy-start.2
  37.5 76.3 %all-to-all-start = ((bf16[8,2,192,512]{3,2,1,0:T(8,128)(2,1)}), bf16[8,2,192,512]{3,2,1,0:T(8,128)(2,1)S(1)}, u32[]{:S(2)}, u32[]{:S(2)}) async-start(bf16[8,2,192,512]{3,2,1,0:T(8,128)(2,1)} %broadcast_in_dim.16), calls=%async_computation | async-start | bytes 6291456 | tf_op jit(solution)/shard_map/all_to_all | solution.py:84
  42.5 254.3 %reduce-scatter.2.cloned.1.call-start = ((), (), s32[]{:S(2)}) async-start(), calls=%async_computation.7 | async-start | bytes 10813440 | tf_op jit(solution)/shard_map/reduce_scatter | solution.py:184
  131.5 4.1 %copy-start = (f32[24,8,8,512]{3,1,2,0:T(8,128)S(1)}, f32[24,8,8,512]{3,1,2,0:T(8,128)}, u32[]{:S(2)}) copy-start(f32[24,8,8,512]{3,1,2,0:T(8,128)} %copy.107) | copy-start | bytes 9437188
  131.9 5.5 %copy-start.11 = (f32[192]{0:T(256)}, f32[192]{0:T(256)S(1)}, u32[]{:S(2)}) copy-start(f32[192]{0:T(256)S(1)} %add_rsqrt_fusion) | copy-start | bytes 2308
  137.4 9.2 %copy-start.9 = (pred[192,192]{0,1:T(8,128)(4,1)S(1)}, pred[192,192]{0,1:T(8,128)(4,1)}, u32[]{:S(2)}) copy-start(pred[192,192]{0,1:T(8,128)(4,1)} %iota_compare_fusion.2) | copy-start | bytes 110596
  152.0 2.9 copy-start.1
  152.0 2.9 copy-start.4
  152.0 2.9 copy-start.7
  152.0 2.9 copy-start.8
  179.7 59.4 %all-to-all-start.2 = ((bf16[8,400,512]{2,1,0:T(8,128)(2,1)}), bf16[8,400,512]{2,1,0:T(8,128)(2,1)}, u32[]{:S(2)}, u32[]{:S(2)}) async-start(bf16[8,400,512]{2,1,0:T(8,128)(2,1)} %pad_maximum_fusion.1), calls=%async_computation.2 | async-start | bytes 6553600 | tf_op jit(solution)/shard_map/all_to_all | solution.py:158
  186.8 55.0 %copy-start.3 = (bf16[1,192,512]{2,1,0:T(8,128)(2,1)S(1)}, bf16[1,192,512]{2,1,0:T(8,128)(2,1)}, u32[]{:S(2)}) copy-start(bf16[1,192,512]{2,1,0:T(8,128)(2,1)} %copy-done.2) | copy-start | bytes 589828
  187.5 54.9 %copy-start.10 = (f32[4096]{0:T(1024)S(1)}, f32[4096]{0:T(1024)}, u32[]{:S(2)}) copy-start(f32[4096]{0:T(1024)} %get-tuple-element.42) | copy-start | bytes 49156
  239.2 2.6 copy-start.12
  239.2 2.6 copy-start.13
  242.1 33.3 %collective-permute-start.1 = (bf16[2,192,512]{2,1,0:T(8,128)(2,1)S(1)}, bf16[2,192,512]{2,1,0:T(8,128)(2,1)S(1)}, u32[]{:S(2)}, u32[]{:S(2)}) collective-permute-start(bf16[2,192,512]{2,1,0:T(8,128)(2,1)S(1)} %get-tuple-element.63), channel_id=1, source_target_pairs={{0,128},{8,136},{16,144},{24,152},{32,160},{40,168},{48,176},{56,1... | collective-permute-start | bytes 1179656 | tf_op jit(solution)/shard_map/ppermute | solution.py:172
  263.5 11.4 %all-to-all-start.4 = ((f32[8,1,128]{2,1,0:T(1,128)}), f32[8,1,128]{2,1,0:T(1,128)S(1)}, u32[]{:S(2)}, u32[]{:S(2)}) async-start(f32[8,1,128]{2,1,0:T(1,128)} %broadcast_in_dim.21), calls=%async_computation.4 | async-start | bytes 8192 | tf_op jit(solution)/shard_map/all_to_all | solution.py:191
Sparse Core Ops, SparseCore 0:
  11.9 114.8 all-gather.1
  164.9 131.8 reduce-scatter.1

commit v7 on v6

--- a/solution.py
+++ b/solution.py
@@ -65,9 +65,11 @@
     c2 = c1 + k_cols
     c3 = c2 + k_cols
     c4 = c3 + o_rows
-    pack = jnp.concatenate([wq, wk, wv, wo.T], axis=1)
+    pack = jnp.concatenate([wq, wk, wv], axis=1)
     packed = lax.all_gather(pack, "dp", axis=0, tiled=True)
     width = packed.shape[1]
+    wo_spread = jnp.broadcast_to(wo.T[None], (dp_size,) + wo.T.shape)
+    wo_blk = lax.all_to_all(wo_spread, "dp", 0, 0, tiled=True)
     gain_spread = jnp.broadcast_to(gain[None], (dp_size, d_local))
     gain_all = lax.all_to_all(gain_spread, "dp", 0, 0, tiled=True).reshape(full_width)
     half = dp_size // 2
@@ -92,19 +94,18 @@
     gain_float = gain_all.astype(jnp.float32)
     normed_float = unit_rows * gain_float
     normed = normed_float.astype(jnp.bfloat16)
-    lhs = jnp.concatenate([normed, upstream], axis=0)
-    proj = jnp.einsum("td,dk->tk", lhs, packed, preferred_element_type=jnp.float32).astype(
+    qkv = jnp.einsum("td,dk->tk", normed, packed, preferred_element_type=jnp.float32).astype(
         jnp.bfloat16
     )
-    qkv = proj[:length]
     query_heads = qkv[:, :c1].reshape(1, length, kv_local, repeat, HD)
     key_heads = qkv[:, c1:c2].reshape(1, length, kv_local, HD)
     value_heads = qkv[:, c2:c3].reshape(1, length, kv_local, HD)
     softmax_out, softmax_low, context = attention_forward(query_heads, key_heads, value_heads)
     context_flat = context.reshape(length, kv_local * repeat * HD)
-    context_wide = jnp.pad(context_flat, ((0, 0), (c3, width - c4)))
     upstream_blk = upstream.reshape(length, dp_size, d_local)
-    grad_context = proj[length:, c3:c4]
+    grad_context = jnp.einsum(
+        "tjl,jlk->tk", upstream_blk, wo_blk, preferred_element_type=jnp.float32
+    ).astype(jnp.bfloat16)
     grad_query, grad_key, grad_value = attention_backward(
         grad_context.reshape(1, length, kv_local, repeat, HD),
         query_heads,
@@ -121,15 +122,10 @@
         ],
         axis=1,
     )
-    grad_wide = jnp.pad(grad_qkv, ((0, 0), (0, width - c3)))
-    back = jnp.einsum(
-        "tk,dk->td",
-        jnp.concatenate([context_wide, grad_wide], axis=0),
-        packed,
-        preferred_element_type=jnp.float32,
-    )
-    partial_value = back[:length]
-    normed_terms = back[length:]
+    normed_terms = jnp.einsum("tk,dk->td", grad_qkv, packed, preferred_element_type=jnp.float32)
+    partial_value = jnp.einsum(
+        "tk,jlk->tjl", context_flat, wo_blk, preferred_element_type=jnp.float32
+    ).reshape(length, full_width)
     grad_w_qkv = jnp.einsum(
         "tjl,tk->jlk", normed.reshape(length, dp_size, d_local), grad_qkv,
         preferred_element_type=jnp.float32,

time: 309 us -> 368 us (1.19)
  waiting for transfers between devices: 151 us -> 213 us
  starting transfers between devices: 30.5 us -> 36.5 us
  other arithmetic: 27 us -> 22.9 us
    all_to_all x0 -> x1, waiting for transfers between devices: none -> 87.9 us  [on_device(): wo_blk = lax.all_to_all(wo_spread, 'dp', 0, 0, tiled=True)]
    all_to_all x1, waiting for transfers between devices: 70.6 us -> 42 us  [on_device(): gathered = lax.all_to_all(spread, 'tensor', 0, 0, tiled=True)]
    reduce_scatter x1, waiting for transfers between devices: 19.7 us -> 32.6 us  [on_device(): lax.psum_scatter(gpack, 'dp', scatter_dimension=0, tiled=True)[0]]
    all_to_all x1, waiting for transfers between devices: 51.7 us -> 39.6 us  [on_device(): received = lax.all_to_all(payload, 'tensor', 0, 0, tiled=True)]
    all_to_all x0 -> x1, starting transfers between devices: none -> 7.5 us  [on_device(): wo_blk = lax.all_to_all(wo_spread, 'dp', 0, 0, tiled=True)]
    unnamed x37 -> x31, local copies, waits for them, and re-layouts: 8.63 us -> 4.29 us
    dot_general x2 -> x4, matrix products: 19.1 us -> 18.3 us  [the longest x1 5.89 us: on_device(): jnp.einsum('tk,dk->td', grad_qkv, packed, preferred_element_type=jnp.floa...]
  transfers between devices with their start and end apart: 8 -> 9, of which waited for: 5 -> 6; matrix products, arithmetic and copies ran while one was open for 17% -> 14% of each run, Pallas kernels for 0% -> 0%
where the time goes in v7:
time: 368 us; the launch traced here: 366 us
  waiting for transfers between devices  213 us (58%)
  starting transfers between devices  36.5 us (10%)
  local copies, waits for them, and re-layouts  32.1 us (9%)
  matrix products  26.8 us (7%)
  other arithmetic  22.9 us (6%)
  blocking collectives  17.4 us (5%)
  between operations  16.9 us (5%)
    all_to_all x1, waiting for transfers between devices, on_device(): wo_blk = lax.all_to_all(wo_spread, 'dp', 0, 0, tiled=True)  87.9 us
    all_to_all x1, waiting for transfers between devices, on_device(): gathered = lax.all_to_all(spread, 'tensor', 0, 0, tiled=True)  42 us
    all_to_all x1, waiting for transfers between devices, on_device(): received = lax.all_to_all(payload, 'tensor', 0, 0, tiled=True)  39.6 us
    reduce_scatter x1, waiting for transfers between devices, on_device(): lax.psum_scatter(gpack, 'dp', scatter_dimension=0, tiled=True)[0]  32.6 us
    all_to_all x1, blocking collectives, on_device(): lax.all_to_all(gain_part.reshape(dp_size, d_local), 'dp', 0, 0, tiled=True)  17.4 us
    all_to_all x1, starting transfers between devices, on_device(): lax.all_to_all(gain_spread, 'dp', 0, 0, tiled=True).reshape(full_width)  10.5 us
    all_to_all x1, waiting for transfers between devices, on_device(): lax.all_to_all(gain_groups, 'tensor', 0, 0, tiled=True)  8.48 us
    convert_element_type x2, local copies, waits for them, and re-layouts, on_device(): wide_float = wide_in.astype(jnp.float32)  7.98 us
  transfers between devices with their start and end apart: 9, of which 6 were waited for; matrix products, arithmetic and copies ran while one was open for 14% of the time, Pallas kernels for 0%

profile of v7, /device:TPU:4, one launch (start us, length us, event | category | flops | bytes accessed | tf_op | source)
XLA Modules:
  0.0 365.9 jit_solution(8486937826131650)
XLA Ops:
  7.2 0.9 slice.69
  8.1 0.9 slice.68
  9.1 2.3 collective-permute-start
  11.4 1.3 broadcast_in_dim.17
  12.7 10.5 %all-to-all-start.1 = ((bf16[32,1,128]{2,1,0:T(2,128)(2,1)}), bf16[32,1,128]{2,1,0:T(2,128)(2,1)S(1)}, u32[]{:S(2)}, u32[]{:S(2)}) async-start(bf16[32,1,128]{2,1,0:T(2,128)(2,1)} %broadcast_in_dim.17), calls=%async_computation.1 | async-start | bytes 32768 | tf_op jit(solution)/shard_map/all_to_all | solution.py:74
  23.2 1.4 fusion.61
  26.5 1.1 slice_select_fusion.1
  27.6 0.7 copy-done.2
  28.3 2.6 all-to-all-done.1
  30.8 1.9 broadcast_in_dim.16
  32.8 5.1 %all-to-all-start = ((bf16[8,2,192,512]{3,2,1,0:T(8,128)(2,1)}), bf16[8,2,192,512]{3,2,1,0:T(8,128)(2,1)S(1)}, u32[]{:S(2)}, u32[]{:S(2)}) async-start(bf16[8,2,192,512]{3,2,1,0:T(8,128)(2,1)} %broadcast_in_dim.16), calls=%async_computation | async-start | bytes 6291456 | tf_op jit(solution)/shard_map/all_to_all | solution.py:86
  37.9 1.5 pad_maximum_fusion.8
  39.4 1.0 copy.76
  40.4 42.0 %all-to-all-done = bf16[8,2,192,512]{3,2,1,0:T(8,128)(2,1)S(1)} async-done(((bf16[8,2,192,512]{3,2,1,0:T(8,128)(2,1)}), bf16[8,2,192,512]{3,2,1,0:T(8,128)(2,1)S(1)}, u32[]{:S(2)}, u32[]{:S(2)}) %all-to-all-start) | async-done | bytes 3145760 | tf_op jit(solution)/shard_map/all_to_all | solution.py:86
  82.5 2.4 broadcast_in_dim.22
  84.9 7.5 %all-to-all-start.2 = ((bf16[32,128,512]{2,1,0:T(8,128)(2,1)}), bf16[32,128,512]{2,1,0:T(8,128)(2,1)}, u32[]{:S(2)}, u32[]{:S(2)}) async-start(bf16[32,128,512]{2,1,0:T(8,128)(2,1)} %broadcast_in_dim.22), calls=%async_computation.2 | async-start | bytes 8388608 | tf_op jit(solution)/shard_map/all_to_all | solution.py:72
  92.5 0.5 fusion.57
  93.0 3.5 copy.72
  96.6 2.0 copy.98
  98.6 2.1 copy.78
  100.6 3.8 %reshape_squeeze.3 = bf16[192,32,128]{2,1,0:T(8,128)(2,1)} reshape(bf16[1,192,8,512]{3,2,1,0:T(8,128)(2,1)} %copy.78) | data formatting | bytes 3145728 | tf_op jit(solution)/shard_map/reshape;squeeze | solution.py:105
  104.4 4.4 %reshape.201 = f32[192,32,128]{2,1,0:T(8,128)} reshape(f32[1,192,8,512]{3,2,1,0:T(8,128)} %copy.72) | data formatting | bytes 6291456 | tf_op jit(solution)/shard_map/convert_element_type | solution.py:91
  108.8 0.4 multiply_reduce_fusion
  109.3 3.8 %multiply_convert_fusion = bf16[192,32,128]{2,1,0:T(8,128)(2,1)} fusion(f32[192,32,128]{2,1,0:T(8,128)} %reshape.201, f32[32,128]{1,0:T(8,128)S(1)} %bitcast.169, f32[192]{0:T(256)S(1)} %add_rsqrt_fusion), kind=kLoop, calls=%fused_computation.10 | loop fusion | flops 2359296 | bytes 4735744 | tf_op jit(solution)/shard_map/convert_element_type | solution.py:96
  113.0 0.4 broadcast_multiply_fusion
  113.4 87.9 %all-to-all-done.2 = bf16[32,128,512]{2,1,0:T(8,128)(2,1)} async-done(((bf16[32,128,512]{2,1,0:T(8,128)(2,1)}), bf16[32,128,512]{2,1,0:T(8,128)(2,1)}, u32[]{:S(2)}, u32[]{:S(2)}) %all-to-all-start.2) | async-done | bytes 4194336 | tf_op jit(solution)/shard_map/all_to_all | solution.py:72
  201.4 4.3 %fusion.19 = bf16[24,4,8,128]{3,2,1,0:T(8,128)(2,1)} fusion(bf16[32,128,512]{2,1,0:T(8,128)(2,1)} %all-to-all-done.2, bf16[192,32,128]{2,1,0:T(8,128)(2,1)} %reshape_squeeze.3), kind=kOutput, calls=%fused_computation.35 | convolution fusion | flops 805404672 | bytes 5963776 | tf_op jit(solution)/shard_map/tjl,jlk->tk/dot_general | solution.py:106
  205.7 4.2 %fusion.9 = bf16[192,768]{1,0:T(8,128)(2,1)S(1)} fusion(bf16[4096,768]{1,0:T(8,128)(2,1)} %all-gather.2.cloned.1.call-done, f32[192,4096]{1,0:T(8,128)S(1)} %broadcast_multiply_fusion, f32[4096]{0:T(1024)S(1)} %bitcast.170), kind=kOutput, calls=%fused_computation.27 | convolution fusion | flops 1209679872 | bytes 9748480 | tf_op jit(solution)/shard_map/td,dk->tk/dot_general | solution.py:97
  209.9 0.3 fusion.62
  210.4 0.9 fusion.24
  211.3 0.3 multiply_reduce_fusion.1
  211.6 0.2 fusion.28
  211.8 0.9 fusion.25
  212.7 0.3 fusion.18
  213.1 0.4 fusion.17
  213.5 0.2 copy.82
  213.6 0.7 copy.141
  214.3 0.2 copy.75
  214.5 0.8 reshape.210
  215.3 2.9 convolution_convert_fusion.3
  218.2 2.5 convolution_convert_fusion.2
  220.7 7.1 %pad_maximum_fusion = bf16[32,128,1280]{2,1,0:T(8,128)(2,1)} fusion(bf16[32,128,512]{2,1,0:T(8,128)(2,1)S(1)} %convolution_convert_fusion.3, bf16[32,128,768]{2,1,0:T(8,128)(2,1)S(1)} %convolution_convert_fusion.2), kind=kLoop, calls=%fused_computation | loop fusion | flops 20971520 | bytes 20971520 | tf_op jit(solution)/shard_map/concatenate | solution.py:173
  227.8 5.9 %fusion.1 = (f32[4096]{0:T(1024)}, bf16[192]{0:T(256)(128)(2,1)S(1)}, bf16[192,4096]{1,0:T(8,128)(2,1)S(1)}) fusion(f32[192,4096]{1,0:T(8,128)S(1)} %broadcast_multiply_fusion, f32[4096]{0:T(1024)S(1)} %bitcast.171, bf16[4096,768]{1,0:T(8,128)(2,1)} %all-gather.2.cloned.1.call-done, bf16[192,128]{1,0:T(8,128)(2,1)} %fusion.24, bf16[192,128]{1,0:T(8,128)(2,1)} %fusion.25, ...), kind=kOutput, calls=%fused_computation.9 | convolution fusion | flops 1214344960 | bytes 11338112 | tf_op jit(solution)/shard_map/tk,dk->td/dot_general | solution.py:125
  233.7 3.8 %convolution_convert_fusion.1 = bf16[192,4096]{1,0:T(8,128)(2,1)S(1)} fusion(bf16[4096,512]{1,0:T(8,128)(2,1)} %bitcast.14, bf16[24,8,4,128]{3,2,1,0:T(4,128)(2,1)S(1)} %bitcast.164), kind=kOutput, calls=%fused_computation.3 | convolution fusion | flops 806092800 | bytes 5963776 | tf_op jit(solution)/shard_map/tk,jlk->tjl/dot_general | solution.py:126
  237.5 0.3 bitcast_bitcast_fusion
  237.8 1.8 pad_maximum_fusion.1
  239.7 4.5 %all-to-all-start.3 = ((bf16[8,400,512]{2,1,0:T(8,128)(2,1)}), bf16[8,400,512]{2,1,0:T(8,128)(2,1)}, u32[]{:S(2)}, u32[]{:S(2)}) async-start(bf16[8,400,512]{2,1,0:T(8,128)(2,1)} %pad_maximum_fusion.1), calls=%async_computation.3 | async-start | bytes 6553600 | tf_op jit(solution)/shard_map/all_to_all | solution.py:154
  244.2 0.7 dynamic_slice.14
  244.9 39.6 %all-to-all-done.3 = bf16[8,400,512]{2,1,0:T(8,128)(2,1)} async-done(((bf16[8,400,512]{2,1,0:T(8,128)(2,1)}), bf16[8,400,512]{2,1,0:T(8,128)(2,1)}, u32[]{:S(2)}, u32[]{:S(2)}) %all-to-all-start.3) | async-done | bytes 3276832 | tf_op jit(solution)/shard_map/all_to_all | solution.py:154
  284.5 2.5 convert_reduce_fusion
  287.0 0.2 fusion.38
  287.3 3.3 collective-permute-start.1
  290.6 17.4 %all_to_all.36 = f32[32,1,128]{2,1,0:T(1,128)S(1)} all-to-all(f32[32,1,128]{2,1,0:T(1,128)S(1)} %bitcast.176), channel_id=1, replica_groups=mesh['dp'=32,'tensor'=8] {'dp'}, dimensions={0} | all-to-all | bytes 32768 | tf_op jit(solution)/shard_map/all_to_all | solution.py:185
  308.0 0.6 broadcast_in_dim.24
  308.6 3.3 all-to-all-start.5
  312.5 8.5 %all-to-all-done.5 = f32[8,1,128]{2,1,0:T(1,128)S(1)} async-done(((f32[8,1,128]{2,1,0:T(1,128)}), f32[8,1,128]{2,1,0:T(1,128)S(1)}, u32[]{:S(2)}, u32[]{:S(2)}) %all-to-all-start.5) | async-done | bytes 4128 | tf_op jit(solution)/shard_map/all_to_all | solution.py:187
  321.0 0.5 reduce_sum.79
  321.7 0.8 pad_maximum_fusion.5
  322.4 0.8 pad_maximum_fusion.6
  323.2 32.6 %reduce-scatter.2.cloned.1.call-done = bf16[1,128,1280]{2,1,0:T(8,128)(2,1)} async-done(((bf16[32,128,1280]{2,1,0:T(8,128)(2,1)}), bf16[1,128,1280]{2,1,0:T(8,128)(2,1)}) %reduce-scatter.2.cloned.1.call-update) | async-done | bytes 327696 | tf_op jit(solution)/shard_map/reduce_scatter | solution.py:180
  355.8 1.0 bitcast_convert_fusion
  356.8 0.8 slice_bitcast_fusion
  357.6 0.7 fusion.58
  358.2 0.8 copy.91
  (50 shorter events, 0.6 us)
Async XLA Ops:
  9.1 17.4 %collective-permute-start = (bf16[2,192,512]{2,1,0:T(8,128)(2,1)S(1)}, bf16[2,192,512]{2,1,0:T(8,128)(2,1)S(1)}, u32[]{:S(2)}, u32[]{:S(2)}) collective-permute-start(bf16[2,192,512]{2,1,0:T(8,128)(2,1)S(1)} %pad_maximum_fusion.2), channel_id=1, source_target_pairs={{0,128},{8,136},{16,144},{24,152},{32,160},{40,168},{48,176},{56,1... | collective-permute-start | bytes 1179656 | tf_op jit(solution)/shard_map/ppermute | solution.py:78
  12.7 18.2 %all-to-all-start.1 = ((bf16[32,1,128]{2,1,0:T(2,128)(2,1)}), bf16[32,1,128]{2,1,0:T(2,128)(2,1)S(1)}, u32[]{:S(2)}, u32[]{:S(2)}) async-start(bf16[32,1,128]{2,1,0:T(2,128)(2,1)} %broadcast_in_dim.17), calls=%async_computation.1 | async-start | bytes 32768 | tf_op jit(solution)/shard_map/all_to_all | solution.py:74
  27.5 0.7 copy-start.2
  32.8 5.1 %copy-start.5 = (bf16[128,512]{1,0:T(8,128)(2,1)S(1)}, bf16[128,512]{1,0:T(8,128)(2,1)}, u32[]{:S(2)}) copy-start(bf16[128,512]{1,0:T(8,128)(2,1)} %param.12) | copy-start | bytes 393220
  32.8 5.1 %copy-start.8 = (bf16[128,128]{1,0:T(8,128)(2,1)S(1)}, bf16[128,128]{1,0:T(8,128)(2,1)}, u32[]{:S(2)}) copy-start(bf16[128,128]{1,0:T(8,128)(2,1)} %param.14) | copy-start | bytes 98308
  32.8 49.7 %all-to-all-start = ((bf16[8,2,192,512]{3,2,1,0:T(8,128)(2,1)}), bf16[8,2,192,512]{3,2,1,0:T(8,128)(2,1)S(1)}, u32[]{:S(2)}, u32[]{:S(2)}) async-start(bf16[8,2,192,512]{3,2,1,0:T(8,128)(2,1)} %broadcast_in_dim.16), calls=%async_computation | async-start | bytes 6291456 | tf_op jit(solution)/shard_map/all_to_all | solution.py:86
  37.9 167.8 %all-gather.2.cloned.1.call-start = ((), (), s32[]{:S(2)}) async-start(), calls=%async_computation.7 | async-start | bytes 6488064 | tf_op jit(solution)/shard_map/all_gather | solution.py:69
  84.9 116.5 %all-to-all-start.2 = ((bf16[32,128,512]{2,1,0:T(8,128)(2,1)}), bf16[32,128,512]{2,1,0:T(8,128)(2,1)}, u32[]{:S(2)}, u32[]{:S(2)}) async-start(bf16[32,128,512]{2,1,0:T(8,128)(2,1)} %broadcast_in_dim.22), calls=%async_computation.2 | async-start | bytes 8388608 | tf_op jit(solution)/shard_map/all_to_all | solution.py:72
  92.4 263.4 %reduce-scatter.2.cloned.1.call-start = ((), (), s32[]{:S(2)}) async-start(), calls=%async_computation.8 | async-start | bytes 10813440 | tf_op jit(solution)/shard_map/reduce_scatter | solution.py:180
  108.8 4.2 %copy-start = (f32[24,8,8,512]{3,1,2,0:T(8,128)S(1)}, f32[24,8,8,512]{3,1,2,0:T(8,128)}, u32[]{:S(2)}) copy-start(f32[24,8,8,512]{3,1,2,0:T(8,128)} %copy.98) | copy-start | bytes 9437188
  109.3 4.2 %copy-start.10 = (f32[192]{0:T(256)}, f32[192]{0:T(256)S(1)}, u32[]{:S(2)}) copy-start(f32[192]{0:T(256)S(1)} %add_rsqrt_fusion) | copy-start | bytes 2308
  205.7 4.7 %copy-start.13 = (bf16[24,4,8,128]{3,2,1,0:T(8,128)(2,1)S(1)}, bf16[24,4,8,128]{3,2,1,0:T(8,128)(2,1)}, u32[]{:S(2)}) copy-start(bf16[24,4,8,128]{3,2,1,0:T(8,128)(2,1)} %fusion.19) | copy-start | bytes 589828
  215.2 2.9 copy-start.1
  215.2 2.9 copy-start.4
  215.2 2.9 copy-start.6
  215.2 2.9 copy-start.7
  239.7 44.8 %all-to-all-start.3 = ((bf16[8,400,512]{2,1,0:T(8,128)(2,1)}), bf16[8,400,512]{2,1,0:T(8,128)(2,1)}, u32[]{:S(2)}, u32[]{:S(2)}) async-start(bf16[8,400,512]{2,1,0:T(8,128)(2,1)} %pad_maximum_fusion.1), calls=%async_computation.3 | async-start | bytes 6553600 | tf_op jit(solution)/shard_map/all_to_all | solution.py:154
  244.2 42.8 %copy-start.3 = (bf16[1,192,512]{2,1,0:T(8,128)(2,1)S(1)}, bf16[1,192,512]{2,1,0:T(8,128)(2,1)}, u32[]{:S(2)}) copy-start(bf16[1,192,512]{2,1,0:T(8,128)(2,1)} %copy-done.2) | copy-start | bytes 589828
  244.9 45.7 %copy-start.9 = (f32[4096]{0:T(1024)S(1)}, f32[4096]{0:T(1024)}, u32[]{:S(2)}) copy-start(f32[4096]{0:T(1024)} %get-tuple-element.42) | copy-start | bytes 49156
  284.5 2.5 copy-start.11
  284.5 2.5 copy-start.12
  287.3 34.3 %collective-permute-start.1 = (bf16[2,192,512]{2,1,0:T(8,128)(2,1)S(1)}, bf16[2,192,512]{2,1,0:T(8,128)(2,1)S(1)}, u32[]{:S(2)}, u32[]{:S(2)}) collective-permute-start(bf16[2,192,512]{2,1,0:T(8,128)(2,1)S(1)} %get-tuple-element.57), channel_id=1, source_target_pairs={{0,128},{8,136},{16,144},{24,152},{32,160},{40,168},{48,176},{56,1... | collective-permute-start | bytes 1179656 | tf_op jit(solution)/shard_map/ppermute | solution.py:168
  308.6 12.4 %all-to-all-start.5 = ((f32[8,1,128]{2,1,0:T(1,128)}), f32[8,1,128]{2,1,0:T(1,128)S(1)}, u32[]{:S(2)}, u32[]{:S(2)}) async-start(f32[8,1,128]{2,1,0:T(1,128)} %broadcast_in_dim.24), calls=%async_computation.5 | async-start | bytes 8192 | tf_op jit(solution)/shard_map/all_to_all | solution.py:187
Sparse Core Ops, SparseCore 0:
  41.8 102.4 all-gather.1
  227.9 127.8 reduce-scatter.1
